TPU v7x, 32 devices: a whole 2x2x4 slice. The times are simulated.
32 devices in a mesh: groups: 2 (over y), seq: 4 (over z), grid: 4 (over x, core).
Axes of the slice: x: 2, y: 2, z: 4, core: 2. Of those that a mesh axis runs over, the one named last changes fastest.
Arguments:
- queries: bfloat16 [16384, 2048], P(('groups', 'seq'), 'grid'), parts along dimension 0, may hold values from -6 to 6
- keys: bfloat16 [16384, 1024], P(('groups', 'seq'), 'grid'), parts along dimension 0, may hold values from -6 to 6
- values: bfloat16 [16384, 1024], P(('groups', 'seq'), 'grid'), parts along dimension 0, may hold values from -6 to 6
- out_grad: bfloat16 [16384, 2048], P(('groups', 'seq'), 'grid'), parts along dimension 0, may hold values from -6 to 6
- layer_input: bfloat16 [16384, 2048], P(('groups', 'seq')), parts along dimension 0, may hold values from -6 to 6
- moment: bfloat16 [64, 512, 512], P(('groups', 'grid'), 'seq'), parts along dimension 0, may hold values from -6 to 6
- left_old: bfloat16 [64, 512, 512], P(('groups', 'grid'), 'seq'), parts along dimension 0, may hold values from -0.25 to 0.25
- left_new: bfloat16 [64, 512, 512], P(('groups', 'grid'), 'seq'), parts along dimension 0, may hold values from -0.25 to 0.25
- right_old: bfloat16 [64, 512, 512], P(('groups', 'grid'), 'seq'), parts along dimension 0, may hold values from -0.25 to 0.25
- right_new: bfloat16 [64, 512, 512], P(('groups', 'grid'), 'seq'), parts along dimension 0, may hold values from -0.25 to 0.25
Outputs:
- attention_out: bfloat16 [16384, 2048], P(('groups', 'seq'), 'grid'), parts along dimension 0
- query_grad: bfloat16 [16384, 2048], P(('groups', 'seq'), 'grid'), parts along dimension 0
- key_grad: bfloat16 [16384, 1024], P(('groups', 'seq'), 'grid'), parts along dimension 0
- value_grad: bfloat16 [16384, 1024], P(('groups', 'seq'), 'grid'), parts along dimension 0
- new_moment: float32 [64, 512, 512], P(('groups', 'grid'), 'seq'), parts along dimension 0
There are 2 independent parts, one for each index of `groups`. A program takes and returns all parts, laid end to end along the dimension named above; each array names one. Nothing has to cross between parts.
All inputs are finite; a program needn't handle non-finite values.
Results may differ from a plain program's by a relative error of at most 0.024.
Values may be sent and summed in bfloat16 or wider, within the bound.
No kernel may reach another device: no remote copies, remote signals or barrier semaphores. Data moves between devices by JAX's collectives and lax.ppermute only.
A program may use at most 640 MiB of HBM per device.

v0:
```python
import jax
import jax.numpy as jnp
from jax import lax
from jax.sharding import PartitionSpec as P

HEAD_DIM = 128


moment_decay = 0.8


def shifted(x, axis, by):
    length = lax.axis_size(axis)
    pairs = [(i, i + by) for i in range(length) if 0 <= i + by < length]
    return lax.ppermute(x, axis, pairs)


def per_device(
    queries, keys, values, out_grad, layer_input, moment, left_old, left_new, right_old, right_new
):
    reach_devs = lax.axis_size("seq") // 2
    local_rows = queries.shape[0]
    seq_index = lax.axis_index("seq")
    query_heads = queries.shape[1] // HEAD_DIM
    kv_count = keys.shape[1] // HEAD_DIM
    group_size = query_heads // kv_count
    score_scale = HEAD_DIM ** (-0.5)
    key_value = jnp.concatenate([keys, values], axis=1)
    shards_in = [shifted(key_value, "seq", distance) for distance in range(reach_devs, 0, -1)]
    window_pair = jnp.concatenate(shards_in + [key_value], axis=0)
    window_rows = window_pair.shape[0]
    key_index = jnp.arange(window_rows, dtype=jnp.int32)[None, :]
    query_index = jnp.arange(local_rows, dtype=jnp.int32)[:, None]
    visible = (
        (key_index > query_index)
        & (key_index <= reach_devs * local_rows + query_index)
        & (key_index >= (reach_devs - seq_index) * local_rows)
    )
    key_sums = [jnp.zeros((window_rows, HEAD_DIM), jnp.float32) for kv_slot in range(kv_count)]
    value_sums = [jnp.zeros((window_rows, HEAD_DIM), jnp.float32) for kv_slot in range(kv_count)]
    head_outs = []
    query_grads = []
    for q_head in range(query_heads):
        kv_slot = q_head // group_size
        q_block = queries[:, q_head * HEAD_DIM : (q_head + 1) * HEAD_DIM]
        g_block = out_grad[:, q_head * HEAD_DIM : (q_head + 1) * HEAD_DIM]
        k_block = window_pair[:, kv_slot * HEAD_DIM : (kv_slot + 1) * HEAD_DIM]
        v_block = window_pair[
            :, (kv_count + kv_slot) * HEAD_DIM : (kv_count + kv_slot + 1) * HEAD_DIM
        ]
        scores = jnp.where(
            visible,
            jnp.einsum("qd,cd->qc", q_block, k_block, preferred_element_type=jnp.float32)
            * score_scale,
            -jnp.inf,
        )
        row_max = jnp.max(scores, axis=1, keepdims=True)
        log_total = row_max + jnp.log(jnp.sum(jnp.exp(scores - row_max), axis=1, keepdims=True))
        weights = jnp.exp(scores - log_total)
        weights_bf = weights.astype(jnp.bfloat16)
        head_out = jnp.dot(weights_bf, v_block, preferred_element_type=jnp.float32).astype(
            jnp.bfloat16
        )
        row_dot = jnp.sum(
            g_block.astype(jnp.float32) * head_out.astype(jnp.float32), axis=1, keepdims=True
        )
        weight_grad = jnp.einsum("qd,cd->qc", g_block, v_block, preferred_element_type=jnp.float32)
        score_grad = (weights * (weight_grad - row_dot) * score_scale).astype(jnp.bfloat16)
        query_grads.append(
            jnp.dot(score_grad, k_block, preferred_element_type=jnp.float32).astype(jnp.bfloat16)
        )
        head_outs.append(head_out)
        key_sums[kv_slot] = key_sums[kv_slot] + jnp.einsum(
            "qc,qd->cd", score_grad, q_block, preferred_element_type=jnp.float32
        )
        value_sums[kv_slot] = value_sums[kv_slot] + jnp.einsum(
            "qc,qd->cd", weights_bf, g_block, preferred_element_type=jnp.float32
        )
    grad_window = jnp.concatenate(key_sums + value_sums, axis=1)
    own_rows = grad_window[reach_devs * local_rows :]
    summed = own_rows
    for distance in range(1, reach_devs + 1):
        summed = summed + shifted(
            grad_window[
                (reach_devs - distance) * local_rows : (reach_devs - distance + 1) * local_rows
            ],
            "seq",
            -distance,
        )
    attention_out = jnp.concatenate(head_outs, axis=1)
    query_grad = jnp.concatenate(query_grads, axis=1)
    key_grad = summed[:, : kv_count * HEAD_DIM].astype(jnp.bfloat16)
    value_grad = summed[:, kv_count * HEAD_DIM :].astype(jnp.bfloat16)
    joined_parts = []
    for kv_slot in range(kv_count):
        joined_parts.append(
            query_grad[:, kv_slot * group_size * HEAD_DIM : (kv_slot + 1) * group_size * HEAD_DIM]
        )
        joined_parts.append(key_grad[:, kv_slot * HEAD_DIM : (kv_slot + 1) * HEAD_DIM])
        joined_parts.append(value_grad[:, kv_slot * HEAD_DIM : (kv_slot + 1) * HEAD_DIM])
    joined_local = jnp.concatenate(joined_parts, axis=1)
    local_blocks = moment.shape[0]
    share_rows = moment.shape[1]
    order_size = moment.shape[2]
    row_blocks = layer_input.shape[1] // order_size
    col_local = joined_local.shape[1] // order_size
    input_blocks = layer_input.reshape(local_rows, row_blocks, order_size)
    joined_blocks = joined_local.reshape(local_rows, col_local, order_size)
    term = jnp.einsum(
        "trk,tcj->kcrj", input_blocks, joined_blocks, preferred_element_type=jnp.float32
    )
    grad_share = lax.psum_scatter(
        term.reshape(share_rows * lax.axis_size("seq"), local_blocks, order_size),
        "seq",
        scatter_dimension=0,
        tiled=True,
    )
    grad_blocks = jnp.transpose(grad_share, (1, 0, 2)).astype(jnp.bfloat16)
    old_cols = right_old
    turn_share = lax.psum_scatter(
        jnp.einsum("brk,brj->kbj", old_cols, right_new, preferred_element_type=jnp.float32),
        "seq",
        scatter_dimension=0,
        tiled=True,
    )
    right_turn = jnp.transpose(turn_share, (1, 0, 2)).astype(jnp.bfloat16)
    moment_term = jnp.einsum(
        "brk,bkj->brj",
        moment,
        lax.all_gather(right_turn, "seq", axis=1, tiled=True),
        preferred_element_type=jnp.float32,
    )
    grad_term = jnp.einsum(
        "brk,bkj->brj",
        grad_blocks,
        lax.all_gather(right_new, "seq", axis=1, tiled=True),
        preferred_element_type=jnp.float32,
    )
    turned = moment_term.astype(jnp.bfloat16)
    old_cols = left_old
    carried = jnp.einsum(
        "brk,bkj->brj",
        old_cols,
        lax.all_gather(turned, "seq", axis=1, tiled=True),
        preferred_element_type=jnp.float32,
    )
    inner = (moment_decay * carried + (1.0 - moment_decay) * grad_term).astype(jnp.bfloat16)
    new_share = lax.psum_scatter(
        jnp.einsum("brk,brj->kbj", left_new, inner, preferred_element_type=jnp.float32),
        "seq",
        scatter_dimension=0,
        tiled=True,
    )
    new_moment = jnp.transpose(new_share, (1, 0, 2))
    return (attention_out, query_grad, key_grad, value_grad, new_moment)


def solution(mesh):
    return jax.shard_map(
        per_device,
        mesh=mesh,
        in_specs=(
            P(("groups", "seq"), "grid"),
            P(("groups", "seq"), "grid"),
            P(("groups", "seq"), "grid"),
            P(("groups", "seq"), "grid"),
            P(("groups", "seq"), None),
            P(("groups", "grid"), "seq", None),
            P(("groups", "grid"), "seq", None),
            P(("groups", "grid"), "seq", None),
            P(("groups", "grid"), "seq", None),
            P(("groups", "grid"), "seq", None),
        ),
        out_specs=(
            P(("groups", "seq"), "grid"),
            P(("groups", "seq"), "grid"),
            P(("groups", "seq"), "grid"),
            P(("groups", "seq"), "grid"),
            P(("groups", "grid"), "seq", None),
        ),
        check_vma=False,
    )
```

profile of v0, /device:TPU:0, one launch (start us, length us, event | category | flops | bytes accessed | tf_op | source)
XLA Modules:
  0.0 1565.7 jit_solution(128038068195384930)
XLA Ops:
  11.8 6.3 collective-permute-start.1
  18.1 4.5 collective-permute-start
  22.6 5.8 convolution_bitcast_fusion.1
  37.4 56.0 %collective-permute-done.1 = bf16[2048,512]{1,0:T(8,128)(2,1)} collective-permute-done((bf16[2048,512]{1,0:T(8,128)(2,1)}, bf16[2048,512]{1,0:T(8,128)(2,1)}, u32[]{:S(2)}, u32[]{:S(2)}) %collective-permute-start.1) | collective-permute-done | bytes 2097184 | tf_op jit(solution)/shard_map/ppermute | solution.py:15
  93.4 88.7 %collective-permute-done = bf16[2048,512]{1,0:T(8,128)(2,1)} collective-permute-done((bf16[2048,512]{1,0:T(8,128)(2,1)}, bf16[2048,512]{1,0:T(8,128)(2,1)}, u32[]{:S(2)}, u32[]{:S(2)}) %collective-permute-start) | collective-permute-done | bytes 2097184 | tf_op jit(solution)/shard_map/ppermute | solution.py:15
  182.1 4.0 pad_maximum_fusion.1
  186.1 24.1 %fusion.93 = (f32[2048]{0:T(1024)S(1)}, f32[2048,6144]{0,1:T(8,128)}) fusion(bf16[2048,512]{1,0:T(8,128)(2,1)S(1)} %copy-done.6, bf16[6144,512]{1,0:T(8,128)(2,1)S(1)} %pad_maximum_fusion.1, pred[6144]{0:T(1024)(128)(4,1)S(1)} %iota_compare_fusion.2, s32[2048]{0:T(1024)S(1)} %iota_add_fusion), kind=kOutput, calls=%fused_computation.132 | convolution fusion | flops 3309303808 | bytes 52451328 | tf_op jit(solution)/shard_map/qd,cd->qc/dot_general | solution.py:53
  210.3 24.1 %fusion.91 = (f32[2048]{0:T(1024)S(1)}, f32[2048,6144]{0,1:T(8,128)}) fusion(bf16[2048,512]{1,0:T(8,128)(2,1)S(1)} %copy-done.6, bf16[6144,512]{1,0:T(8,128)(2,1)S(1)} %pad_maximum_fusion.1, pred[6144]{0:T(1024)(128)(4,1)S(1)} %iota_compare_fusion.2, s32[2048]{0:T(1024)S(1)} %iota_add_fusion), kind=kOutput, calls=%fused_computation.130 | convolution fusion | flops 3309303808 | bytes 52451328 | tf_op jit(solution)/shard_map/qd,cd->qc/dot_general | solution.py:53
  234.4 24.1 %fusion.92 = (f32[2048]{0:T(1024)S(1)}, f32[2048,6144]{0,1:T(8,128)}) fusion(bf16[2048,512]{1,0:T(8,128)(2,1)S(1)} %copy-done.6, bf16[6144,512]{1,0:T(8,128)(2,1)S(1)} %pad_maximum_fusion.1, pred[6144]{0:T(1024)(128)(4,1)S(1)} %iota_compare_fusion.2, s32[2048]{0:T(1024)S(1)} %iota_add_fusion), kind=kOutput, calls=%fused_computation.131 | convolution fusion | flops 3309303808 | bytes 52451328 | tf_op jit(solution)/shard_map/qd,cd->qc/dot_general | solution.py:53
  258.5 24.4 %fusion.94 = (f32[2048]{0:T(1024)S(1)}, f32[2048,6144]{0,1:T(8,128)}) fusion(bf16[2048,512]{1,0:T(8,128)(2,1)S(1)} %copy-done.6, bf16[6144,512]{1,0:T(8,128)(2,1)S(1)} %pad_maximum_fusion.1, pred[6144]{0:T(1024)(128)(4,1)S(1)} %iota_compare_fusion.2, s32[2048]{0:T(1024)S(1)} %iota_add_fusion), kind=kOutput, calls=%fused_computation.133 | convolution fusion | flops 3309303808 | bytes 52451328 | tf_op jit(solution)/shard_map/qd,cd->qc/dot_general | solution.py:53
  282.9 19.4 %exponential_reduce_fusion.2 = f32[2048]{0:T(1024)S(1)} fusion(f32[2048,6144]{0,1:T(8,128)} %get-tuple-element.23, f32[2048]{0:T(1024)S(1)} %get-tuple-element.22), kind=kLoop, calls=%fused_computation.23 | loop fusion | flops 25163776 | bytes 50348032 | tf_op jit(solution)/shard_map/reduce_sum | solution.py:58
  302.9 19.4 %exponential_reduce_fusion = f32[2048]{0:T(1024)S(1)} fusion(f32[2048,6144]{0,1:T(8,128)} %get-tuple-element.19, f32[2048]{0:T(1024)S(1)} %get-tuple-element.18), kind=kLoop, calls=%fused_computation.19 | loop fusion | flops 25163776 | bytes 50348032 | tf_op jit(solution)/shard_map/reduce_sum | solution.py:58
  322.3 19.4 %exponential_reduce_fusion.1 = f32[2048]{0:T(1024)S(1)} fusion(f32[2048,6144]{0,1:T(8,128)} %get-tuple-element.21, f32[2048]{0:T(1024)S(1)} %get-tuple-element.20), kind=kLoop, calls=%fused_computation.21 | loop fusion | flops 25163776 | bytes 50348032 | tf_op jit(solution)/shard_map/reduce_sum | solution.py:58
  341.8 19.6 %multiply_reduce_fusion.1 = (f32[2048]{0:T(1024)S(1)}, bf16[2048,128]{0,1:T(8,128)(2,1)}) fusion(bf16[2048,128]{0,1:T(8,128)(2,1)S(1)} %copy-done.10, bf16[6144,512]{1,0:T(8,128)(2,1)S(1)} %pad_maximum_fusion.1, f32[2048,6144]{0,1:T(8,128)} %get-tuple-element.21, f32[2048]{0:T(1024)S(1)} %log_add_fusion.1), kind=kOutput, calls=%fused_computation.72 | convolution fusion | flops 3247699968 | bytes 52969472 | tf_op jit(solution)/shard_map/dot_general | solution.py:61
  361.3 26.0 %fusion.3 = bf16[2048,6144]{0,1:T(8,128)(2,1)} fusion(f32[2048,6144]{0,1:T(8,128)} %get-tuple-element.21, f32[2048]{0:T(1024)S(1)} %get-tuple-element.28, f32[2048]{0:T(1024)S(1)} %log_add_fusion.1, bf16[6144,512]{1,0:T(8,128)(2,1)} %copy-done.2, bf16[2048,512]{1,0:T(8,128)(2,1)S(1)} %copy-done.5), kind=kOutput, calls=%fused_computation.7 | convolution fusion | flops 3284140032 | bytes 77611008 | tf_op jit(solution)/shard_map/qd,cd->qc/dot_general | solution.py:67
  387.4 14.8 fusion.70
  402.1 19.4 %exponential_reduce_fusion.3 = f32[2048]{0:T(1024)S(1)} fusion(f32[2048,6144]{0,1:T(8,128)} %get-tuple-element.25, f32[2048]{0:T(1024)S(1)} %get-tuple-element.24), kind=kLoop, calls=%fused_computation.25 | loop fusion | flops 25163776 | bytes 50348032 | tf_op jit(solution)/shard_map/reduce_sum | solution.py:58
  421.6 19.8 %multiply_reduce_fusion.3 = (f32[2048]{0:T(1024)S(1)}, bf16[2048,128]{0,1:T(8,128)(2,1)}) fusion(bf16[2048,128]{0,1:T(8,128)(2,1)S(1)} %copy-done.8, bf16[6144,512]{1,0:T(8,128)(2,1)} %copy-done.2, f32[2048,6144]{0,1:T(8,128)} %get-tuple-element.25, f32[2048]{0:T(1024)S(1)} %log_add_fusion.3), kind=kOutput, calls=%fused_computation.74 | convolution fusion | flops 3247699968 | bytes 52969472 | tf_op jit(solution)/shard_map/dot_general | solution.py:61
  441.4 26.0 %fusion.7 = bf16[2048,6144]{0,1:T(8,128)(2,1)} fusion(f32[2048,6144]{0,1:T(8,128)} %get-tuple-element.25, f32[2048]{0:T(1024)S(1)} %get-tuple-element.32, f32[2048]{0:T(1024)S(1)} %log_add_fusion.3, bf16[6144,512]{1,0:T(8,128)(2,1)} %copy-done.2, bf16[2048,512]{1,0:T(8,128)(2,1)S(1)} %copy-done.5), kind=kOutput, calls=%fused_computation.13 | convolution fusion | flops 3284140032 | bytes 77611008 | tf_op jit(solution)/shard_map/qd,cd->qc/dot_general | solution.py:67
  467.4 14.5 fusion.75
  481.9 19.8 %multiply_reduce_fusion = (f32[2048]{0:T(1024)S(1)}, bf16[2048,128]{0,1:T(8,128)(2,1)}) fusion(bf16[2048,128]{0,1:T(8,128)(2,1)S(1)} %copy-done.9, bf16[6144,512]{1,0:T(8,128)(2,1)} %copy-done.2, f32[2048,6144]{0,1:T(8,128)} %get-tuple-element.19, f32[2048]{0:T(1024)S(1)} %log_add_fusion), kind=kOutput, calls=%fused_computation.71 | convolution fusion | flops 3247699968 | bytes 52969472 | tf_op jit(solution)/shard_map/dot_general | solution.py:61
  501.7 26.0 %fusion.1 = bf16[2048,6144]{0,1:T(8,128)(2,1)} fusion(f32[2048,6144]{0,1:T(8,128)} %get-tuple-element.19, f32[2048]{0:T(1024)S(1)} %get-tuple-element.26, f32[2048]{0:T(1024)S(1)} %log_add_fusion, bf16[6144,512]{1,0:T(8,128)(2,1)} %copy-done.2, bf16[2048,512]{1,0:T(8,128)(2,1)S(1)} %copy-done.5), kind=kOutput, calls=%fused_computation.4 | convolution fusion | flops 3284140032 | bytes 77611008 | tf_op jit(solution)/shard_map/qd,cd->qc/dot_general | solution.py:67
  527.7 14.8 convolution_add_fusion.2
  542.6 19.7 %fusion.19 = f32[6144,128]{0,1:T(8,128)} fusion(f32[2048,6144]{0,1:T(8,128)} %get-tuple-element.21, f32[2048]{0:T(1024)S(1)} %log_add_fusion.1, bf16[2048,512]{1,0:T(8,128)(2,1)S(1)} %copy-done.5), kind=kOutput, calls=%fused_computation.41 | convolution fusion | flops 3246391296 | bytes 54009856 | tf_op jit(solution)/shard_map/qc,qd->cd/dot_general | solution.py:76
  562.3 19.7 %multiply_reduce_fusion.2 = (f32[2048]{0:T(1024)S(1)}, bf16[2048,128]{0,1:T(8,128)(2,1)}) fusion(bf16[2048,128]{0,1:T(8,128)(2,1)S(1)} %copy-done.7, bf16[6144,512]{1,0:T(8,128)(2,1)} %copy-done.2, f32[2048,6144]{0,1:T(8,128)} %get-tuple-element.23, f32[2048]{0:T(1024)S(1)} %copy-done.14), kind=kOutput, calls=%fused_computation.73 | convolution fusion | flops 3247699968 | bytes 52969472 | tf_op jit(solution)/shard_map/dot_general | solution.py:61
  582.0 20.7 %convolution_add_fusion = f32[6144,128]{0,1:T(8,128)} fusion(f32[6144,128]{0,1:T(8,128)} %fusion.19, f32[2048,6144]{0,1:T(8,128)} %get-tuple-element.19, f32[2048]{0:T(1024)S(1)} %log_add_fusion, bf16[2048,512]{1,0:T(8,128)(2,1)S(1)} %copy-done.5), kind=kOutput, calls=%fused_computation.36 | convolution fusion | flops 3247177728 | bytes 57155584 | tf_op jit(solution)/shard_map/qc,qd->cd/dot_general | solution.py:76
  605.6 19.7 %fusion.26 = f32[6144,128]{0,1:T(8,128)} fusion(f32[2048,6144]{0,1:T(8,128)} %get-tuple-element.25, f32[2048]{0:T(1024)S(1)} %log_add_fusion.3, bf16[2048,512]{1,0:T(8,128)(2,1)S(1)} %copy-done.5), kind=kOutput, calls=%fused_computation.44 | convolution fusion | flops 3246391296 | bytes 54009856 | tf_op jit(solution)/shard_map/qc,qd->cd/dot_general | solution.py:76
  625.3 26.1 %fusion.5 = bf16[2048,6144]{0,1:T(8,128)(2,1)} fusion(f32[2048,6144]{0,1:T(8,128)} %get-tuple-element.23, f32[2048]{0:T(1024)S(1)} %get-tuple-element.30, f32[2048]{0:T(1024)S(1)} %copy-done.14, bf16[6144,512]{1,0:T(8,128)(2,1)} %copy-done.2, bf16[2048,512]{1,0:T(8,128)(2,1)S(1)} %copy-done.5), kind=kOutput, calls=%fused_computation.10 | convolution fusion | flops 3284140032 | bytes 77611008 | tf_op jit(solution)/shard_map/qd,cd->qc/dot_general | solution.py:67
  651.4 141.4 %all-gather.4.cloned.1.call-done = bf16[8,512,512]{1,2,0:T(8,128)(2,1)} async-done(((bf16[8,128,512]{1,2,0:T(8,128)(2,1)}), bf16[8,512,512]{1,2,0:T(8,128)(2,1)}) %all-gather.4.cloned.1.call-update) | async-done | bytes 4194320 | tf_op jit(solution)/shard_map/all_gather | solution.py:130
  792.8 4.7 fusion.45
  797.6 16.0 %convolution_add_fusion.3 = f32[6144,128]{0,1:T(8,128)} fusion(f32[6144,128]{0,1:T(8,128)} %fusion.75, bf16[2048,6144]{0,1:T(8,128)(2,1)} %fusion.5, bf16[2048,512]{1,0:T(8,128)(2,1)} %param.10), kind=kOutput, calls=%fused_computation.39 | convolution fusion | flops 3222011904 | bytes 31981568 | tf_op jit(solution)/shard_map/qc,qd->cd/dot_general | solution.py:73
  813.6 20.9 %convolution_add_fusion.1 = f32[6144,128]{0,1:T(8,128)} fusion(f32[6144,128]{0,1:T(8,128)} %fusion.26, f32[2048,6144]{0,1:T(8,128)} %get-tuple-element.23, f32[2048]{0:T(1024)S(1)} %copy-done.14, bf16[2048,512]{1,0:T(8,128)(2,1)S(1)} %copy-done.5), kind=kOutput, calls=%fused_computation.37 | convolution fusion | flops 3247177728 | bytes 57155584 | tf_op jit(solution)/shard_map/qc,qd->cd/dot_general | solution.py:76
  834.5 5.2 pad_maximum_fusion
  839.7 4.2 fusion.88
  843.9 3.3 copy-done.3
  850.1 12.9 constant_dynamic-update-slice_fusion.5
  863.0 13.1 constant_dynamic-update-slice_fusion.4
  876.2 157.0 %collective-permute-done.2 = f32[2048,512]{0,1:T(8,128)} collective-permute-done((f32[2048,512]{0,1:T(8,128)}, f32[2048,512]{0,1:T(8,128)}, u32[]{:S(2)}, u32[]{:S(2)}) %collective-permute-start.2) | collective-permute-done | bytes 4194336 | tf_op jit(solution)/shard_map/ppermute | solution.py:15
  1033.2 180.2 %collective-permute-done.3 = f32[2048,512]{0,1:T(8,128)} collective-permute-done((f32[2048,512]{0,1:T(8,128)}, f32[2048,512]{0,1:T(8,128)}, u32[]{:S(2)}, u32[]{:S(2)}) %collective-permute-start.3) | collective-permute-done | bytes 4194336 | tf_op jit(solution)/shard_map/ppermute | solution.py:15
  1213.3 5.7 fusion.31
  1219.2 12.8 constant_dynamic-update-slice_fusion.3
  1232.0 12.6 constant_dynamic-update-slice_fusion.2
  1244.7 13.3 fusion.14
  1259.2 4.8 fusion.95
  1264.0 136.8 %reduce-scatter.6.cloned.1.call-done = f32[128,8,512]{0,2,1:T(8,128)} async-done(((f32[512,8,512]{0,2,1:T(8,128)}), f32[128,8,512]{0,2,1:T(8,128)}) %reduce-scatter.6.cloned.1.call-update) | async-done | bytes 2097168 | tf_op jit(solution)/shard_map/reduce_scatter | solution.py:112
  1400.8 9.4 convolution_bitcast_fusion
  1414.1 3.9 copy.20
  1427.0 128.6 %reduce-scatter.8.cloned.1.call-done = f32[128,8,512]{0,2,1:T(8,128)} async-done(((f32[512,8,512]{0,2,1:T(8,128)}), f32[128,8,512]{0,2,1:T(8,128)}) %reduce-scatter.8.cloned.1.call-update) | async-done | bytes 2097168 | tf_op jit(solution)/shard_map/reduce_scatter | solution.py:148
  (76 shorter events, 37.1 us)
Async XLA Ops:
  7.2 15.4 copy-start
  7.2 595.6 %reduce-scatter.4.cloned.1.call-start = ((), (), s32[]{:S(2)}) async-start(), calls=%async_computation.3 | async-start | bytes 10485760 | tf_op jit(solution)/shard_map/reduce_scatter | solution.py:120
  11.8 81.6 %collective-permute-start.1 = (bf16[2048,512]{1,0:T(8,128)(2,1)}, bf16[2048,512]{1,0:T(8,128)(2,1)}, u32[]{:S(2)}, u32[]{:S(2)}) collective-permute-start(bf16[2048,512]{1,0:T(8,128)(2,1)} %constant_dynamic-update-slice_fusion), channel_id=1, source_target_pairs={{0,4},{4,8},{8,12},{1,5},{5,9},{9,13},{2,6},{6,10},{10,14},{3,7},{... | collective-permute-start | bytes 6291464 | tf_op jit(solution)/shard_map/ppermute | solution.py:15
  18.1 164.1 %collective-permute-start = (bf16[2048,512]{1,0:T(8,128)(2,1)}, bf16[2048,512]{1,0:T(8,128)(2,1)}, u32[]{:S(2)}, u32[]{:S(2)}) collective-permute-start(bf16[2048,512]{1,0:T(8,128)(2,1)} %constant_dynamic-update-slice_fusion), channel_id=1, source_target_pairs={{0,8},{4,12},{1,9},{5,13},{2,10},{6,14},{3,11},{7,15},{16,24},{20,... | collective-permute-start | bytes 6291464 | tf_op jit(solution)/shard_map/ppermute | solution.py:15
  28.3 1.6 copy-start.4
  28.4 764.4 %all-gather.4.cloned.1.call-start = ((), (), s32[]{:S(2)}) async-start(), calls=%async_computation.4 | async-start | bytes 5242880 | tf_op jit(solution)/shard_map/all_gather | solution.py:130
  37.4 148.7 %copy-start.6 = (bf16[2048,512]{1,0:T(8,128)(2,1)S(1)}, bf16[2048,512]{1,0:T(8,128)(2,1)}, u32[]{:S(2)}) copy-start(bf16[2048,512]{1,0:T(8,128)(2,1)} %param.10) | copy-start | bytes 6291460
  186.1 155.6 %copy-start.2 = (bf16[6144,512]{1,0:T(8,128)(2,1)}, bf16[6144,512]{1,0:T(8,128)(2,1)S(1)}, u32[]{:S(2)}) copy-start(bf16[6144,512]{1,0:T(8,128)(2,1)S(1)} %pad_maximum_fusion.1) | copy-start | bytes 18874372
  322.3 19.5 %copy-start.10 = (bf16[2048,128]{0,1:T(8,128)(2,1)S(1)}, bf16[2048,128]{0,1:T(8,128)(2,1)}, u32[]{:S(2)}) copy-start(bf16[2048,128]{0,1:T(8,128)(2,1)} %copy.28) | copy-start | bytes 1572868
  341.8 19.6 %copy-start.5 = (bf16[2048,512]{1,0:T(8,128)(2,1)S(1)}, bf16[2048,512]{1,0:T(8,128)(2,1)}, u32[]{:S(2)}) copy-start(bf16[2048,512]{1,0:T(8,128)(2,1)} %param.13) | copy-start | bytes 6291460
  402.1 19.4 %copy-start.8 = (bf16[2048,128]{0,1:T(8,128)(2,1)S(1)}, bf16[2048,128]{0,1:T(8,128)(2,1)}, u32[]{:S(2)}) copy-start(bf16[2048,128]{0,1:T(8,128)(2,1)} %copy.26) | copy-start | bytes 1572868
  467.4 14.5 copy-start.9
  542.6 19.7 %copy-start.7 = (bf16[2048,128]{0,1:T(8,128)(2,1)S(1)}, bf16[2048,128]{0,1:T(8,128)(2,1)}, u32[]{:S(2)}) copy-start(bf16[2048,128]{0,1:T(8,128)(2,1)} %copy.27) | copy-start | bytes 1572868
  542.6 19.7 %copy-start.14 = (f32[2048]{0:T(1024)S(1)}, f32[2048]{0:T(1024)}, u32[]{:S(2)}) copy-start(f32[2048]{0:T(1024)} %log_add_fusion.2) | copy-start | bytes 24580
  605.5 652.8 %all-gather.6.cloned.1.call-start = ((), (), s32[]{:S(2)}) async-start(), calls=%async_computation.5 | async-start | bytes 5242880 | tf_op jit(solution)/shard_map/all_gather | solution.py:144
  797.5 466.5 %all-gather.8.cloned.1.call-start = ((), (), s32[]{:S(2)}) async-start(), calls=%async_computation.7 | async-start | bytes 5242880 | tf_op jit(solution)/shard_map/all_gather | solution.py:136
  839.7 7.6 copy-start.3
  847.3 185.9 %collective-permute-start.2 = (f32[2048,512]{0,1:T(8,128)}, f32[2048,512]{0,1:T(8,128)}, u32[]{:S(2)}, u32[]{:S(2)}) collective-permute-start(f32[2048,512]{0,1:T(8,128)} %get-tuple-element.10), channel_id=1, source_target_pairs={{4,0},{8,4},{12,8},{5,1},{9,5},{13,9},{6,2},{10,6},{14,10},{7,3},{... | collective-permute-start | bytes 12582920 | tf_op jit(solution)/shard_map/ppermute | solution.py:15
  848.5 364.8 %collective-permute-start.3 = (f32[2048,512]{0,1:T(8,128)}, f32[2048,512]{0,1:T(8,128)}, u32[]{:S(2)}, u32[]{:S(2)}) collective-permute-start(f32[2048,512]{0,1:T(8,128)} %get-tuple-element.11), channel_id=1, source_target_pairs={{8,0},{12,4},{9,1},{13,5},{10,2},{14,6},{11,3},{15,7},{24,16},{28,... | collective-permute-start | bytes 12582920 | tf_op jit(solution)/shard_map/ppermute | solution.py:15
  849.9 550.9 %reduce-scatter.6.cloned.1.call-start = ((), (), s32[]{:S(2)}) async-start(), calls=%async_computation.6 | async-start | bytes 10485760 | tf_op jit(solution)/shard_map/reduce_scatter | solution.py:112
  863.0 356.2 %slice-start = ((s8[6291456]{0:T(1024)(128)(4,1)}), s8[4194304]{0:T(1024)(128)(4,1)S(1)}, s32[]{:S(2)}) async-start(s8[6291456]{0:T(1024)(128)(4,1)} %bitcast.83), calls=%async_computation.9 | async-start | bytes 8388608
  863.0 356.2 %slice-start.1 = ((s8[6291456]{0:T(1024)(128)(4,1)}), s8[2097152]{0:T(1024)(128)(4,1)S(1)}, s32[]{:S(2)}) async-start(s8[6291456]{0:T(1024)(128)(4,1)} %bitcast.83), calls=%async_computation.10 | async-start | bytes 4194304
  1258.0 1.2 copy-start.13
  1258.0 297.5 %reduce-scatter.8.cloned.1.call-start = ((), (), s32[]{:S(2)}) async-start(), calls=%async_computation.8 | async-start | bytes 10485760 | tf_op jit(solution)/shard_map/reduce_scatter | solution.py:148
  1410.2 1.0 copy-start.11
  1410.2 1.2 copy-start.12
  1420.5 138.0 %copy-start.1 = (bf16[8,128,512]{2,1,0:T(8,128)(2,1)S(1)}, bf16[8,128,512]{2,1,0:T(8,128)(2,1)}, u32[]{:S(2)}) copy-start(bf16[8,128,512]{2,1,0:T(8,128)(2,1)} %param.18) | copy-start | bytes 3145732
Sparse Core Ops, SparseCore 0:
  28.5 236.1 reduce-scatter.3
  605.6 187.1 all-gather.3
  797.6 95.2 all-gather.5
  894.4 119.9 all-gather.7
  1258.1 142.6 reduce-scatter.5
  1410.3 145.1 reduce-scatter.7
where the time goes:
time: 1580 us; the launch traced here: 1570 us
  waiting for transfers between devices  889 us (56%)
  matrix products  510 us (32%)
  other arithmetic  100 us (6%)
  local copies, waits for them, and re-layouts  37.4 us (2%)
    ppermute x4, waiting for transfers between devices, shifted(): return lax.ppermute(x, axis, pairs)  482 us
    all_gather x1, waiting for transfers between devices, per_device(): lax.all_gather(right_turn, 'seq', axis=1, tiled=True)  141 us
    reduce_scatter x1, waiting for transfers between devices, per_device(): lax.psum_scatter(term.reshape(share_rows * lax.axis_size('seq'), local_bl...  137 us
    reduce_scatter x1, waiting for transfers between devices, per_device(): lax.psum_scatter(jnp.einsum('brk,brj->kbj', left_new, inner, preferred_el...  129 us
    dot_general x4, matrix products, per_device(): jnp.einsum('qd,cd->qc', g_block, v_block, preferred_element_type=jnp.floa...  104 us
    dot_general x4, matrix products, per_device(): jnp.einsum('qd,cd->qc', q_block, k_block, preferred_element_type=jnp.floa...  96.8 us
    dot_general x4, matrix products, per_device(): jnp.einsum('qc,qd->cd', weights_bf, g_block, preferred_element_type=jnp.f...  81.1 us
    dot_general x4, matrix products, per_device(): jnp.dot(weights_bf, v_block, preferred_element_type=jnp.float32)  78.9 us
  transfers between devices with their start and end apart: 10, of which 7 were waited for; matrix products, arithmetic and copies ran while one was open for 39% of the time, Pallas kernels for 0%

commit v1 on v0

v1 whole, which is shorter than its diff:
```python
import functools

import jax
import jax.numpy as jnp
from jax import lax
from jax.experimental import pallas as pl
from jax.experimental.pallas import tpu as pltpu
from jax.sharding import PartitionSpec as P

HEAD_DIM = 128
NEG = -1e30
LOG2E = 1.4426950408889634
NT = (((1,), (1,)), ((), ()))
NN = (((1,), (0,)), ((), ()))


def mm(a, b, dims):
    return lax.dot_general(a, b, dims, preferred_element_type=jnp.float32)


def attn_body(reach, tile, group, bk, q_ref, g_ref, bias_ref, *rest):
    kv_refs = rest[: reach + 1]
    o_ref, dq_ref, far_ref, own_ref, kb, vb, kt, vt, s_buf, e_buf, dkt, dvt = rest[reach + 1:]
    hd = HEAD_DIM
    t = pl.program_id(0)
    rows = kv_refs[0].shape[0]
    win = reach * rows
    cols = group * tile
    scale = hd ** -0.5

    @pl.when(t == 0)
    def _():
        for s, ref in enumerate(kv_refs):
            here = pl.ds(s * rows, rows)
            k = ref[:, :hd]
            v = ref[:, hd:]
            kb[here, :hd] = k
            kb[here, hd:] = bias_ref[here, :]
            vb[here, :] = v
            kt[:, here] = k.T
            vt[:hd, here] = v.T
        vt[hd:, :] = jnp.ones((16, win + rows), jnp.bfloat16)
        dkt[...] = jnp.zeros_like(dkt)
        dvt[...] = jnp.zeros_like(dvt)

    q = jnp.concatenate([q_ref[:, h * hd:(h + 1) * hd] for h in range(group)], axis=0)
    g = jnp.concatenate([g_ref[:, h * hd:(h + 1) * hd] for h in range(group)], axis=0)
    lane = lax.broadcasted_iota(jnp.int32, (cols, hd), 1)
    qa = jnp.concatenate([q, jnp.where(lane == 0, 1.0, 0.0).astype(jnp.bfloat16)], axis=1)
    base = t * tile
    n_full = win - tile

    ki = lax.broadcasted_iota(jnp.int32, (tile, cols), 0)
    qi = lax.broadcasted_iota(jnp.int32, (tile, cols), 1) % tile

    def scores(off, size, keep=None):
        at = pl.ds(pl.multiple_of(base + off, tile), size)
        s = mm(kb[at, :], qa, NT)
        if keep is not None:
            s = jnp.where(keep, s, NEG)
        s_buf[pl.ds(off, size), :] = s
        return jnp.max(s.reshape(size // 8, 8, cols), axis=0)

    m8 = jnp.maximum(scores(0, tile, ki > qi), scores(win, tile, ki <= qi))
    m8 = lax.fori_loop(
        0, n_full // bk,
        lambda i, m: jnp.maximum(m, scores(pl.multiple_of(tile + i * bk, tile), bk)), m8)
    m = jnp.max(m8, axis=0, keepdims=True)
    mc = m * (scale * LOG2E)

    def weigh(off, size):
        at = pl.ds(pl.multiple_of(base + off, tile), size)
        e = jnp.exp2(s_buf[pl.ds(off, size), :] * (scale * LOG2E) - mc).astype(jnp.bfloat16)
        e_buf[pl.ds(off, size), :] = e
        return mm(vt[:, at], e, NN)

    ot = weigh(0, tile) + weigh(win, tile)
    ot = lax.fori_loop(
        0, n_full // bk,
        lambda i, a: a + weigh(pl.multiple_of(tile + i * bk, tile), bk), ot)
    rl = 1.0 / ot[hd:hd + 1, :]
    on = (ot[:hd, :] * rl).astype(jnp.bfloat16)
    on32 = on.astype(jnp.float32)
    gt = g.astype(jnp.float32).T
    qt = q.astype(jnp.float32).T
    dd = jnp.sum(gt * on32, axis=0, keepdims=True)
    for h in range(group):
        o_ref[:, h * hd:(h + 1) * hd] = on32[:, h * tile:(h + 1) * tile].T.astype(jnp.bfloat16)
    glt = (gt * rl).astype(jnp.bfloat16)
    rs = rl * scale
    qrt = (qt * rs).astype(jnp.bfloat16)

    def back(off, size):
        at = pl.ds(pl.multiple_of(base + off, tile), size)
        e = e_buf[pl.ds(off, size), :]
        dp = mm(vb[at, :], g, NT) - dd
        ds = (e.astype(jnp.float32) * dp).astype(jnp.bfloat16)
        dvt[:, at] += mm(glt, e, NT)
        dkt[:, at] += mm(qrt, ds, NT)
        return mm(kt[:, at], ds, NN)

    dqt = back(0, tile) + back(win, tile)
    dqt = lax.fori_loop(
        0, n_full // bk,
        lambda i, a: a + back(pl.multiple_of(tile + i * bk, tile), bk), dqt)
    dqt = dqt * rs
    for h in range(group):
        dq_ref[:, h * hd:(h + 1) * hd] = dqt[:, h * tile:(h + 1) * tile].T.astype(jnp.bfloat16)

    @pl.when(t == pl.num_programs(0) - 1)
    def _():
        for s in range(reach + 1):
            here = pl.ds(s * rows, rows)
            dk = dkt[:, here].T
            dv = dvt[:, here].T
            if s < reach:
                far_ref[here, :hd] = dk.astype(jnp.bfloat16)
                far_ref[here, hd:] = dv.astype(jnp.bfloat16)
            else:
                own_ref[:, :hd] = dk
                own_ref[:, hd:] = dv


def attention(queries, out_grad, bias, shards, slot, group, tile=256, bk=1920):
    hd = HEAD_DIM
    rows = queries.shape[0]
    reach = len(shards) - 1
    win = reach * rows
    total = win + rows
    cols = group * tile
    while (win - tile) % bk:
        bk -= tile
    whole = lambda shape: pl.BlockSpec(shape, lambda t: (0, 0), pipeline_mode=pl.Buffered(1))
    part = pl.BlockSpec((tile, group * hd), lambda t: (t, slot))
    outp = pl.BlockSpec((tile, group * hd), lambda t: (t, 0))
    area = win * rows * group
    return pl.pallas_call(
        functools.partial(attn_body, reach, tile, group, bk),
        out_shape=(
            jax.ShapeDtypeStruct((rows, group * hd), jnp.bfloat16),
            jax.ShapeDtypeStruct((rows, group * hd), jnp.bfloat16),
            jax.ShapeDtypeStruct((win, 2 * hd), jnp.bfloat16),
            jax.ShapeDtypeStruct((rows, 2 * hd), jnp.float32),
        ),
        grid=(rows // tile,),
        in_specs=[part, part, whole((total, hd))] + [whole((rows, 2 * hd))] * (reach + 1),
        out_specs=(outp, outp, whole((win, 2 * hd)), whole((rows, 2 * hd))),
        scratch_shapes=[
            pltpu.VMEM((total, 2 * hd), jnp.bfloat16),
            pltpu.VMEM((total, hd), jnp.bfloat16),
            pltpu.VMEM((hd, total), jnp.bfloat16),
            pltpu.VMEM((hd + 16, total), jnp.bfloat16),
            pltpu.VMEM((win + tile, cols), jnp.float32),
            pltpu.VMEM((win + tile, cols), jnp.bfloat16),
            pltpu.VMEM((hd, total), jnp.float32),
            pltpu.VMEM((hd, total), jnp.float32),
        ],
        compiler_params=pltpu.CompilerParams(
            dimension_semantics=("arbitrary",), vmem_limit_bytes=60 << 20),
        cost_estimate=pl.CostEstimate(
            flops=12 * area * hd, bytes_accessed=16 << 20, transcendentals=area),
        name="window_attention",
    )(queries, out_grad, bias, *shards)


moment_decay = 0.8


def shifted(x, axis, by):
    length = lax.axis_size(axis)
    pairs = [(i, i + by) for i in range(length) if 0 <= i + by < length]
    return lax.ppermute(x, axis, pairs)


def after(value, *others):
    return lax.optimization_barrier((value,) + others)[0]


def row_split_refresh(grad_term_sum, moment, left_old, left_new, right_old, right_new):
    turn_share = lax.psum_scatter(
        jnp.einsum("brk,brj->kbj", right_old, right_new, preferred_element_type=jnp.float32),
        "seq", scatter_dimension=0, tiled=True)
    right_turn = jnp.transpose(turn_share, (1, 0, 2)).astype(jnp.bfloat16)
    turned = jnp.einsum(
        "brk,bkj->brj", moment, lax.all_gather(right_turn, "seq", axis=1, tiled=True),
        preferred_element_type=jnp.float32).astype(jnp.bfloat16)
    carried = jnp.einsum(
        "brk,bkj->brj", left_old, lax.all_gather(turned, "seq", axis=1, tiled=True),
        preferred_element_type=jnp.float32)
    grad_term = jnp.einsum(
        "brk,bkj->brj", grad_term_sum, lax.all_gather(right_new, "seq", axis=1, tiled=True),
        preferred_element_type=jnp.float32)
    inner = (moment_decay * carried + (1.0 - moment_decay) * grad_term).astype(jnp.bfloat16)
    new_share = lax.psum_scatter(
        jnp.einsum("brk,brj->kbj", left_new, inner, preferred_element_type=jnp.float32),
        "seq", scatter_dimension=0, tiled=True)
    return jnp.transpose(new_share, (1, 0, 2))


def bmm(spec, a, b):
    return jnp.einsum(spec, a, b, preferred_element_type=jnp.float32)


def per_device(
    queries, keys, values, out_grad, layer_input, moment, left_old, left_new, right_old, right_new
):
    n = lax.axis_size("seq")
    reach = n // 2
    seq_index = lax.axis_index("seq")
    rows = queries.shape[0]
    hd = HEAD_DIM
    kv_count = keys.shape[1] // hd
    group = queries.shape[1] // keys.shape[1]
    blocks, share_rows, order = moment.shape
    row_blocks = layer_input.shape[1] // order
    whole_blocks = row_blocks % n == 0 and (group + 2) * hd == order
    per_owner = row_blocks // n

    pairs = [
        jnp.concatenate([keys[:, k * hd:(k + 1) * hd], values[:, k * hd:(k + 1) * hd]], axis=1)
        for k in range(kv_count)
    ]
    key_row = lax.broadcasted_iota(jnp.int32, ((reach + 1) * rows, hd), 0)
    key_col = lax.broadcasted_iota(jnp.int32, ((reach + 1) * rows, hd), 1)
    bias = jnp.where(
        (key_row < (reach - seq_index) * rows) & (key_col == 0), NEG, 0.0).astype(jnp.bfloat16)

    windows = []
    gate = None
    for k in range(kv_count):
        held = pairs[k] if gate is None else after(pairs[k], gate)
        shards = [pairs[k]]
        if k == 0:
            for _ in range(reach):
                held = shifted(held, "seq", 1)
                shards.insert(0, held)
            gate = held
        else:
            for d in range(1, reach + 1):
                shards.insert(0, shifted(held, "seq", d))
        windows.append(shards)

    if whole_blocks:
        cut = [
            x.reshape(kv_count, n, per_owner, share_rows, order)
            for x in (moment, left_old, left_new, right_old, right_new)
        ]

        def message(owner):
            return jnp.stack([
                lax.dynamic_slice_in_dim(x, owner, 1, 1)[:, 0] for x in cut])

        whole = jnp.zeros((5, kv_count, per_owner, n, share_rows, order), jnp.bfloat16)
        whole = lax.dynamic_update_slice_in_dim(
            whole, message(seq_index)[:, :, :, None], seq_index, 3)
        leftward = []
        for d in range(1, n):
            packed = after(message((seq_index + n - d) % n), windows[0][reach - 1])
            leftward.append(shifted(packed, "seq", -d))
        rightward = []
    outs, query_grads, key_grads, value_grads, news, joined = [], [], [], [], [], []
    for k in range(kv_count):
        mask = after(bias, *leftward) if whole_blocks and k == 1 else bias
        head_out, head_dq, far, own = attention(
            queries, out_grad, mask, windows[k], k, group)
        if whole_blocks and k == 0:
            for d in range(1, n):
                packed = after(message((seq_index + d) % n), head_out)
                rightward.append(shifted(packed, "seq", d))
        outs.append(head_out)
        query_grads.append(head_dq)
        own = own.astype(jnp.float32)
        if k < kv_count - 1:
            for d in range(1, reach + 1):
                back = shifted(far[(reach - d) * rows:(reach - d + 1) * rows], "seq", -d)
                own = own + back.astype(jnp.float32)
        else:
            carry = far[:rows]
            for d in range(reach, 0, -1):
                carry = shifted(carry, "seq", -1)
                if whole_blocks and d == reach:
                    carry = after(carry, *rightward)
                carry = carry.astype(jnp.float32)
                if d > 1:
                    carry = (carry + far[(reach - d + 1) * rows:(reach - d + 2) * rows].astype(jnp.float32)).astype(jnp.bfloat16)
            own = own + carry
        kv_grad = own.astype(jnp.bfloat16)
        key_grads.append(kv_grad[:, :hd])
        value_grads.append(kv_grad[:, hd:])
        columns = jnp.concatenate([head_dq, kv_grad], axis=1)
        joined.append(columns)
        if whole_blocks and k == 0:
            for d in range(1, n):
                source = (seq_index + d) % n
                piece = jnp.where(seq_index + d < n, leftward[d - 1], rightward[n - d - 1])
                whole = lax.dynamic_update_slice_in_dim(whole, piece[:, :, :, None], source, 3)
            m_own, lo_own, ln_own, ro_own, rn_own = whole.reshape(
                5, kv_count, per_owner, order, order)
            right_turn = bmm("cbrk,cbrj->cbkj", ro_own, rn_own).astype(jnp.bfloat16)
            turned = bmm("cbrk,cbkj->cbrj", m_own, right_turn).astype(jnp.bfloat16)
            carried = moment_decay * bmm("cbrk,cbkj->cbrj", lo_own, turned)
        if whole_blocks:
            term = bmm("tk,tj->kj", layer_input, columns).astype(jnp.bfloat16)
            terms = lax.all_to_all(term.reshape(n, per_owner, order, order), "seq", 0, 0)
            grad = jnp.sum(terms.astype(jnp.float32), axis=0).astype(jnp.bfloat16)
            inner = carried[k] + (1.0 - moment_decay) * bmm("brk,bkj->brj", grad, rn_own[k])
            new = bmm("brk,brj->bkj", ln_own[k], inner.astype(jnp.bfloat16)).astype(jnp.bfloat16)
            new = jnp.transpose(new.reshape(per_owner, n, share_rows, order), (1, 0, 2, 3))
            new = lax.all_to_all(new, "seq", 0, 0)
            news.append(new.reshape(row_blocks, share_rows, order).astype(jnp.float32))
    if whole_blocks:
        new_moment = jnp.concatenate(news, axis=0)
    else:
        joined = jnp.concatenate(joined, axis=1)
        term = bmm(
            "trk,tcj->kcrj",
            layer_input.reshape(rows, row_blocks, order),
            joined.reshape(rows, joined.shape[1] // order, order))
        share = lax.psum_scatter(
            term.reshape(order, blocks, order), "seq", scatter_dimension=0, tiled=True)
        new_moment = row_split_refresh(
            jnp.transpose(share, (1, 0, 2)).astype(jnp.bfloat16),
            moment, left_old, left_new, right_old, right_new)
    join = lambda parts: parts[0] if len(parts) == 1 else jnp.concatenate(parts, axis=1)
    return (join(outs), join(query_grads), join(key_grads), join(value_grads), new_moment)


def solution(mesh):
    both = P(("groups", "seq"), "grid")
    block = P(("groups", "grid"), "seq", None)
    return jax.shard_map(
        per_device,
        mesh=mesh,
        in_specs=(both, both, both, both, P(("groups", "seq"), None)) + (block,) * 5,
        out_specs=(both, both, both, both, block),
        check_vma=False,
    )
```

time: 1580 us -> 447 us (0.28)
  waiting for transfers between devices: 889 us -> 122 us
  matrix products: 510 us -> 31.3 us
  Pallas kernels: 0 us -> 161 us
  other arithmetic: 100 us -> 26.3 us
  starting transfers between devices: 14 us -> 65 us
    dot_general x29 -> x6, matrix products: 510 us -> 31.3 us  [bmm(): return jnp.einsum(spec, a, b, preferred_element_type=jnp.float32)]
    ppermute x4 -> x14, waiting for transfers between devices: 482 us -> 88 us  [shifted(): return lax.ppermute(x, axis, pairs)]
    reduce_scatter x3 -> x0, waiting for transfers between devices: 265 us -> none  [the longest x1 137 us: per_device(): lax.psum_scatter(term.reshape(share_rows * lax.axis_size('seq'), local_bl...]
    pallas_call x0 -> x2, Pallas kernels: none -> 161 us  [attention(): pl.pallas_call(functools.partial(attn_body, reach, tile, group, bk), out_...]
    all_gather x3 -> x0, waiting for transfers between devices: 141 us -> none  [the longest x1 141 us: per_device(): lax.all_gather(right_turn, 'seq', axis=1, tiled=True)]
    reduce_sum x4 -> x2, other arithmetic: 77.6 us -> 3.42 us  [per_device(): grad = jnp.sum(terms.astype(jnp.float32), axis=0).astype(jnp.bfloat16)]
    all_to_all x0 -> x4, waiting for transfers between devices: none -> 34.5 us  [the longest x2 19.2 us: per_device(): new = lax.all_to_all(new, 'seq', 0, 0)]
    ppermute x4 -> x14, starting transfers between devices: 13.3 us -> 42.2 us  [shifted(): return lax.ppermute(x, axis, pairs)]
  transfers between devices with their start and end apart: 10 -> 18, of which waited for: 7 -> 8; matrix products, arithmetic and copies ran while one was open for 39% -> 20% of each run, Pallas kernels for 0% -> 36%
where the time goes in v1:
time: 447 us; the launch traced here: 446 us
  Pallas kernels  161 us (36%)
  waiting for transfers between devices  122 us (27%)
  starting transfers between devices  65 us (15%)
  local copies, waits for them, and re-layouts  39 us (9%)
  matrix products  31.3 us (7%)
  other arithmetic  26.3 us (6%)
    pallas_call x2, Pallas kernels, attention(): pl.pallas_call(functools.partial(attn_body, reach, tile, group, bk), out_...  161 us
    ppermute x14, waiting for transfers between devices, shifted(): return lax.ppermute(x, axis, pairs)  88 us
    ppermute x14, starting transfers between devices, shifted(): return lax.ppermute(x, axis, pairs)  42.2 us
    dot_general x6, matrix products, bmm(): return jnp.einsum(spec, a, b, preferred_element_type=jnp.float32)  31.3 us
    all_to_all x2, waiting for transfers between devices, per_device(): new = lax.all_to_all(new, 'seq', 0, 0)  19.2 us
    all_to_all x2, waiting for transfers between devices, per_device(): lax.all_to_all(term.reshape(n, per_owner, order, order), 'seq', 0, 0)  15.2 us
    all_to_all x2, starting transfers between devices, per_device(): lax.all_to_all(term.reshape(n, per_owner, order, order), 'seq', 0, 0)  15 us
    reshape x4, local copies, waits for them, and re-layouts, per_device(): term.reshape(n, per_owner, order, order)  12.8 us
  transfers between devices with their start and end apart: 18, of which 8 were waited for; matrix products, arithmetic and copies ran while one was open for 20% of the time, Pallas kernels for 36%

profile of v1, /device:TPU:0, one launch (start us, length us, event | category | flops | bytes accessed | tf_op | source)
XLA Modules:
  0.0 446.1 jit_solution(12617991276175283142)
XLA Ops:
  0.6 1.7 fusion.21
  3.4 5.9 %collective-permute-start = (bf16[2048,256]{1,0:T(8,128)(2,1)}, bf16[2048,256]{1,0:T(8,128)(2,1)}, u32[]{:S(2)}, u32[]{:S(2)}) collective-permute-start(bf16[2048,256]{1,0:T(8,128)(2,1)} %pad_maximum_fusion.4.rest_2_), channel_id=1, source_target_pairs={{0,4},{4,8},{8,12},{1,5},{5,9},{9,13},{2,6},{6,10},{10,14},{3,7},{... | collective-permute-start | bytes 3145736 | tf_op jit(solution)/shard_map/ppermute | solution.py:172
  15.6 15.4 %collective-permute-done.rest_1_ = bf16[2048,256]{1,0:T(8,128)(2,1)} collective-permute-done((bf16[2048,256]{1,0:T(8,128)(2,1)}, bf16[2048,256]{1,0:T(8,128)(2,1)}, u32[]{:S(2)}, u32[]{:S(2)}) %collective-permute-start) | collective-permute-done | bytes 1048608 | tf_op jit(solution)/shard_map/ppermute | solution.py:172
  31.0 5.4 %collective-permute-start.1 = (bf16[2048,256]{1,0:T(8,128)(2,1)}, bf16[2048,256]{1,0:T(8,128)(2,1)}, u32[]{:S(2)}, u32[]{:S(2)}) collective-permute-start(bf16[2048,256]{1,0:T(8,128)(2,1)} %collective-permute-done.rest_1_), channel_id=1, source_target_pairs={{0,4},{4,8},{8,12},{1,5},{5,9},{9,13},{2,6},{6,10},{10,14},{3,7},{... | collective-permute-start | bytes 3145736 | tf_op jit(solution)/shard_map/ppermute | solution.py:172
  36.5 3.9 select_convert_fusion.bias_ref
  44.3 13.0 %collective-permute-done.1.rest_0_ = bf16[2048,256]{1,0:T(8,128)(2,1)} collective-permute-done((bf16[2048,256]{1,0:T(8,128)(2,1)}, bf16[2048,256]{1,0:T(8,128)(2,1)}, u32[]{:S(2)}, u32[]{:S(2)}) %collective-permute-start.1) | collective-permute-done | bytes 1048608 | tf_op jit(solution)/shard_map/ppermute | solution.py:172
  57.3 5.4 %collective-permute-start.6 = (bf16[2048,256]{1,0:T(8,128)(2,1)}, bf16[2048,256]{1,0:T(8,128)(2,1)}, u32[]{:S(2)}, u32[]{:S(2)}) collective-permute-start(bf16[2048,256]{1,0:T(8,128)(2,1)} %pad_maximum_fusion.5.rest_2_), channel_id=1, source_target_pairs={{0,4},{4,8},{8,12},{1,5},{5,9},{9,13},{2,6},{6,10},{10,14},{3,7},{... | collective-permute-start | bytes 3145736 | tf_op jit(solution)/shard_map/ppermute | solution.py:172
  62.7 4.5 %collective-permute-start.5 = (bf16[2048,256]{1,0:T(8,128)(2,1)}, bf16[2048,256]{1,0:T(8,128)(2,1)}, u32[]{:S(2)}, u32[]{:S(2)}) collective-permute-start(bf16[2048,256]{1,0:T(8,128)(2,1)} %pad_maximum_fusion.5.rest_2_), channel_id=1, source_target_pairs={{0,8},{4,12},{1,9},{5,13},{2,10},{6,14},{3,11},{7,15},{16,24},{20,... | collective-permute-start | bytes 3145736 | tf_op jit(solution)/shard_map/ppermute | solution.py:172
  67.2 80.5 %window_attention.2 = (bf16[2048,256]{1,0:T(8,128)(2,1)}, bf16[2048,256]{1,0:T(8,128)(2,1)}, bf16[4096,256]{1,0:T(8,128)(2,1)}, f32[2048,256]{1,0:T(8,128)}) custom-call(bf16[2048,512]{1,0:T(8,128)(2,1)} %q_ref.3, bf16[2048,512]{1,0:T(8,128)(2,1)} %g_ref.3, bf16[6144,128]{1,0:T(8,128)(2,1)} %select_convert_fusion.bias_ref, ...), custom_call_target="tpu_custom_call" | custom-call | flops 25769803776 | bytes 16777216 | tf_op jit(solution)/shard_map/window_attention/pallas_call | solution.py:137
  147.7 3.1 fusion.18
  152.1 6.4 %collective-permute-done.3 = bf16[5,2,1,128,512]{4,3,1,0,2:T(8,128)(2,1)S(1)} collective-permute-done((bf16[5,2,1,128,512]{4,3,1,0,2:T(8,128)(2,1)}, bf16[5,2,1,128,512]{4,3,1,0,2:T(8,128)(2,1)S(1)}, u32[]{:S(2)}, u32[]{:S(2)}) %collective-permute-start.3) | collective-permute-done | bytes 1310752 | tf_op jit(solution)/shard_map/ppermute | solution.py:172
  159.7 3.3 collective-permute-start.12
  163.0 6.0 %collective-permute-start.11 = (bf16[5,2,1,128,512]{4,3,1,0,2:T(8,128)(2,1)}, bf16[5,2,1,128,512]{4,3,1,0,2:T(8,128)(2,1)}, u32[]{:S(2)}, u32[]{:S(2)}) collective-permute-start(bf16[5,2,1,128,512]{4,3,1,0,2:T(8,128)(2,1)} %get-tuple-element.36), channel_id=1, source_target_pairs={{0,8},{4,12},{1,9},{5,13},{2,10},{6,14},{3,11},{7,15},{16,24},{20,... | collective-permute-start | bytes 3932168 | tf_op jit(solution)/shard_map/ppermute | solution.py:172
  169.0 2.4 collective-permute-start.10
  171.5 80.5 %window_attention.3 = (bf16[2048,256]{1,0:T(8,128)(2,1)}, bf16[2048,256]{1,0:T(8,128)(2,1)}, bf16[4096,256]{1,0:T(8,128)(2,1)}, f32[2048,256]{1,0:T(8,128)}) custom-call(bf16[2048,512]{1,0:T(8,128)(2,1)} %q_ref.3, bf16[2048,512]{1,0:T(8,128)(2,1)} %g_ref.3, bf16[6144,128]{1,0:T(8,128)(2,1)} %select_convert_fusion.bias_ref, ...), custom_call_target="tpu_custom_call" | custom-call | flops 25769803776 | bytes 16777216 | tf_op jit(solution)/shard_map/window_attention/pallas_call | solution.py:137
  252.0 2.4 slice.76
  255.8 2.1 add_convert_fusion.2
  257.9 9.2 %fusion = bf16[2048,512]{0,1:T(8,128)(2,1)} fusion(bf16[2048,2048]{1,0:T(8,128)(2,1)} %param.14, bf16[2048,256]{1,0:T(8,128)(2,1)S(1)} %copy-done.16, bf16[2048,256]{1,0:T(8,128)(2,1)S(1)} %add_convert_fusion.2), kind=kOutput, calls=%fused_computation.3 | convolution fusion | flops 4300210176 | bytes 12582912 | tf_op jit(solution)/shard_map/tk,tj->kj/dot_general | solution.py:201
  267.1 3.3 reshape.138
  270.4 1.7 copy.15
  272.1 3.9 all-to-all-start
  276.1 11.3 %collective-permute-done.9 = bf16[2048,256]{1,0:T(8,128)(2,1)} collective-permute-done((bf16[2048,256]{1,0:T(8,128)(2,1)}, bf16[2048,256]{1,0:T(8,128)(2,1)}, u32[]{:S(2)}, u32[]{:S(2)}) %collective-permute-start.9) | collective-permute-done | bytes 1048608 | tf_op jit(solution)/shard_map/ppermute | solution.py:172
  287.4 1.8 add_convert_fusion.1
  289.2 1.5 collective-permute-start.13
  290.7 41.9 %collective-permute-done.13 = bf16[2048,256]{1,0:T(8,128)(2,1)S(1)} collective-permute-done((bf16[2048,256]{1,0:T(8,128)(2,1)S(1)}, bf16[2048,256]{1,0:T(8,128)(2,1)S(1)}, u32[]{:S(2)}, u32[]{:S(2)}) %collective-permute-start.13) | collective-permute-done | bytes 1048608 | tf_op jit(solution)/shard_map/ppermute | solution.py:172
  333.9 9.2 %fusion.1 = bf16[2048,512]{0,1:T(8,128)(2,1)} fusion(bf16[2048,2048]{1,0:T(8,128)(2,1)} %param.14, bf16[2048,256]{1,0:T(8,128)(2,1)S(1)} %add_convert_fusion, bf16[2048,256]{1,0:T(8,128)(2,1)S(1)} %copy-done.18), kind=kOutput, calls=%fused_computation.4 | convolution fusion | flops 4300210176 | bytes 12582912 | tf_op jit(solution)/shard_map/tk,tj->kj/dot_general | solution.py:201
  343.2 4.5 %reshape.141 = bf16[4,1,512,512]{2,0,3,1:T(4,128)(2,1)} reshape(bf16[2048,512]{0,1:T(8,128)(2,1)} %fusion.1) | data formatting | bytes 4194304 | tf_op jit(solution)/shard_map/reshape | solution.py:304
  347.6 3.3 copy.18
  351.0 11.1 %all-to-all-start.2 = ((bf16[4,1,512,512]{2,3,1,0:T(8,128)(2,1)}), bf16[4,1,512,512]{2,3,1,0:T(8,128)(2,1)}, u32[]{:S(2)}, u32[]{:S(2)}) async-start(bf16[4,1,512,512]{2,3,1,0:T(8,128)(2,1)} %copy.18), calls=%async_computation.2 | async-start | bytes 4194304 | tf_op jit(solution)/shard_map/all_to_all | solution.py:304
  362.0 2.9 broadcast_in_dim.25
  364.9 2.5 bitcast_dynamic-update-slice_fusion.3
  367.4 3.2 pad_maximum_fusion.1
  370.6 1.5 pad_maximum_fusion.3
  372.4 1.5 bitcast_dynamic-update-slice_fusion.2
  373.9 1.4 bitcast_dynamic-update-slice_fusion.1
  376.8 2.9 fusion.16
  379.7 3.9 fusion.17
  383.7 1.8 convolution_convert_fusion.3
  385.5 4.5 %convolution_multiply_fusion = f32[2,512,512]{2,1,0:T(8,128)} fusion(bf16[2,512,512]{2,1,0:T(8,128)(2,1)} %bitcast.110, bf16[2,512,512]{2,1,0:T(8,128)(2,1)} %bitcast.109, bf16[2,512,512]{2,1,0:T(8,128)(2,1)} %convolution_convert_fusion.3), kind=kOutput, calls=%fused_computation.15 | convolution fusion | flops 1074790400 | bytes 5242880 | tf_op jit(solution)/shard_map/cbrk,cbkj->cbrj/dot_general | solution.py:201
  391.2 3.3 convolution_convert_fusion.5
  394.5 15.2 %all-to-all-done.2 = bf16[4,1,512,512]{2,3,1,0:T(8,128)(2,1)} async-done(((bf16[4,1,512,512]{2,3,1,0:T(8,128)(2,1)}), bf16[4,1,512,512]{2,3,1,0:T(8,128)(2,1)}, u32[]{:S(2)}, u32[]{:S(2)}) %all-to-all-start.2) | async-done | bytes 2097184 | tf_op jit(solution)/shard_map/all_to_all | solution.py:304
  409.8 4.4 all-to-all-start.1
  414.3 2.2 reduce_sum.25
  416.5 3.2 convolution_convert_fusion.4
  419.7 7.8 %all-to-all-done.1 = bf16[4,1,128,512]{3,2,1,0:T(8,128)(2,1)S(1)} async-done(((bf16[4,1,128,512]{3,2,1,0:T(8,128)(2,1)}), bf16[4,1,128,512]{3,2,1,0:T(8,128)(2,1)S(1)}, u32[]{:S(2)}, u32[]{:S(2)}) %all-to-all-start.1) | async-done | bytes 524320 | tf_op jit(solution)/shard_map/all_to_all | solution.py:309
  427.5 3.5 all-to-all-start.3
  433.2 11.5 %all-to-all-done.3 = bf16[4,1,128,512]{3,2,1,0:T(8,128)(2,1)S(1)} async-done(((bf16[4,1,128,512]{3,2,1,0:T(8,128)(2,1)}), bf16[4,1,128,512]{3,2,1,0:T(8,128)(2,1)S(1)}, u32[]{:S(2)}, u32[]{:S(2)}) %all-to-all-start.3) | async-done | bytes 524320 | tf_op jit(solution)/shard_map/all_to_all | solution.py:309
  444.7 1.5 maximum_convert_fusion
  (70 shorter events, 21.8 us)
Async XLA Ops:
  2.3 7.0 %copy-start.10 = (bf16[8,128,512]{2,1,0:T(8,128)(2,1)S(1)}, bf16[8,128,512]{2,1,0:T(8,128)(2,1)}, u32[]{:S(2)}) copy-start(bf16[8,128,512]{2,1,0:T(8,128)(2,1)} %param.15) | copy-start | bytes 3145732
  2.3 8.1 %copy-start.11 = (bf16[8,128,512]{2,1,0:T(8,128)(2,1)S(1)}, bf16[8,128,512]{2,1,0:T(8,128)(2,1)}, u32[]{:S(2)}) copy-start(bf16[8,128,512]{2,1,0:T(8,128)(2,1)} %param.16) | copy-start | bytes 3145732
  3.4 27.6 %collective-permute-start = (bf16[2048,256]{1,0:T(8,128)(2,1)}, bf16[2048,256]{1,0:T(8,128)(2,1)}, u32[]{:S(2)}, u32[]{:S(2)}) collective-permute-start(bf16[2048,256]{1,0:T(8,128)(2,1)} %pad_maximum_fusion.4.rest_2_), channel_id=1, source_target_pairs={{0,4},{4,8},{8,12},{1,5},{5,9},{9,13},{2,6},{6,10},{10,14},{3,7},{... | collective-permute-start | bytes 3145736 | tf_op jit(solution)/shard_map/ppermute | solution.py:172
  9.3 2.1 copy-start.12
  10.4 2.1 copy-start.13
  11.4 2.1 copy-start.14
  31.0 26.2 %collective-permute-start.1 = (bf16[2048,256]{1,0:T(8,128)(2,1)}, bf16[2048,256]{1,0:T(8,128)(2,1)}, u32[]{:S(2)}, u32[]{:S(2)}) collective-permute-start(bf16[2048,256]{1,0:T(8,128)(2,1)} %collective-permute-done.rest_1_), channel_id=1, source_target_pairs={{0,4},{4,8},{8,12},{1,5},{5,9},{9,13},{2,6},{6,10},{10,14},{3,7},{... | collective-permute-start | bytes 3145736 | tf_op jit(solution)/shard_map/ppermute | solution.py:172
  40.4 110.4 %collective-permute-start.2 = (bf16[5,2,1,128,512]{4,3,1,0,2:T(8,128)(2,1)}, bf16[5,2,1,128,512]{4,3,1,0,2:T(8,128)(2,1)S(1)}, u32[]{:S(2)}, u32[]{:S(2)}) collective-permute-start(bf16[5,2,1,128,512]{4,3,1,0,2:T(8,128)(2,1)} %get-tuple-element.37), channel_id=1, source_target_pairs={{4,0},{8,4},{12,8},{5,1},{9,5},{13,9},{6,2},{10,6},{14,10},{7,3},{... | collective-permute-start | bytes 3932168 | tf_op jit(solution)/shard_map/ppermute | solution.py:172
  41.7 116.8 %collective-permute-start.3 = (bf16[5,2,1,128,512]{4,3,1,0,2:T(8,128)(2,1)}, bf16[5,2,1,128,512]{4,3,1,0,2:T(8,128)(2,1)S(1)}, u32[]{:S(2)}, u32[]{:S(2)}) collective-permute-start(bf16[5,2,1,128,512]{4,3,1,0,2:T(8,128)(2,1)} %get-tuple-element.36), channel_id=1, source_target_pairs={{8,0},{12,4},{9,1},{13,5},{10,2},{14,6},{11,3},{15,7},{24,16},{28,... | collective-permute-start | bytes 3932168 | tf_op jit(solution)/shard_map/ppermute | solution.py:172
  43.0 116.8 %collective-permute-start.4 = (bf16[5,2,1,128,512]{4,3,1,0,2:T(8,128)(2,1)}, bf16[5,2,1,128,512]{4,3,1,0,2:T(8,128)(2,1)S(1)}, u32[]{:S(2)}, u32[]{:S(2)}) collective-permute-start(bf16[5,2,1,128,512]{4,3,1,0,2:T(8,128)(2,1)} %get-tuple-element.35), channel_id=1, source_target_pairs={{12,0},{13,1},{14,2},{15,3},{28,16},{29,17},{30,18},{31,19}} | collective-permute-start | bytes 3932168 | tf_op jit(solution)/shard_map/ppermute | solution.py:172
  57.3 105.8 %collective-permute-start.6 = (bf16[2048,256]{1,0:T(8,128)(2,1)}, bf16[2048,256]{1,0:T(8,128)(2,1)}, u32[]{:S(2)}, u32[]{:S(2)}) collective-permute-start(bf16[2048,256]{1,0:T(8,128)(2,1)} %pad_maximum_fusion.5.rest_2_), channel_id=1, source_target_pairs={{0,4},{4,8},{8,12},{1,5},{5,9},{9,13},{2,6},{6,10},{10,14},{3,7},{... | collective-permute-start | bytes 3145736 | tf_op jit(solution)/shard_map/ppermute | solution.py:172
  62.7 106.3 %collective-permute-start.5 = (bf16[2048,256]{1,0:T(8,128)(2,1)}, bf16[2048,256]{1,0:T(8,128)(2,1)}, u32[]{:S(2)}, u32[]{:S(2)}) collective-permute-start(bf16[2048,256]{1,0:T(8,128)(2,1)} %pad_maximum_fusion.5.rest_2_), channel_id=1, source_target_pairs={{0,8},{4,12},{1,9},{5,13},{2,10},{6,14},{3,11},{7,15},{16,24},{20,... | collective-permute-start | bytes 3145736 | tf_op jit(solution)/shard_map/ppermute | solution.py:172
  150.8 101.2 %copy-start.8 = (bf16[5,2,1,128,512]{4,3,1,0,2:T(8,128)(2,1)}, bf16[5,2,1,128,512]{4,3,1,0,2:T(8,128)(2,1)S(1)}, u32[]{:S(2)}) copy-start(bf16[5,2,1,128,512]{4,3,1,0,2:T(8,128)(2,1)S(1)} %collective-permute-done.2) | copy-start | bytes 3932164
  150.8 103.7 %collective-permute-start.7 = (bf16[2048,256]{1,0:T(8,128)(2,1)}, bf16[2048,256]{1,0:T(8,128)(2,1)}, u32[]{:S(2)}, u32[]{:S(2)}) collective-permute-start(bf16[2048,256]{1,0:T(8,128)(2,1)} %get-tuple-element.47), channel_id=1, source_target_pairs={{4,0},{8,4},{12,8},{5,1},{9,5},{13,9},{6,2},{10,6},{14,10},{7,3},{... | collective-permute-start | bytes 3145736 | tf_op jit(solution)/shard_map/ppermute | solution.py:172
  158.4 93.6 %copy-start.6 = (bf16[5,2,1,128,512]{4,3,1,0,2:T(8,128)(2,1)}, bf16[5,2,1,128,512]{4,3,1,0,2:T(8,128)(2,1)S(1)}, u32[]{:S(2)}) copy-start(bf16[5,2,1,128,512]{4,3,1,0,2:T(8,128)(2,1)S(1)} %collective-permute-done.3) | copy-start | bytes 3932164
  158.4 97.3 %collective-permute-start.8 = (bf16[2048,256]{1,0:T(8,128)(2,1)}, bf16[2048,256]{1,0:T(8,128)(2,1)}, u32[]{:S(2)}, u32[]{:S(2)}) collective-permute-start(bf16[2048,256]{1,0:T(8,128)(2,1)} %get-tuple-element.48), channel_id=1, source_target_pairs={{8,0},{12,4},{9,1},{13,5},{10,2},{14,6},{11,3},{15,7},{24,16},{28,... | collective-permute-start | bytes 3145736 | tf_op jit(solution)/shard_map/ppermute | solution.py:172
  159.7 92.3 %copy-start.4 = (bf16[5,2,1,128,512]{4,3,1,0,2:T(8,128)(2,1)}, bf16[5,2,1,128,512]{4,3,1,0,2:T(8,128)(2,1)S(1)}, u32[]{:S(2)}) copy-start(bf16[5,2,1,128,512]{4,3,1,0,2:T(8,128)(2,1)S(1)} %collective-permute-done.4) | copy-start | bytes 3932164
  159.7 116.3 %collective-permute-start.12 = (bf16[5,2,1,128,512]{4,3,1,0,2:T(8,128)(2,1)}, bf16[5,2,1,128,512]{4,3,1,0,2:T(8,128)(2,1)}, u32[]{:S(2)}, u32[]{:S(2)}) collective-permute-start(bf16[5,2,1,128,512]{4,3,1,0,2:T(8,128)(2,1)} %get-tuple-element.37), channel_id=1, source_target_pairs={{0,12},{1,13},{2,14},{3,15},{16,28},{17,29},{18,30},{19,31}} | collective-permute-start | bytes 3932168 | tf_op jit(solution)/shard_map/ppermute | solution.py:172
  163.0 113.0 %collective-permute-start.11 = (bf16[5,2,1,128,512]{4,3,1,0,2:T(8,128)(2,1)}, bf16[5,2,1,128,512]{4,3,1,0,2:T(8,128)(2,1)}, u32[]{:S(2)}, u32[]{:S(2)}) collective-permute-start(bf16[5,2,1,128,512]{4,3,1,0,2:T(8,128)(2,1)} %get-tuple-element.36), channel_id=1, source_target_pairs={{0,8},{4,12},{1,9},{5,13},{2,10},{6,14},{3,11},{7,15},{16,24},{20,... | collective-permute-start | bytes 3932168 | tf_op jit(solution)/shard_map/ppermute | solution.py:172
  169.0 107.1 %collective-permute-start.10 = (bf16[5,2,1,128,512]{4,3,1,0,2:T(8,128)(2,1)}, bf16[5,2,1,128,512]{4,3,1,0,2:T(8,128)(2,1)}, u32[]{:S(2)}, u32[]{:S(2)}) collective-permute-start(bf16[5,2,1,128,512]{4,3,1,0,2:T(8,128)(2,1)} %get-tuple-element.35), channel_id=1, source_target_pairs={{0,4},{4,8},{8,12},{1,5},{5,9},{9,13},{2,6},{6,10},{10,14},{3,7},{... | collective-permute-start | bytes 3932168 | tf_op jit(solution)/shard_map/ppermute | solution.py:172
  252.0 3.7 copy-start.2
  254.5 32.9 %collective-permute-start.9 = (bf16[2048,256]{1,0:T(8,128)(2,1)}, bf16[2048,256]{1,0:T(8,128)(2,1)}, u32[]{:S(2)}, u32[]{:S(2)}) collective-permute-start(bf16[2048,256]{1,0:T(8,128)(2,1)} %slice.76), channel_id=1, source_target_pairs={{4,0},{8,4},{12,8},{5,1},{9,5},{13,9},{6,2},{10,6},{14,10},{7,3},{... | collective-permute-start | bytes 3145736 | tf_op jit(solution)/shard_map/ppermute | solution.py:172
  255.8 2.1 copy-start.16
  272.1 78.8 %all-to-all-start = ((bf16[4,1,512,512]{2,3,1,0:T(8,128)(2,1)}), bf16[4,1,512,512]{2,3,1,0:T(8,128)(2,1)S(1)}, u32[]{:S(2)}, u32[]{:S(2)}) async-start(bf16[4,1,512,512]{2,3,1,0:T(8,128)(2,1)} %copy.15), calls=%async_computation | async-start | bytes 4194304 | tf_op jit(solution)/shard_map/all_to_all | solution.py:304
  276.0 56.6 %copy-start.3 = (f32[2048,256]{1,0:T(8,128)S(1)}, f32[2048,256]{1,0:T(8,128)}, u32[]{:S(2)}) copy-start(f32[2048,256]{1,0:T(8,128)} %get-tuple-element.33) | copy-start | bytes 6291460
  289.2 43.4 %collective-permute-start.13 = (bf16[2048,256]{1,0:T(8,128)(2,1)S(1)}, bf16[2048,256]{1,0:T(8,128)(2,1)S(1)}, u32[]{:S(2)}, u32[]{:S(2)}) collective-permute-start(bf16[2048,256]{1,0:T(8,128)(2,1)S(1)} %add_convert_fusion.1), channel_id=1, source_target_pairs={{4,0},{8,4},{12,8},{5,1},{9,5},{13,9},{6,2},{10,6},{14,10},{7,3},{... | collective-permute-start | bytes 3145736 | tf_op jit(solution)/shard_map/ppermute | solution.py:172
  332.7 1.3 copy-start.18
  332.9 1.0 copy-start
  351.0 58.8 %all-to-all-start.2 = ((bf16[4,1,512,512]{2,3,1,0:T(8,128)(2,1)}), bf16[4,1,512,512]{2,3,1,0:T(8,128)(2,1)}, u32[]{:S(2)}, u32[]{:S(2)}) async-start(bf16[4,1,512,512]{2,3,1,0:T(8,128)(2,1)} %copy.18), calls=%async_computation.2 | async-start | bytes 4194304 | tf_op jit(solution)/shard_map/all_to_all | solution.py:304
  367.4 3.2 copy-start.15
  367.4 3.2 copy-start.17
  370.5 1.8 copy-start.9
  372.4 1.5 copy-start.7
  373.9 1.4 copy-start.5
  409.8 17.7 %all-to-all-start.1 = ((bf16[4,1,128,512]{3,2,1,0:T(8,128)(2,1)}), bf16[4,1,128,512]{3,2,1,0:T(8,128)(2,1)S(1)}, u32[]{:S(2)}, u32[]{:S(2)}) async-start(bf16[4,1,128,512]{3,2,1,0:T(8,128)(2,1)} %bitcast.38), calls=%async_computation.1 | async-start | bytes 1048576 | tf_op jit(solution)/shard_map/all_to_all | solution.py:309
  416.4 14.5 %copy-start.1 = (bf16[2048,256]{1,0:T(8,128)(2,1)S(1)}, bf16[2048,256]{1,0:T(8,128)(2,1)}, u32[]{:S(2)}) copy-start(bf16[2048,256]{1,0:T(8,128)(2,1)} %copy-done) | copy-start | bytes 3145732
  427.5 17.2 %all-to-all-start.3 = ((bf16[4,1,128,512]{3,2,1,0:T(8,128)(2,1)}), bf16[4,1,128,512]{3,2,1,0:T(8,128)(2,1)S(1)}, u32[]{:S(2)}, u32[]{:S(2)}) async-start(bf16[4,1,128,512]{3,2,1,0:T(8,128)(2,1)} %bitcast.111), calls=%async_computation.3 | async-start | bytes 1048576 | tf_op jit(solution)/shard_map/all_to_all | solution.py:309

commit v2 on v1

--- a/solution.py
+++ b/solution.py
@@ -18,9 +18,11 @@
     return lax.dot_general(a, b, dims, preferred_element_type=jnp.float32)
 
 
-def attn_body(reach, tile, group, bk, q_ref, g_ref, bias_ref, *rest):
+def attn_body(reach, tile, group, bk, skip_ref, q_ref, g_ref, *rest):
     kv_refs = rest[: reach + 1]
-    o_ref, dq_ref, far_ref, own_ref, kb, vb, kt, vt, s_buf, e_buf, dkt, dvt = rest[reach + 1:]
+    o_ref, dq_ref = rest[reach + 1: reach + 3]
+    far_refs = rest[reach + 3: 2 * reach + 3]
+    own_ref, kb, vb, kt, vt, s_buf, e_buf, dkt, dvt = rest[2 * reach + 3:]
     hd = HEAD_DIM
     t = pl.program_id(0)
     rows = kv_refs[0].shape[0]
@@ -30,12 +32,14 @@
 
     @pl.when(t == 0)
     def _():
+        first = lax.broadcasted_iota(jnp.int32, (rows, hd), 1) == 0
         for s, ref in enumerate(kv_refs):
             here = pl.ds(s * rows, rows)
             k = ref[:, :hd]
             v = ref[:, hd:]
             kb[here, :hd] = k
-            kb[here, hd:] = bias_ref[here, :]
+            hide = jnp.where(s < skip_ref[0], NEG, 0.0)
+            kb[here, hd:] = jnp.where(first, hide, 0.0).astype(jnp.bfloat16)
             vb[here, :] = v
             kt[:, here] = k.T
             vt[:hd, here] = v.T
@@ -114,14 +118,14 @@
             dk = dkt[:, here].T
             dv = dvt[:, here].T
             if s < reach:
-                far_ref[here, :hd] = dk.astype(jnp.bfloat16)
-                far_ref[here, hd:] = dv.astype(jnp.bfloat16)
+                far_refs[s][:, :hd] = dk.astype(jnp.bfloat16)
+                far_refs[s][:, hd:] = dv.astype(jnp.bfloat16)
             else:
                 own_ref[:, :hd] = dk
                 own_ref[:, hd:] = dv
 
 
-def attention(queries, out_grad, bias, shards, slot, group, tile=256, bk=1920):
+def attention(queries, out_grad, skip, shards, slot, group, tile=256, bk=1920):
     hd = HEAD_DIM
     rows = queries.shape[0]
     reach = len(shards) - 1
@@ -139,12 +143,12 @@
         out_shape=(
             jax.ShapeDtypeStruct((rows, group * hd), jnp.bfloat16),
             jax.ShapeDtypeStruct((rows, group * hd), jnp.bfloat16),
-            jax.ShapeDtypeStruct((win, 2 * hd), jnp.bfloat16),
+        ) + (jax.ShapeDtypeStruct((rows, 2 * hd), jnp.bfloat16),) * reach + (
             jax.ShapeDtypeStruct((rows, 2 * hd), jnp.float32),
         ),
         grid=(rows // tile,),
-        in_specs=[part, part, whole((total, hd))] + [whole((rows, 2 * hd))] * (reach + 1),
-        out_specs=(outp, outp, whole((win, 2 * hd)), whole((rows, 2 * hd))),
+        in_specs=[pl.BlockSpec(memory_space=pltpu.SMEM), part, part] + [whole((rows, 2 * hd))] * (reach + 1),
+        out_specs=(outp, outp) + (whole((rows, 2 * hd)),) * (reach + 1),
         scratch_shapes=[
             pltpu.VMEM((total, 2 * hd), jnp.bfloat16),
             pltpu.VMEM((total, hd), jnp.bfloat16),
@@ -160,7 +164,7 @@
         cost_estimate=pl.CostEstimate(
             flops=12 * area * hd, bytes_accessed=16 << 20, transcendentals=area),
         name="window_attention",
-    )(queries, out_grad, bias, *shards)
+    )(skip, queries, out_grad, *shards)
 
 
 moment_decay = 0.8
@@ -201,6 +205,34 @@
     return jnp.einsum(spec, a, b, preferred_element_type=jnp.float32)
 
 
+def project(columns, layer_input):
+    return bmm("tj,tk->jk", columns, layer_input).astype(jnp.bfloat16)
+
+
+def swap_sum(term, n, width):
+    index = lax.axis_index("seq")
+    if n & (n - 1):
+        parts = jnp.stack([term[:, i * width:(i + 1) * width] for i in range(n)])
+        return jnp.sum(lax.all_to_all(parts, "seq", 0, 0).astype(jnp.float32), axis=0)
+    pieces = [lax.dynamic_slice_in_dim(term, 0, width, 1)] if n == 1 else None
+    step = 1
+    while step < n:
+        mine = (index // step) % 2
+        if pieces is None:
+            starts = range(n // 2)
+            keep = [lax.dynamic_slice_in_dim(term, (2 * i + mine) * width, width, 1) for i in starts]
+            send = [lax.dynamic_slice_in_dim(term, (2 * i + 1 - mine) * width, width, 1) for i in starts]
+            keep, send = jnp.stack(keep), jnp.stack(send)
+        else:
+            pairs = pieces.reshape((pieces.shape[0] // 2, 2) + pieces.shape[1:])
+            keep = lax.dynamic_index_in_dim(pairs, mine, 1, False)
+            send = lax.dynamic_index_in_dim(pairs, 1 - mine, 1, False).astype(jnp.bfloat16)
+        got = lax.ppermute(send, "seq", [(i, i ^ step) for i in range(n)])
+        pieces = keep.astype(jnp.float32) + got.astype(jnp.float32)
+        step *= 2
+    return pieces[0].astype(jnp.float32)
+
+
 def per_device(
     queries, keys, values, out_grad, layer_input, moment, left_old, left_new, right_old, right_new
 ):
@@ -220,10 +252,7 @@
         jnp.concatenate([keys[:, k * hd:(k + 1) * hd], values[:, k * hd:(k + 1) * hd]], axis=1)
         for k in range(kv_count)
     ]
-    key_row = lax.broadcasted_iota(jnp.int32, ((reach + 1) * rows, hd), 0)
-    key_col = lax.broadcasted_iota(jnp.int32, ((reach + 1) * rows, hd), 1)
-    bias = jnp.where(
-        (key_row < (reach - seq_index) * rows) & (key_col == 0), NEG, 0.0).astype(jnp.bfloat16)
+    skip = jnp.reshape(reach - seq_index, (1,)).astype(jnp.int32)
 
     windows = []
     gate = None
@@ -258,52 +287,56 @@
             packed = after(message((seq_index + n - d) % n), windows[0][reach - 1])
             leftward.append(shifted(packed, "seq", -d))
         rightward = []
-    outs, query_grads, key_grads, value_grads, news, joined = [], [], [], [], [], []
+    outs, query_grads, key_grads, value_grads, joined = [], [], [], [], []
+    parts_sent = []
     for k in range(kv_count):
-        mask = after(bias, *leftward) if whole_blocks and k == 1 else bias
-        head_out, head_dq, far, own = attention(
-            queries, out_grad, mask, windows[k], k, group)
+        last = k == kv_count - 1
+        gate = after(skip, *leftward) if whole_blocks and k == 1 else skip
+        head_out, head_dq, *grads = attention(queries, out_grad, gate, windows[k], k, group)
+        far, own = grads[:reach], grads[reach]
+        outs.append(head_out)
+        query_grads.append(head_dq)
         if whole_blocks and k == 0:
             for d in range(1, n):
                 packed = after(message((seq_index + d) % n), head_out)
                 rightward.append(shifted(packed, "seq", d))
-        outs.append(head_out)
-        query_grads.append(head_dq)
-        own = own.astype(jnp.float32)
-        if k < kv_count - 1:
+        if not last:
             for d in range(1, reach + 1):
-                back = shifted(far[(reach - d) * rows:(reach - d + 1) * rows], "seq", -d)
-                own = own + back.astype(jnp.float32)
+                own = own + shifted(far[reach - d], "seq", -d).astype(jnp.float32)
         else:
-            carry = far[:rows]
+            if whole_blocks:
+                early = jnp.concatenate(joined + [head_dq], axis=1)
+                early_term = swap_sum(project(early, layer_input), n, per_owner * order)
+            carry = far[0]
             for d in range(reach, 0, -1):
                 carry = shifted(carry, "seq", -1)
                 if whole_blocks and d == reach:
                     carry = after(carry, *rightward)
-                carry = carry.astype(jnp.float32)
                 if d > 1:
-                    carry = (carry + far[(reach - d + 1) * rows:(reach - d + 2) * rows].astype(jnp.float32)).astype(jnp.bfloat16)
-            own = own + carry
+                    carry = (carry.astype(jnp.float32) + far[reach - d + 1].astype(jnp.float32)).astype(jnp.bfloat16)
+            if whole_blocks:
+                for d in range(1, n):
+                    source = (seq_index + d) % n
+                    piece = jnp.where(seq_index + d < n, leftward[d - 1], rightward[n - d - 1])
+                    whole = lax.dynamic_update_slice_in_dim(whole, piece[:, :, :, None], source, 3)
+                m_own, lo_own, ln_own, ro_own, rn_own = whole.reshape(
+                    5, kv_count, per_owner, order, order)
+                right_turn = bmm("cbrk,cbrj->cbkj", ro_own, rn_own).astype(jnp.bfloat16)
+                turned = bmm("cbrk,cbkj->cbrj", m_own, right_turn).astype(jnp.bfloat16)
+                carried = moment_decay * bmm("cbrk,cbkj->cbrj", lo_own, turned)
+                carry = after(carry, carried)
+            own = own + carry.astype(jnp.float32)
         kv_grad = own.astype(jnp.bfloat16)
         key_grads.append(kv_grad[:, :hd])
         value_grads.append(kv_grad[:, hd:])
-        columns = jnp.concatenate([head_dq, kv_grad], axis=1)
-        joined.append(columns)
-        if whole_blocks and k == 0:
-            for d in range(1, n):
-                source = (seq_index + d) % n
-                piece = jnp.where(seq_index + d < n, leftward[d - 1], rightward[n - d - 1])
-                whole = lax.dynamic_update_slice_in_dim(whole, piece[:, :, :, None], source, 3)
-            m_own, lo_own, ln_own, ro_own, rn_own = whole.reshape(
-                5, kv_count, per_owner, order, order)
-            right_turn = bmm("cbrk,cbrj->cbkj", ro_own, rn_own).astype(jnp.bfloat16)
-            turned = bmm("cbrk,cbkj->cbrj", m_own, right_turn).astype(jnp.bfloat16)
-            carried = moment_decay * bmm("cbrk,cbkj->cbrj", lo_own, turned)
-        if whole_blocks:
-            term = bmm("tk,tj->kj", layer_input, columns).astype(jnp.bfloat16)
-            terms = lax.all_to_all(term.reshape(n, per_owner, order, order), "seq", 0, 0)
-            grad = jnp.sum(terms.astype(jnp.float32), axis=0).astype(jnp.bfloat16)
-            inner = carried[k] + (1.0 - moment_decay) * bmm("brk,bkj->brj", grad, rn_own[k])
+        joined.append(jnp.concatenate([head_dq, kv_grad], axis=1))
+    if whole_blocks:
+        late_term = swap_sum(project(kv_grad, layer_input), n, per_owner * order)
+        grads = jnp.concatenate([early_term, late_term], axis=0).astype(jnp.bfloat16)
+        news = []
+        for k in range(kv_count):
+            grad = grads[k * order:(k + 1) * order].reshape(order, per_owner, order)
+            inner = carried[k] + (1.0 - moment_decay) * bmm("jbr,bjk->brk", grad, rn_own[k])
             new = bmm("brk,brj->bkj", ln_own[k], inner.astype(jnp.bfloat16)).astype(jnp.bfloat16)
             new = jnp.transpose(new.reshape(per_owner, n, share_rows, order), (1, 0, 2, 3))
             new = lax.all_to_all(new, "seq", 0, 0)

time: 447 us -> 402 us (0.90)
  local copies, waits for them, and re-layouts: 39 us -> 19.4 us
  starting transfers between devices: 65 us -> 51.9 us
  waiting for transfers between devices: 122 us -> 116 us
    ppermute x0 -> x4, waiting for transfers between devices: none -> 45.3 us  [swap_sum(): got = lax.ppermute(send, 'seq', [(i, i ^ step) for i in range(n)])]
    ppermute x14, waiting for transfers between devices: 88 us -> 62.4 us  [shifted(): return lax.ppermute(x, axis, pairs)]
    all_to_all x2 -> x0, waiting for transfers between devices: 15.2 us -> none  [per_device(): lax.all_to_all(term.reshape(n, per_owner, order, order), 'seq', 0, 0)]
    all_to_all x2 -> x0, starting transfers between devices: 15 us -> none  [per_device(): lax.all_to_all(term.reshape(n, per_owner, order, order), 'seq', 0, 0)]
    reshape x4 -> x0, local copies, waits for them, and re-layouts: 12.8 us -> none  [per_device(): term.reshape(n, per_owner, order, order)]
    all_to_all x2, waiting for transfers between devices: 19.2 us -> 8.01 us  [per_device(): new = lax.all_to_all(new, 'seq', 0, 0)]
    slice x2 -> x0, local copies, waits for them, and re-layouts: 5.48 us -> none  [the longest x1 3.07 us: per_device(): back = shifted(far[(reach - d) * rows:(reach - d + 1) * rows], 'seq', -d)]
  transfers between devices with their start and end apart: 18 -> 20, of which waited for: 8 -> 8; matrix products, arithmetic and copies ran while one was open for 20% -> 17% of each run, Pallas kernels for 36% -> 40%
where the time goes in v2:
time: 402 us
  Pallas kernels  160 us (40%)
  waiting for transfers between devices  116 us (29%)
  starting transfers between devices  51.9 us (13%)
  matrix products  27.5 us (7%)
  other arithmetic  26 us (6%)
  local copies, waits for them, and re-layouts  19.4 us (5%)
    pallas_call x2, Pallas kernels, attention(): pl.pallas_call(functools.partial(attn_body, reach, tile, group, bk), out_...  160 us
    ppermute x14, waiting for transfers between devices, shifted(): return lax.ppermute(x, axis, pairs)  62.4 us
    ppermute x4, waiting for transfers between devices, swap_sum(): got = lax.ppermute(send, 'seq', [(i, i ^ step) for i in range(n)])  45.3 us
    ppermute x14, starting transfers between devices, shifted(): return lax.ppermute(x, axis, pairs)  42.2 us
    dot_general x6, matrix products, bmm(): return jnp.einsum(spec, a, b, preferred_element_type=jnp.float32)  27.5 us
  transfers between devices with their start and end apart: 20, of which 8 were waited for; matrix products, arithmetic and copies ran while one was open for 17% of the time, Pallas kernels for 40%

profile of v2, /device:TPU:0, one launch (start us, length us, event | category | flops | bytes accessed | tf_op | source)
XLA Modules:
  0.0 401.5 jit_solution(9399304656901788349)
XLA Ops:
  0.6 1.7 fusion.23
  3.4 5.9 %collective-permute-start = (bf16[2048,256]{1,0:T(8,128)(2,1)}, bf16[2048,256]{1,0:T(8,128)(2,1)}, u32[]{:S(2)}, u32[]{:S(2)}) collective-permute-start(bf16[2048,256]{1,0:T(8,128)(2,1)} %pad_maximum_fusion.3.rest_2_), channel_id=1, source_target_pairs={{0,4},{4,8},{8,12},{1,5},{5,9},{9,13},{2,6},{6,10},{10,14},{3,7},{... | collective-permute-start | bytes 3145736 | tf_op jit(solution)/shard_map/ppermute | solution.py:176
  10.2 20.8 %collective-permute-done.rest_1_ = bf16[2048,256]{1,0:T(8,128)(2,1)} collective-permute-done((bf16[2048,256]{1,0:T(8,128)(2,1)}, bf16[2048,256]{1,0:T(8,128)(2,1)}, u32[]{:S(2)}, u32[]{:S(2)}) %collective-permute-start) | collective-permute-done | bytes 1048608 | tf_op jit(solution)/shard_map/ppermute | solution.py:176
  31.0 5.4 %collective-permute-start.1 = (bf16[2048,256]{1,0:T(8,128)(2,1)}, bf16[2048,256]{1,0:T(8,128)(2,1)}, u32[]{:S(2)}, u32[]{:S(2)}) collective-permute-start(bf16[2048,256]{1,0:T(8,128)(2,1)} %collective-permute-done.rest_1_), channel_id=1, source_target_pairs={{0,4},{4,8},{8,12},{1,5},{5,9},{9,13},{2,6},{6,10},{10,14},{3,7},{... | collective-permute-start | bytes 3145736 | tf_op jit(solution)/shard_map/ppermute | solution.py:176
  41.2 3.0 broadcast_in_dim.15
  45.4 1.3 collective-permute-start.2
  46.7 1.3 collective-permute-start.3
  48.0 1.3 collective-permute-start.4
  49.3 8.0 %collective-permute-done.1.rest_0_ = bf16[2048,256]{1,0:T(8,128)(2,1)} collective-permute-done((bf16[2048,256]{1,0:T(8,128)(2,1)}, bf16[2048,256]{1,0:T(8,128)(2,1)}, u32[]{:S(2)}, u32[]{:S(2)}) %collective-permute-start.1) | collective-permute-done | bytes 1048608 | tf_op jit(solution)/shard_map/ppermute | solution.py:176
  57.3 5.4 %collective-permute-start.6 = (bf16[2048,256]{1,0:T(8,128)(2,1)}, bf16[2048,256]{1,0:T(8,128)(2,1)}, u32[]{:S(2)}, u32[]{:S(2)}) collective-permute-start(bf16[2048,256]{1,0:T(8,128)(2,1)} %pad_maximum_fusion.4.rest_2_), channel_id=1, source_target_pairs={{0,4},{4,8},{8,12},{1,5},{5,9},{9,13},{2,6},{6,10},{10,14},{3,7},{... | collective-permute-start | bytes 3145736 | tf_op jit(solution)/shard_map/ppermute | solution.py:176
  62.7 4.5 %collective-permute-start.5 = (bf16[2048,256]{1,0:T(8,128)(2,1)}, bf16[2048,256]{1,0:T(8,128)(2,1)}, u32[]{:S(2)}, u32[]{:S(2)}) collective-permute-start(bf16[2048,256]{1,0:T(8,128)(2,1)} %pad_maximum_fusion.4.rest_2_), channel_id=1, source_target_pairs={{0,8},{4,12},{1,9},{5,13},{2,10},{6,14},{3,11},{7,15},{16,24},{20,... | collective-permute-start | bytes 3145736 | tf_op jit(solution)/shard_map/ppermute | solution.py:176
  67.2 80.0 %window_attention.2 = (bf16[2048,256]{1,0:T(8,128)(2,1)}, bf16[2048,256]{1,0:T(8,128)(2,1)}, bf16[2048,256]{1,0:T(8,128)(2,1)}, bf16[2048,256]{1,0:T(8,128)(2,1)}, f32[2048,256]{1,0:T(8,128)}) custom-call(s32[1]{0:T(128)} %bitcast.skip_ref, bf16[2048,512]{1,0:T(8,128)(2,1)} %q_ref.3, bf16[2048,512]{1,0:T(8,128)(2,1)} %g_ref.3, ...), custom_call_target="tpu_custom_call" | custom-call | flops 25769803776 | bytes 16777216 | tf_op jit(solution)/shard_map/window_attention/pallas_call | solution.py:141
  147.2 1.3 collective-permute-start.7
  148.5 15.0 %collective-permute-done.3 = bf16[5,2,1,128,512]{4,3,1,0,2:T(8,128)(2,1)S(1)} collective-permute-done((bf16[5,2,1,128,512]{4,3,1,0,2:T(8,128)(2,1)}, bf16[5,2,1,128,512]{4,3,1,0,2:T(8,128)(2,1)S(1)}, u32[]{:S(2)}, u32[]{:S(2)}) %collective-permute-start.3) | collective-permute-done | bytes 1310752 | tf_op jit(solution)/shard_map/ppermute | solution.py:176
  164.6 1.4 collective-permute-start.8
  166.1 2.4 collective-permute-start.12
  168.5 6.9 %collective-permute-start.11 = (bf16[5,2,1,128,512]{4,3,1,0,2:T(8,128)(2,1)}, bf16[5,2,1,128,512]{4,3,1,0,2:T(8,128)(2,1)}, u32[]{:S(2)}, u32[]{:S(2)}) collective-permute-start(bf16[5,2,1,128,512]{4,3,1,0,2:T(8,128)(2,1)} %get-tuple-element.39), channel_id=1, source_target_pairs={{0,8},{4,12},{1,9},{5,13},{2,10},{6,14},{3,11},{7,15},{16,24},{20,... | collective-permute-start | bytes 3932168 | tf_op jit(solution)/shard_map/ppermute | solution.py:176
  175.3 2.4 collective-permute-start.10
  177.7 80.0 %window_attention.3 = (bf16[2048,256]{1,0:T(8,128)(2,1)}, bf16[2048,256]{1,0:T(8,128)(2,1)}, bf16[2048,256]{1,0:T(8,128)(2,1)}, bf16[2048,256]{1,0:T(8,128)(2,1)}, f32[2048,256]{1,0:T(8,128)}) custom-call(s32[1]{0:T(128)} %bitcast.skip_ref, bf16[2048,512]{1,0:T(8,128)(2,1)} %q_ref.3, bf16[2048,512]{1,0:T(8,128)(2,1)} %g_ref.3, ...), custom_call_target="tpu_custom_call" | custom-call | flops 25769803776 | bytes 16777216 | tf_op jit(solution)/shard_map/window_attention/pallas_call | solution.py:141
  257.8 1.5 collective-permute-start.9
  259.3 2.0 add_convert_fusion.2
  261.5 9.3 %convolution_convert_fusion = bf16[768,2048]{1,0:T(8,128)(2,1)S(1)} fusion(bf16[2048,2048]{1,0:T(8,128)(2,1)} %param.14, bf16[2048,256]{1,0:T(8,128)(2,1)S(1)} %copy-done.15, bf16[2048,256]{1,0:T(8,128)(2,1)S(1)} %add_convert_fusion.2, bf16[2048,256]{1,0:T(8,128)(2,1)S(1)} %copy-done.14), kind=kOutput, calls=%fused_computation | convolution fusion | flops 6453460992 | bytes 14680064 | tf_op jit(solution)/shard_map/tj,tk->jk/dot_general | solution.py:205
  271.2 1.3 pad_maximum_fusion.2
  272.5 2.6 collective-permute-start.14
  275.1 1.5 pad_maximum_fusion.1
  276.7 2.9 bitcast_dynamic-update-slice_fusion.2
  279.6 1.5 bitcast_dynamic-update-slice_fusion.1
  281.1 1.4 bitcast_dynamic-update-slice_fusion
  282.5 4.0 fusion.20
  286.5 1.7 convolution_convert_fusion.3
  288.2 1.3 add_convert_fusion.1
  289.6 1.3 collective-permute-start.13
  290.8 2.9 fusion.19
  293.7 4.4 %convolution_multiply_fusion = f32[2,512,512]{2,1,0:T(8,128)} fusion(bf16[2,512,512]{2,1,0:T(8,128)(2,1)} %bitcast.125, bf16[2,512,512]{2,1,0:T(8,128)(2,1)} %bitcast.124, bf16[2,512,512]{2,1,0:T(8,128)(2,1)} %convolution_convert_fusion.3), kind=kOutput, calls=%fused_computation.13 | convolution fusion | flops 1074790400 | bytes 5242880 | tf_op jit(solution)/shard_map/cbrk,cbkj->cbrj/dot_general | solution.py:205
  298.2 30.0 %collective-permute-done.14 = bf16[2,768,512]{2,1,0:T(8,128)(2,1)} collective-permute-done((bf16[2,768,512]{2,1,0:T(8,128)(2,1)}, bf16[2,768,512]{2,1,0:T(8,128)(2,1)}, u32[]{:S(2)}, u32[]{:S(2)}) %collective-permute-start.14) | collective-permute-done | bytes 1572896 | tf_op jit(solution)/shard_map/ppermute | solution.py:230
  328.2 2.1 convert_add_fusion
  330.5 18.5 %collective-permute-done.13 = bf16[2048,256]{1,0:T(8,128)(2,1)} collective-permute-done((bf16[2048,256]{1,0:T(8,128)(2,1)}, bf16[2048,256]{1,0:T(8,128)(2,1)}, u32[]{:S(2)}, u32[]{:S(2)}) %collective-permute-start.13) | collective-permute-done | bytes 1048608 | tf_op jit(solution)/shard_map/ppermute | solution.py:176
  349.0 1.6 add_convert_fusion
  350.5 5.7 %convolution_convert_fusion.1 = bf16[256,2048]{1,0:T(8,128)(2,1)S(1)} fusion(bf16[2048,256]{1,0:T(8,128)(2,1)S(1)} %add_convert_fusion, bf16[2048,2048]{1,0:T(8,128)(2,1)} %param.14), kind=kOutput, calls=%fused_computation.7 | convolution fusion | flops 2148007936 | bytes 10485760 | tf_op jit(solution)/shard_map/tj,tk->jk/dot_general | solution.py:205
  358.4 3.2 convolution_convert_fusion.5
  361.6 3.5 all-to-all-start
  365.1 7.6 %collective-permute-done.16 = bf16[2,256,512]{2,1,0:T(8,128)(2,1)} collective-permute-done((bf16[2,256,512]{2,1,0:T(8,128)(2,1)}, bf16[2,256,512]{2,1,0:T(8,128)(2,1)}, u32[]{:S(2)}, u32[]{:S(2)}) %collective-permute-start.16) | collective-permute-done | bytes 524320 | tf_op jit(solution)/shard_map/ppermute | solution.py:230
  374.1 1.5 pad_maximum_fusion
  375.5 7.6 %collective-permute-done.17 = bf16[1,256,512]{2,1,0:T(8,128)(2,1)S(1)} collective-permute-done((bf16[1,256,512]{2,1,0:T(8,128)(2,1)S(1)}, bf16[1,256,512]{2,1,0:T(8,128)(2,1)S(1)}, u32[]{:S(2)}, u32[]{:S(2)}) %collective-permute-start.17) | collective-permute-done | bytes 262176 | tf_op jit(solution)/shard_map/ppermute | solution.py:230
  383.3 3.1 convolution_convert_fusion.4
  386.4 3.5 all-to-all-start.1
  392.1 8.0 %all-to-all-done.1 = bf16[4,1,128,512]{3,2,1,0:T(8,128)(2,1)S(1)} async-done(((bf16[4,1,128,512]{3,2,1,0:T(8,128)(2,1)}), bf16[4,1,128,512]{3,2,1,0:T(8,128)(2,1)S(1)}, u32[]{:S(2)}, u32[]{:S(2)}) %all-to-all-start.1) | async-done | bytes 524320 | tf_op jit(solution)/shard_map/all_to_all | solution.py:342
  400.1 1.5 maximum_convert_fusion
  (71 shorter events, 15.6 us)
Async XLA Ops:
  2.3 7.0 %copy-start.7 = (bf16[8,128,512]{2,1,0:T(8,128)(2,1)S(1)}, bf16[8,128,512]{2,1,0:T(8,128)(2,1)}, u32[]{:S(2)}) copy-start(bf16[8,128,512]{2,1,0:T(8,128)(2,1)} %param.15) | copy-start | bytes 3145732
  2.3 34.1 %copy-start.8 = (bf16[8,128,512]{2,1,0:T(8,128)(2,1)S(1)}, bf16[8,128,512]{2,1,0:T(8,128)(2,1)}, u32[]{:S(2)}) copy-start(bf16[8,128,512]{2,1,0:T(8,128)(2,1)} %param.16) | copy-start | bytes 3145732
  3.4 27.6 %collective-permute-start = (bf16[2048,256]{1,0:T(8,128)(2,1)}, bf16[2048,256]{1,0:T(8,128)(2,1)}, u32[]{:S(2)}, u32[]{:S(2)}) collective-permute-start(bf16[2048,256]{1,0:T(8,128)(2,1)} %pad_maximum_fusion.3.rest_2_), channel_id=1, source_target_pairs={{0,4},{4,8},{8,12},{1,5},{5,9},{9,13},{2,6},{6,10},{10,14},{3,7},{... | collective-permute-start | bytes 3145736 | tf_op jit(solution)/shard_map/ppermute | solution.py:176
  9.3 28.1 %copy-start.9 = (bf16[8,128,512]{2,1,0:T(8,128)(2,1)S(1)}, bf16[8,128,512]{2,1,0:T(8,128)(2,1)}, u32[]{:S(2)}) copy-start(bf16[8,128,512]{2,1,0:T(8,128)(2,1)} %param.17) | copy-start | bytes 3145732
  31.0 26.2 %collective-permute-start.1 = (bf16[2048,256]{1,0:T(8,128)(2,1)}, bf16[2048,256]{1,0:T(8,128)(2,1)}, u32[]{:S(2)}, u32[]{:S(2)}) collective-permute-start(bf16[2048,256]{1,0:T(8,128)(2,1)} %collective-permute-done.rest_1_), channel_id=1, source_target_pairs={{0,4},{4,8},{8,12},{1,5},{5,9},{9,13},{2,6},{6,10},{10,14},{3,7},{... | collective-permute-start | bytes 3145736 | tf_op jit(solution)/shard_map/ppermute | solution.py:176
  36.4 1.9 copy-start.10
  37.4 1.8 copy-start.11
  45.4 101.8 %collective-permute-start.2 = (bf16[5,2,1,128,512]{4,3,1,0,2:T(8,128)(2,1)}, bf16[5,2,1,128,512]{4,3,1,0,2:T(8,128)(2,1)}, u32[]{:S(2)}, u32[]{:S(2)}) collective-permute-start(bf16[5,2,1,128,512]{4,3,1,0,2:T(8,128)(2,1)} %get-tuple-element.40), channel_id=1, source_target_pairs={{4,0},{8,4},{12,8},{5,1},{9,5},{13,9},{6,2},{10,6},{14,10},{7,3},{... | collective-permute-start | bytes 3932168 | tf_op jit(solution)/shard_map/ppermute | solution.py:176
  46.7 116.9 %collective-permute-start.3 = (bf16[5,2,1,128,512]{4,3,1,0,2:T(8,128)(2,1)}, bf16[5,2,1,128,512]{4,3,1,0,2:T(8,128)(2,1)S(1)}, u32[]{:S(2)}, u32[]{:S(2)}) collective-permute-start(bf16[5,2,1,128,512]{4,3,1,0,2:T(8,128)(2,1)} %get-tuple-element.39), channel_id=1, source_target_pairs={{8,0},{12,4},{9,1},{13,5},{10,2},{14,6},{11,3},{15,7},{24,16},{28,... | collective-permute-start | bytes 3932168 | tf_op jit(solution)/shard_map/ppermute | solution.py:176
  48.0 118.1 %collective-permute-start.4 = (bf16[5,2,1,128,512]{4,3,1,0,2:T(8,128)(2,1)}, bf16[5,2,1,128,512]{4,3,1,0,2:T(8,128)(2,1)S(1)}, u32[]{:S(2)}, u32[]{:S(2)}) collective-permute-start(bf16[5,2,1,128,512]{4,3,1,0,2:T(8,128)(2,1)} %get-tuple-element.38), channel_id=1, source_target_pairs={{12,0},{13,1},{14,2},{15,3},{28,16},{29,17},{30,18},{31,19}} | collective-permute-start | bytes 3932168 | tf_op jit(solution)/shard_map/ppermute | solution.py:176
  57.3 111.2 %collective-permute-start.6 = (bf16[2048,256]{1,0:T(8,128)(2,1)}, bf16[2048,256]{1,0:T(8,128)(2,1)}, u32[]{:S(2)}, u32[]{:S(2)}) collective-permute-start(bf16[2048,256]{1,0:T(8,128)(2,1)} %pad_maximum_fusion.4.rest_2_), channel_id=1, source_target_pairs={{0,4},{4,8},{8,12},{1,5},{5,9},{9,13},{2,6},{6,10},{10,14},{3,7},{... | collective-permute-start | bytes 3145736 | tf_op jit(solution)/shard_map/ppermute | solution.py:176
  62.7 112.6 %collective-permute-start.5 = (bf16[2048,256]{1,0:T(8,128)(2,1)}, bf16[2048,256]{1,0:T(8,128)(2,1)}, u32[]{:S(2)}, u32[]{:S(2)}) collective-permute-start(bf16[2048,256]{1,0:T(8,128)(2,1)} %pad_maximum_fusion.4.rest_2_), channel_id=1, source_target_pairs={{0,8},{4,12},{1,9},{5,13},{2,10},{6,14},{3,11},{7,15},{16,24},{20,... | collective-permute-start | bytes 3145736 | tf_op jit(solution)/shard_map/ppermute | solution.py:176
  147.2 110.5 %collective-permute-start.7 = (bf16[2048,256]{1,0:T(8,128)(2,1)}, bf16[2048,256]{1,0:T(8,128)(2,1)}, u32[]{:S(2)}, u32[]{:S(2)}) collective-permute-start(bf16[2048,256]{1,0:T(8,128)(2,1)} %get-tuple-element.34), channel_id=1, source_target_pairs={{4,0},{8,4},{12,8},{5,1},{9,5},{13,9},{6,2},{10,6},{14,10},{7,3},{... | collective-permute-start | bytes 3145736 | tf_op jit(solution)/shard_map/ppermute | solution.py:176
  163.5 1.1 copy-start.4
  164.6 94.7 %copy-start.1 = (f32[2048,256]{1,0:T(8,128)S(1)}, f32[2048,256]{1,0:T(8,128)}, u32[]{:S(2)}) copy-start(f32[2048,256]{1,0:T(8,128)} %get-tuple-element.33) | copy-start | bytes 6291460
  164.6 94.7 %collective-permute-start.8 = (bf16[2048,256]{1,0:T(8,128)(2,1)}, bf16[2048,256]{1,0:T(8,128)(2,1)}, u32[]{:S(2)}, u32[]{:S(2)}) collective-permute-start(bf16[2048,256]{1,0:T(8,128)(2,1)} %get-tuple-element.35), channel_id=1, source_target_pairs={{8,0},{12,4},{9,1},{13,5},{10,2},{14,6},{11,3},{15,7},{24,16},{28,... | collective-permute-start | bytes 3145736 | tf_op jit(solution)/shard_map/ppermute | solution.py:176
  166.1 91.7 %copy-start.2 = (bf16[5,2,1,128,512]{4,3,1,0,2:T(8,128)(2,1)}, bf16[5,2,1,128,512]{4,3,1,0,2:T(8,128)(2,1)S(1)}, u32[]{:S(2)}) copy-start(bf16[5,2,1,128,512]{4,3,1,0,2:T(8,128)(2,1)S(1)} %collective-permute-done.4) | copy-start | bytes 3932164
  166.1 110.6 %collective-permute-start.12 = (bf16[5,2,1,128,512]{4,3,1,0,2:T(8,128)(2,1)}, bf16[5,2,1,128,512]{4,3,1,0,2:T(8,128)(2,1)}, u32[]{:S(2)}, u32[]{:S(2)}) collective-permute-start(bf16[5,2,1,128,512]{4,3,1,0,2:T(8,128)(2,1)} %get-tuple-element.40), channel_id=1, source_target_pairs={{0,12},{1,13},{2,14},{3,15},{16,28},{17,29},{18,30},{19,31}} | collective-permute-start | bytes 3932168 | tf_op jit(solution)/shard_map/ppermute | solution.py:176
  168.5 111.1 %collective-permute-start.11 = (bf16[5,2,1,128,512]{4,3,1,0,2:T(8,128)(2,1)}, bf16[5,2,1,128,512]{4,3,1,0,2:T(8,128)(2,1)}, u32[]{:S(2)}, u32[]{:S(2)}) collective-permute-start(bf16[5,2,1,128,512]{4,3,1,0,2:T(8,128)(2,1)} %get-tuple-element.39), channel_id=1, source_target_pairs={{0,8},{4,12},{1,9},{5,13},{2,10},{6,14},{3,11},{7,15},{16,24},{20,... | collective-permute-start | bytes 3932168 | tf_op jit(solution)/shard_map/ppermute | solution.py:176
  175.3 105.7 %collective-permute-start.10 = (bf16[5,2,1,128,512]{4,3,1,0,2:T(8,128)(2,1)}, bf16[5,2,1,128,512]{4,3,1,0,2:T(8,128)(2,1)}, u32[]{:S(2)}, u32[]{:S(2)}) collective-permute-start(bf16[5,2,1,128,512]{4,3,1,0,2:T(8,128)(2,1)} %get-tuple-element.38), channel_id=1, source_target_pairs={{0,4},{4,8},{8,12},{1,5},{5,9},{9,13},{2,6},{6,10},{10,14},{3,7},{... | collective-permute-start | bytes 3932168 | tf_op jit(solution)/shard_map/ppermute | solution.py:176
  257.8 30.5 %collective-permute-start.9 = (bf16[2048,256]{1,0:T(8,128)(2,1)}, bf16[2048,256]{1,0:T(8,128)(2,1)S(1)}, u32[]{:S(2)}, u32[]{:S(2)}) collective-permute-start(bf16[2048,256]{1,0:T(8,128)(2,1)} %get-tuple-element.37), channel_id=1, source_target_pairs={{4,0},{8,4},{12,8},{5,1},{9,5},{13,9},{6,2},{10,6},{14,10},{7,3},{... | collective-permute-start | bytes 3145736 | tf_op jit(solution)/shard_map/ppermute | solution.py:176
  259.3 2.0 copy-start.14
  259.3 2.2 copy-start.15
  272.5 55.7 %collective-permute-start.14 = (bf16[2,768,512]{2,1,0:T(8,128)(2,1)}, bf16[2,768,512]{2,1,0:T(8,128)(2,1)}, u32[]{:S(2)}, u32[]{:S(2)}) collective-permute-start(bf16[2,768,512]{2,1,0:T(8,128)(2,1)} %pad_maximum_fusion.2), channel_id=1, source_target_pairs={{0,4},{4,0},{8,12},{12,8},{1,5},{5,1},{9,13},{13,9},{2,6},{6,2},{1... | collective-permute-start | bytes 4718600 | tf_op jit(solution)/shard_map/ppermute | solution.py:230
  276.7 2.9 copy-start.5
  279.6 1.5 copy-start.3
  286.5 1.8 copy-start.6
  289.6 59.4 %collective-permute-start.13 = (bf16[2048,256]{1,0:T(8,128)(2,1)}, bf16[2048,256]{1,0:T(8,128)(2,1)}, u32[]{:S(2)}, u32[]{:S(2)}) collective-permute-start(bf16[2048,256]{1,0:T(8,128)(2,1)} %add_convert_fusion.1), channel_id=1, source_target_pairs={{4,0},{8,4},{12,8},{5,1},{9,5},{13,9},{6,2},{10,6},{14,10},{7,3},{... | collective-permute-start | bytes 3145736 | tf_op jit(solution)/shard_map/ppermute | solution.py:176
  328.2 20.8 %copy-start = (f32[2048,256]{1,0:T(8,128)S(1)}, f32[2048,256]{1,0:T(8,128)}, u32[]{:S(2)}) copy-start(f32[2048,256]{1,0:T(8,128)} %get-tuple-element.36) | copy-start | bytes 6291460
  330.4 26.9 %collective-permute-start.15 = (bf16[1,768,512]{2,1,0:T(8,128)(2,1)S(1)}, bf16[1,768,512]{2,1,0:T(8,128)(2,1)S(1)}, u32[]{:S(2)}, u32[]{:S(2)}) collective-permute-start(bf16[1,768,512]{2,1,0:T(8,128)(2,1)S(1)} %dynamic-slice_convert_fusion), channel_id=1, source_target_pairs={{0,8},{4,12},{8,0},{12,4},{1,9},{5,13},{9,1},{13,5},{2,10},{6,14},... | collective-permute-start | bytes 2359304 | tf_op jit(solution)/shard_map/ppermute | solution.py:230
  357.2 1.2 copy-start.17
  357.2 15.5 %collective-permute-start.16 = (bf16[2,256,512]{2,1,0:T(8,128)(2,1)}, bf16[2,256,512]{2,1,0:T(8,128)(2,1)}, u32[]{:S(2)}, u32[]{:S(2)}) collective-permute-start(bf16[2,256,512]{2,1,0:T(8,128)(2,1)} %pad_maximum_fusion.10), channel_id=1, source_target_pairs={{0,4},{4,0},{8,12},{12,8},{1,5},{5,1},{9,13},{13,9},{2,6},{6,2},{1... | collective-permute-start | bytes 1572872 | tf_op jit(solution)/shard_map/ppermute | solution.py:230
  361.6 24.8 %all-to-all-start = ((bf16[4,1,128,512]{3,2,1,0:T(8,128)(2,1)}), bf16[4,1,128,512]{3,2,1,0:T(8,128)(2,1)S(1)}, u32[]{:S(2)}, u32[]{:S(2)}) async-start(bf16[4,1,128,512]{3,2,1,0:T(8,128)(2,1)} %bitcast.127), calls=%async_computation | async-start | bytes 1048576 | tf_op jit(solution)/shard_map/all_to_all | solution.py:342
  365.1 9.0 %copy-start.12 = (bf16[2048,256]{1,0:T(8,128)(2,1)S(1)}, bf16[2048,256]{1,0:T(8,128)(2,1)}, u32[]{:S(2)}) copy-start(bf16[2048,256]{1,0:T(8,128)(2,1)} %get-tuple-element.24) | copy-start | bytes 3145732
  365.1 9.0 %copy-start.13 = (bf16[2048,256]{1,0:T(8,128)(2,1)S(1)}, bf16[2048,256]{1,0:T(8,128)(2,1)}, u32[]{:S(2)}) copy-start(bf16[2048,256]{1,0:T(8,128)(2,1)} %get-tuple-element.30) | copy-start | bytes 3145732
  374.0 9.2 %collective-permute-start.17 = (bf16[1,256,512]{2,1,0:T(8,128)(2,1)S(1)}, bf16[1,256,512]{2,1,0:T(8,128)(2,1)S(1)}, u32[]{:S(2)}, u32[]{:S(2)}) collective-permute-start(bf16[1,256,512]{2,1,0:T(8,128)(2,1)S(1)} %dynamic-slice_convert_fusion.1), channel_id=1, source_target_pairs={{0,8},{4,12},{8,0},{12,4},{1,9},{5,13},{9,1},{13,5},{2,10},{6,14},... | collective-permute-start | bytes 786440 | tf_op jit(solution)/shard_map/ppermute | solution.py:230
  374.1 9.2 %copy-start.16 = (bf16[1,1,1,4,128,512]{5,4,3,1,2,0:T(8,128)(2,1)S(1)}, bf16[1,1,1,4,128,512]{5,4,3,1,2,0:T(8,128)(2,1)}, u32[]{:S(2)}) copy-start(bf16[1,1,1,4,128,512]{5,4,3,1,2,0:T(8,128)(2,1)} %get-tuple-element.44) | copy-start | bytes 1572868
  386.4 13.7 %all-to-all-start.1 = ((bf16[4,1,128,512]{3,2,1,0:T(8,128)(2,1)}), bf16[4,1,128,512]{3,2,1,0:T(8,128)(2,1)S(1)}, u32[]{:S(2)}, u32[]{:S(2)}) async-start(bf16[4,1,128,512]{3,2,1,0:T(8,128)(2,1)} %bitcast.128), calls=%async_computation.1 | async-start | bytes 1048576 | tf_op jit(solution)/shard_map/all_to_all | solution.py:342

commit v3 on v2

--- a/solution.py
+++ b/solution.py
@@ -18,7 +18,7 @@
     return lax.dot_general(a, b, dims, preferred_element_type=jnp.float32)
 
 
-def attn_body(reach, tile, group, bk, skip_ref, q_ref, g_ref, *rest):
+def attn_body(reach, tile, group, skip_ref, q_ref, g_ref, *rest):
     kv_refs = rest[: reach + 1]
     o_ref, dq_ref = rest[reach + 1: reach + 3]
     far_refs = rest[reach + 3: 2 * reach + 3]
@@ -66,9 +66,7 @@
         return jnp.max(s.reshape(size // 8, 8, cols), axis=0)
 
     m8 = jnp.maximum(scores(0, tile, ki > qi), scores(win, tile, ki <= qi))
-    m8 = lax.fori_loop(
-        0, n_full // bk,
-        lambda i, m: jnp.maximum(m, scores(pl.multiple_of(tile + i * bk, tile), bk)), m8)
+    m8 = jnp.maximum(m8, scores(tile, n_full))
     m = jnp.max(m8, axis=0, keepdims=True)
     mc = m * (scale * LOG2E)
 
@@ -78,10 +76,7 @@
         e_buf[pl.ds(off, size), :] = e
         return mm(vt[:, at], e, NN)
 
-    ot = weigh(0, tile) + weigh(win, tile)
-    ot = lax.fori_loop(
-        0, n_full // bk,
-        lambda i, a: a + weigh(pl.multiple_of(tile + i * bk, tile), bk), ot)
+    ot = weigh(0, win + tile)
     rl = 1.0 / ot[hd:hd + 1, :]
     on = (ot[:hd, :] * rl).astype(jnp.bfloat16)
     on32 = on.astype(jnp.float32)
@@ -90,23 +85,20 @@
     dd = jnp.sum(gt * on32, axis=0, keepdims=True)
     for h in range(group):
         o_ref[:, h * hd:(h + 1) * hd] = on32[:, h * tile:(h + 1) * tile].T.astype(jnp.bfloat16)
-    glt = (gt * rl).astype(jnp.bfloat16)
+    gl = (gt * rl).T.astype(jnp.bfloat16)
     rs = rl * scale
-    qrt = (qt * rs).astype(jnp.bfloat16)
+    qr = (qt * rs).T.astype(jnp.bfloat16)
 
     def back(off, size):
         at = pl.ds(pl.multiple_of(base + off, tile), size)
         e = e_buf[pl.ds(off, size), :]
         dp = mm(vb[at, :], g, NT) - dd
         ds = (e.astype(jnp.float32) * dp).astype(jnp.bfloat16)
-        dvt[:, at] += mm(glt, e, NT)
-        dkt[:, at] += mm(qrt, ds, NT)
+        dvt[at, :] += mm(e, gl, NN)
+        dkt[at, :] += mm(ds, qr, NN)
         return mm(kt[:, at], ds, NN)
 
-    dqt = back(0, tile) + back(win, tile)
-    dqt = lax.fori_loop(
-        0, n_full // bk,
-        lambda i, a: a + back(pl.multiple_of(tile + i * bk, tile), bk), dqt)
+    dqt = back(0, win + tile)
     dqt = dqt * rs
     for h in range(group):
         dq_ref[:, h * hd:(h + 1) * hd] = dqt[:, h * tile:(h + 1) * tile].T.astype(jnp.bfloat16)
@@ -115,8 +107,8 @@
     def _():
         for s in range(reach + 1):
             here = pl.ds(s * rows, rows)
-            dk = dkt[:, here].T
-            dv = dvt[:, here].T
+            dk = dkt[here, :]
+            dv = dvt[here, :]
             if s < reach:
                 far_refs[s][:, :hd] = dk.astype(jnp.bfloat16)
                 far_refs[s][:, hd:] = dv.astype(jnp.bfloat16)
@@ -125,21 +117,19 @@
                 own_ref[:, hd:] = dv
 
 
-def attention(queries, out_grad, skip, shards, slot, group, tile=256, bk=1920):
+def attention(queries, out_grad, skip, shards, slot, group, tile=256):
     hd = HEAD_DIM
     rows = queries.shape[0]
     reach = len(shards) - 1
     win = reach * rows
     total = win + rows
     cols = group * tile
-    while (win - tile) % bk:
-        bk -= tile
     whole = lambda shape: pl.BlockSpec(shape, lambda t: (0, 0), pipeline_mode=pl.Buffered(1))
     part = pl.BlockSpec((tile, group * hd), lambda t: (t, slot))
     outp = pl.BlockSpec((tile, group * hd), lambda t: (t, 0))
     area = win * rows * group
     return pl.pallas_call(
-        functools.partial(attn_body, reach, tile, group, bk),
+        functools.partial(attn_body, reach, tile, group),
         out_shape=(
             jax.ShapeDtypeStruct((rows, group * hd), jnp.bfloat16),
             jax.ShapeDtypeStruct((rows, group * hd), jnp.bfloat16),
@@ -156,8 +146,8 @@
             pltpu.VMEM((hd + 16, total), jnp.bfloat16),
             pltpu.VMEM((win + tile, cols), jnp.float32),
             pltpu.VMEM((win + tile, cols), jnp.bfloat16),
-            pltpu.VMEM((hd, total), jnp.float32),
-            pltpu.VMEM((hd, total), jnp.float32),
+            pltpu.VMEM((total, hd), jnp.float32),
+            pltpu.VMEM((total, hd), jnp.float32),
         ],
         compiler_params=pltpu.CompilerParams(
             dimension_semantics=("arbitrary",), vmem_limit_bytes=60 << 20),
@@ -170,9 +160,9 @@
 moment_decay = 0.8
 
 
-def shifted(x, axis, by):
+def shifted(x, axis, by, first=0):
     length = lax.axis_size(axis)
-    pairs = [(i, i + by) for i in range(length) if 0 <= i + by < length]
+    pairs = [(i, i + by) for i in range(first, length) if 0 <= i + by < length]
     return lax.ppermute(x, axis, pairs)
 
 
@@ -260,8 +250,8 @@
         held = pairs[k] if gate is None else after(pairs[k], gate)
         shards = [pairs[k]]
         if k == 0:
-            for _ in range(reach):
-                held = shifted(held, "seq", 1)
+            for hop in range(reach):
+                held = shifted(held, "seq", 1, hop)
                 shards.insert(0, held)
             gate = held
         else:
@@ -284,7 +274,9 @@
             whole, message(seq_index)[:, :, :, None], seq_index, 3)
         leftward = []
         for d in range(1, n):
-            packed = after(message((seq_index + n - d) % n), windows[0][reach - 1])
+            packed = message((seq_index + n - d) % n)
+            if d > 1:
+                packed = after(packed, windows[0][reach - 1])
             leftward.append(shifted(packed, "seq", -d))
         rightward = []
     outs, query_grads, key_grads, value_grads, joined = [], [], [], [], []
@@ -309,9 +301,9 @@
                 early_term = swap_sum(project(early, layer_input), n, per_owner * order)
             carry = far[0]
             for d in range(reach, 0, -1):
-                carry = shifted(carry, "seq", -1)
+                carry = shifted(carry, "seq", -1, d)
                 if whole_blocks and d == reach:
-                    carry = after(carry, *rightward)
+                    whole = after(whole, carry)
                 if d > 1:
                     carry = (carry.astype(jnp.float32) + far[reach - d + 1].astype(jnp.float32)).astype(jnp.bfloat16)
             if whole_blocks:

time: 402 us -> 408 us (1.015)
  Pallas kernels: 160 us -> 129 us
  waiting for transfers between devices: 116 us -> 142 us
  starting transfers between devices: 51.9 us -> 60.2 us
    pallas_call x2, Pallas kernels: 160 us -> 129 us  [attention(): pl.pallas_call(functools.partial(attn_body, reach, tile, group), out_shap...]
    ppermute x14, waiting for transfers between devices: 62.4 us -> 92.3 us  [shifted(): return lax.ppermute(x, axis, pairs)]
    ppermute x14, starting transfers between devices: 42.2 us -> 48.4 us  [shifted(): return lax.ppermute(x, axis, pairs)]
  transfers between devices with their start and end apart: 20 -> 20, of which waited for: 8 -> 7; matrix products, arithmetic and copies ran while one was open for 17% -> 17% of each run, Pallas kernels for 40% -> 32%
where the time goes in v3:
time: 408 us; the launch traced here: 407 us
  waiting for transfers between devices  142 us (35%)
  Pallas kernels  129 us (32%)
  starting transfers between devices  60.2 us (15%)
  matrix products  27.5 us (7%)
  other arithmetic  25.9 us (6%)
  local copies, waits for them, and re-layouts  21 us (5%)
    pallas_call x2, Pallas kernels, attention(): pl.pallas_call(functools.partial(attn_body, reach, tile, group), out_shap...  129 us
    ppermute x14, waiting for transfers between devices, shifted(): return lax.ppermute(x, axis, pairs)  92.3 us
    ppermute x14, starting transfers between devices, shifted(): return lax.ppermute(x, axis, pairs)  48.4 us
    ppermute x4, waiting for transfers between devices, swap_sum(): got = lax.ppermute(send, 'seq', [(i, i ^ step) for i in range(n)])  42.1 us
    dot_general x6, matrix products, bmm(): return jnp.einsum(spec, a, b, preferred_element_type=jnp.float32)  27.5 us
    all_to_all x2, starting transfers between devices, per_device(): new = lax.all_to_all(new, 'seq', 0, 0)  10.2 us
  transfers between devices with their start and end apart: 20, of which 7 were waited for; matrix products, arithmetic and copies ran while one was open for 17% of the time, Pallas kernels for 32%

profile of v3, /device:TPU:0, one launch (start us, length us, event | category | flops | bytes accessed | tf_op | source)
XLA Modules:
  0.0 407.3 jit_solution(15255098749015714326)
XLA Ops:
  0.6 1.7 fusion.23
  3.4 5.9 %collective-permute-start = (bf16[2048,256]{1,0:T(8,128)(2,1)}, bf16[2048,256]{1,0:T(8,128)(2,1)}, u32[]{:S(2)}, u32[]{:S(2)}) collective-permute-start(bf16[2048,256]{1,0:T(8,128)(2,1)} %pad_maximum_fusion.3.rest_2_), channel_id=1, source_target_pairs={{0,4},{4,8},{8,12},{1,5},{5,9},{9,13},{2,6},{6,10},{10,14},{3,7},{... | collective-permute-start | bytes 3145736 | tf_op jit(solution)/shard_map/ppermute | solution.py:166
  10.2 20.8 %collective-permute-done.rest_1_ = bf16[2048,256]{1,0:T(8,128)(2,1)} collective-permute-done((bf16[2048,256]{1,0:T(8,128)(2,1)}, bf16[2048,256]{1,0:T(8,128)(2,1)}, u32[]{:S(2)}, u32[]{:S(2)}) %collective-permute-start) | collective-permute-done | bytes 1048608 | tf_op jit(solution)/shard_map/ppermute | solution.py:166
  31.0 1.7 collective-permute-start.1
  32.7 2.2 bitcast_dynamic-update-slice_fusion.7
  37.6 1.3 collective-permute-start.2
  40.1 3.0 broadcast_in_dim.15
  43.0 1.3 bitcast_dynamic-update-slice_fusion.3
  44.3 1.3 collective-permute-start.3
  45.6 1.3 collective-permute-start.4
  46.9 14.9 %collective-permute-start.6 = (bf16[2048,256]{1,0:T(8,128)(2,1)}, bf16[2048,256]{1,0:T(8,128)(2,1)}, u32[]{:S(2)}, u32[]{:S(2)}) collective-permute-start(bf16[2048,256]{1,0:T(8,128)(2,1)} %pad_maximum_fusion.4.rest_2_), channel_id=1, source_target_pairs={{0,4},{4,8},{8,12},{1,5},{5,9},{9,13},{2,6},{6,10},{10,14},{3,7},{... | collective-permute-start | bytes 3145736 | tf_op jit(solution)/shard_map/ppermute | solution.py:166
  61.7 5.4 %collective-permute-start.5 = (bf16[2048,256]{1,0:T(8,128)(2,1)}, bf16[2048,256]{1,0:T(8,128)(2,1)}, u32[]{:S(2)}, u32[]{:S(2)}) collective-permute-start(bf16[2048,256]{1,0:T(8,128)(2,1)} %pad_maximum_fusion.4.rest_2_), channel_id=1, source_target_pairs={{0,8},{4,12},{1,9},{5,13},{2,10},{6,14},{3,11},{7,15},{16,24},{20,... | collective-permute-start | bytes 3145736 | tf_op jit(solution)/shard_map/ppermute | solution.py:166
  67.2 64.6 %window_attention.2 = (bf16[2048,256]{1,0:T(8,128)(2,1)}, bf16[2048,256]{1,0:T(8,128)(2,1)}, bf16[2048,256]{1,0:T(8,128)(2,1)}, bf16[2048,256]{1,0:T(8,128)(2,1)}, f32[2048,256]{1,0:T(8,128)}) custom-call(s32[1]{0:T(128)} %bitcast.skip_ref, bf16[2048,512]{1,0:T(8,128)(2,1)} %q_ref.3, bf16[2048,512]{1,0:T(8,128)(2,1)} %g_ref.3, ...), custom_call_target="tpu_custom_call" | custom-call | flops 25769803776 | bytes 16777216 | tf_op jit(solution)/shard_map/window_attention/pallas_call | solution.py:131
  131.8 1.3 collective-permute-start.7
  133.1 49.9 %collective-permute-done.3 = bf16[5,2,1,128,512]{4,3,1,0,2:T(8,128)(2,1)S(1)} collective-permute-done((bf16[5,2,1,128,512]{4,3,1,0,2:T(8,128)(2,1)}, bf16[5,2,1,128,512]{4,3,1,0,2:T(8,128)(2,1)S(1)}, u32[]{:S(2)}, u32[]{:S(2)}) %collective-permute-start.3) | collective-permute-done | bytes 1310752 | tf_op jit(solution)/shard_map/ppermute | solution.py:166
  184.0 1.4 collective-permute-start.8
  185.5 2.4 collective-permute-start.11
  187.9 6.9 %collective-permute-start.12 = (bf16[5,2,1,128,512]{4,3,1,0,2:T(8,128)(2,1)}, bf16[5,2,1,128,512]{4,3,1,0,2:T(8,128)(2,1)}, u32[]{:S(2)}, u32[]{:S(2)}) collective-permute-start(bf16[5,2,1,128,512]{4,3,1,0,2:T(8,128)(2,1)} %get-tuple-element.39), channel_id=1, source_target_pairs={{0,8},{4,12},{1,9},{5,13},{2,10},{6,14},{3,11},{7,15},{16,24},{20,... | collective-permute-start | bytes 3932168 | tf_op jit(solution)/shard_map/ppermute | solution.py:166
  194.8 2.3 collective-permute-start.13
  197.1 64.6 %window_attention.3 = (bf16[2048,256]{1,0:T(8,128)(2,1)}, bf16[2048,256]{1,0:T(8,128)(2,1)}, bf16[2048,256]{1,0:T(8,128)(2,1)}, bf16[2048,256]{1,0:T(8,128)(2,1)}, f32[2048,256]{1,0:T(8,128)}) custom-call(s32[1]{0:T(128)} %bitcast.skip_ref, bf16[2048,512]{1,0:T(8,128)(2,1)} %q_ref.3, bf16[2048,512]{1,0:T(8,128)(2,1)} %g_ref.3, ...), custom_call_target="tpu_custom_call" | custom-call | flops 25769803776 | bytes 16777216 | tf_op jit(solution)/shard_map/window_attention/pallas_call | solution.py:131
  262.7 2.0 add_convert_fusion.2
  264.9 9.3 %convolution_convert_fusion = bf16[768,2048]{1,0:T(8,128)(2,1)S(1)} fusion(bf16[2048,2048]{1,0:T(8,128)(2,1)} %param.14, bf16[2048,256]{1,0:T(8,128)(2,1)S(1)} %copy-done.14, bf16[2048,256]{1,0:T(8,128)(2,1)S(1)} %add_convert_fusion.2, bf16[2048,256]{1,0:T(8,128)(2,1)S(1)} %copy-done.13), kind=kOutput, calls=%fused_computation | convolution fusion | flops 6453460992 | bytes 14680064 | tf_op jit(solution)/shard_map/tj,tk->jk/dot_general | solution.py:195
  274.7 1.5 pad_maximum_fusion.1
  276.2 1.3 pad_maximum_fusion.2
  277.8 1.3 add_convert_fusion.1
  279.1 1.4 collective-permute-start.10
  280.6 2.8 bitcast_dynamic-update-slice_fusion.2
  283.3 1.5 bitcast_dynamic-update-slice_fusion.1
  284.8 1.5 bitcast_dynamic-update-slice_fusion
  286.3 4.0 fusion.20
  290.3 1.8 convolution_convert_fusion.3
  292.0 2.9 fusion.19
  294.9 4.4 %convolution_multiply_fusion = f32[2,512,512]{2,1,0:T(8,128)} fusion(bf16[2,512,512]{2,1,0:T(8,128)(2,1)} %bitcast.125, bf16[2,512,512]{2,1,0:T(8,128)(2,1)} %bitcast.124, bf16[2,512,512]{2,1,0:T(8,128)(2,1)} %convolution_convert_fusion.3), kind=kOutput, calls=%fused_computation.13 | convolution fusion | flops 1074790400 | bytes 5242880 | tf_op jit(solution)/shard_map/cbrk,cbkj->cbrj/dot_general | solution.py:195
  299.4 24.2 %collective-permute-done.14 = bf16[2,768,512]{2,1,0:T(8,128)(2,1)} collective-permute-done((bf16[2,768,512]{2,1,0:T(8,128)(2,1)}, bf16[2,768,512]{2,1,0:T(8,128)(2,1)}, u32[]{:S(2)}, u32[]{:S(2)}) %collective-permute-start.14) | collective-permute-done | bytes 1572896 | tf_op jit(solution)/shard_map/ppermute | solution.py:220
  323.5 2.1 convert_add_fusion
  325.8 21.6 %collective-permute-done.10 = bf16[2048,256]{1,0:T(8,128)(2,1)} collective-permute-done((bf16[2048,256]{1,0:T(8,128)(2,1)}, bf16[2048,256]{1,0:T(8,128)(2,1)}, u32[]{:S(2)}, u32[]{:S(2)}) %collective-permute-start.10) | collective-permute-done | bytes 1048608 | tf_op jit(solution)/shard_map/ppermute | solution.py:166
  347.4 1.6 add_convert_fusion
  348.9 5.7 %convolution_convert_fusion.1 = bf16[256,2048]{1,0:T(8,128)(2,1)S(1)} fusion(bf16[2048,256]{1,0:T(8,128)(2,1)S(1)} %add_convert_fusion, bf16[2048,2048]{1,0:T(8,128)(2,1)} %param.14), kind=kOutput, calls=%fused_computation.7 | convolution fusion | flops 2148007936 | bytes 10485760 | tf_op jit(solution)/shard_map/tj,tk->jk/dot_general | solution.py:195
  356.8 3.2 convolution_convert_fusion.5
  360.0 6.8 %all-to-all-start = ((bf16[4,1,128,512]{3,2,1,0:T(8,128)(2,1)}), bf16[4,1,128,512]{3,2,1,0:T(8,128)(2,1)S(1)}, u32[]{:S(2)}, u32[]{:S(2)}) async-start(bf16[4,1,128,512]{3,2,1,0:T(8,128)(2,1)} %bitcast.127), calls=%async_computation | async-start | bytes 1048576 | tf_op jit(solution)/shard_map/all_to_all | solution.py:334
  366.8 4.3 %collective-permute-done.16 = bf16[2,256,512]{2,1,0:T(8,128)(2,1)} collective-permute-done((bf16[2,256,512]{2,1,0:T(8,128)(2,1)}, bf16[2,256,512]{2,1,0:T(8,128)(2,1)}, u32[]{:S(2)}, u32[]{:S(2)}) %collective-permute-start.16) | collective-permute-done | bytes 524320 | tf_op jit(solution)/shard_map/ppermute | solution.py:220
  372.3 1.5 collective-permute-start.17
  373.8 1.5 pad_maximum_fusion
  375.2 13.7 %collective-permute-done.17 = bf16[1,256,512]{2,1,0:T(8,128)(2,1)S(1)} collective-permute-done((bf16[1,256,512]{2,1,0:T(8,128)(2,1)S(1)}, bf16[1,256,512]{2,1,0:T(8,128)(2,1)S(1)}, u32[]{:S(2)}, u32[]{:S(2)}) %collective-permute-start.17) | collective-permute-done | bytes 262176 | tf_op jit(solution)/shard_map/ppermute | solution.py:220
  389.0 3.1 convolution_convert_fusion.4
  392.1 3.5 all-to-all-start.1
  397.8 8.0 %all-to-all-done.1 = bf16[4,1,128,512]{3,2,1,0:T(8,128)(2,1)S(1)} async-done(((bf16[4,1,128,512]{3,2,1,0:T(8,128)(2,1)}), bf16[4,1,128,512]{3,2,1,0:T(8,128)(2,1)S(1)}, u32[]{:S(2)}, u32[]{:S(2)}) %all-to-all-start.1) | async-done | bytes 524320 | tf_op jit(solution)/shard_map/all_to_all | solution.py:334
  405.8 1.5 maximum_convert_fusion
  (69 shorter events, 14.7 us)
Async XLA Ops:
  2.3 7.0 %copy-start.7 = (bf16[8,128,512]{2,1,0:T(8,128)(2,1)S(1)}, bf16[8,128,512]{2,1,0:T(8,128)(2,1)}, u32[]{:S(2)}) copy-start(bf16[8,128,512]{2,1,0:T(8,128)(2,1)} %param.15) | copy-start | bytes 3145732
  3.4 27.6 %collective-permute-start = (bf16[2048,256]{1,0:T(8,128)(2,1)}, bf16[2048,256]{1,0:T(8,128)(2,1)}, u32[]{:S(2)}, u32[]{:S(2)}) collective-permute-start(bf16[2048,256]{1,0:T(8,128)(2,1)} %pad_maximum_fusion.3.rest_2_), channel_id=1, source_target_pairs={{0,4},{4,8},{8,12},{1,5},{5,9},{9,13},{2,6},{6,10},{10,14},{3,7},{... | collective-permute-start | bytes 3145736 | tf_op jit(solution)/shard_map/ppermute | solution.py:166
  9.3 25.6 %copy-start.8 = (bf16[8,128,512]{2,1,0:T(8,128)(2,1)S(1)}, bf16[8,128,512]{2,1,0:T(8,128)(2,1)}, u32[]{:S(2)}) copy-start(bf16[8,128,512]{2,1,0:T(8,128)(2,1)} %param.17) | copy-start | bytes 3145732
  31.0 15.8 %collective-permute-start.1 = (bf16[2048,256]{1,0:T(8,128)(2,1)}, bf16[2048,256]{1,0:T(8,128)(2,1)}, u32[]{:S(2)}, u32[]{:S(2)}) collective-permute-start(bf16[2048,256]{1,0:T(8,128)(2,1)} %collective-permute-done.rest_1_), channel_id=1, source_target_pairs={{4,8},{8,12},{5,9},{9,13},{6,10},{10,14},{7,11},{11,15},{20,24},{2... | collective-permute-start | bytes 3145736 | tf_op jit(solution)/shard_map/ppermute | solution.py:166
  32.7 3.1 copy-start.9
  34.9 1.8 copy-start.10
  37.6 94.1 %collective-permute-start.2 = (bf16[5,2,1,128,512]{4,3,1,0,2:T(8,128)(2,1)}, bf16[5,2,1,128,512]{4,3,1,0,2:T(8,128)(2,1)}, u32[]{:S(2)}, u32[]{:S(2)}) collective-permute-start(bf16[5,2,1,128,512]{4,3,1,0,2:T(8,128)(2,1)} %get-tuple-element.38), channel_id=1, source_target_pairs={{4,0},{8,4},{12,8},{5,1},{9,5},{13,9},{6,2},{10,6},{14,10},{7,3},{... | collective-permute-start | bytes 3932168 | tf_op jit(solution)/shard_map/ppermute | solution.py:166
  44.3 138.7 %collective-permute-start.3 = (bf16[5,2,1,128,512]{4,3,1,0,2:T(8,128)(2,1)}, bf16[5,2,1,128,512]{4,3,1,0,2:T(8,128)(2,1)S(1)}, u32[]{:S(2)}, u32[]{:S(2)}) collective-permute-start(bf16[5,2,1,128,512]{4,3,1,0,2:T(8,128)(2,1)} %get-tuple-element.39), channel_id=1, source_target_pairs={{8,0},{12,4},{9,1},{13,5},{10,2},{14,6},{11,3},{15,7},{24,16},{28,... | collective-permute-start | bytes 3932168 | tf_op jit(solution)/shard_map/ppermute | solution.py:166
  45.6 139.9 %collective-permute-start.4 = (bf16[5,2,1,128,512]{4,3,1,0,2:T(8,128)(2,1)}, bf16[5,2,1,128,512]{4,3,1,0,2:T(8,128)(2,1)S(1)}, u32[]{:S(2)}, u32[]{:S(2)}) collective-permute-start(bf16[5,2,1,128,512]{4,3,1,0,2:T(8,128)(2,1)} %get-tuple-element.40), channel_id=1, source_target_pairs={{12,0},{13,1},{14,2},{15,3},{28,16},{29,17},{30,18},{31,19}} | collective-permute-start | bytes 3932168 | tf_op jit(solution)/shard_map/ppermute | solution.py:166
  46.9 141.0 %collective-permute-start.6 = (bf16[2048,256]{1,0:T(8,128)(2,1)}, bf16[2048,256]{1,0:T(8,128)(2,1)}, u32[]{:S(2)}, u32[]{:S(2)}) collective-permute-start(bf16[2048,256]{1,0:T(8,128)(2,1)} %pad_maximum_fusion.4.rest_2_), channel_id=1, source_target_pairs={{0,4},{4,8},{8,12},{1,5},{5,9},{9,13},{2,6},{6,10},{10,14},{3,7},{... | collective-permute-start | bytes 3145736 | tf_op jit(solution)/shard_map/ppermute | solution.py:166
  61.7 133.0 %collective-permute-start.5 = (bf16[2048,256]{1,0:T(8,128)(2,1)}, bf16[2048,256]{1,0:T(8,128)(2,1)}, u32[]{:S(2)}, u32[]{:S(2)}) collective-permute-start(bf16[2048,256]{1,0:T(8,128)(2,1)} %pad_maximum_fusion.4.rest_2_), channel_id=1, source_target_pairs={{0,8},{4,12},{1,9},{5,13},{2,10},{6,14},{3,11},{7,15},{16,24},{20,... | collective-permute-start | bytes 3145736 | tf_op jit(solution)/shard_map/ppermute | solution.py:166
  131.8 129.9 %collective-permute-start.7 = (bf16[2048,256]{1,0:T(8,128)(2,1)}, bf16[2048,256]{1,0:T(8,128)(2,1)}, u32[]{:S(2)}, u32[]{:S(2)}) collective-permute-start(bf16[2048,256]{1,0:T(8,128)(2,1)} %get-tuple-element.32), channel_id=1, source_target_pairs={{4,0},{8,4},{12,8},{5,1},{9,5},{13,9},{6,2},{10,6},{14,10},{7,3},{... | collective-permute-start | bytes 3145736 | tf_op jit(solution)/shard_map/ppermute | solution.py:166
  183.0 1.1 copy-start.4
  184.0 78.7 %copy-start.1 = (f32[2048,256]{1,0:T(8,128)S(1)}, f32[2048,256]{1,0:T(8,128)}, u32[]{:S(2)}) copy-start(f32[2048,256]{1,0:T(8,128)} %get-tuple-element.31) | copy-start | bytes 6291460
  184.0 78.7 %collective-permute-start.8 = (bf16[2048,256]{1,0:T(8,128)(2,1)}, bf16[2048,256]{1,0:T(8,128)(2,1)}, u32[]{:S(2)}, u32[]{:S(2)}) collective-permute-start(bf16[2048,256]{1,0:T(8,128)(2,1)} %get-tuple-element.33), channel_id=1, source_target_pairs={{8,0},{12,4},{9,1},{13,5},{10,2},{14,6},{11,3},{15,7},{24,16},{28,... | collective-permute-start | bytes 3145736 | tf_op jit(solution)/shard_map/ppermute | solution.py:166
  185.5 76.3 %copy-start.2 = (bf16[5,2,1,128,512]{4,3,1,0,2:T(8,128)(2,1)}, bf16[5,2,1,128,512]{4,3,1,0,2:T(8,128)(2,1)S(1)}, u32[]{:S(2)}) copy-start(bf16[5,2,1,128,512]{4,3,1,0,2:T(8,128)(2,1)S(1)} %collective-permute-done.4) | copy-start | bytes 3932164
  185.5 95.1 %collective-permute-start.11 = (bf16[5,2,1,128,512]{4,3,1,0,2:T(8,128)(2,1)}, bf16[5,2,1,128,512]{4,3,1,0,2:T(8,128)(2,1)}, u32[]{:S(2)}, u32[]{:S(2)}) collective-permute-start(bf16[5,2,1,128,512]{4,3,1,0,2:T(8,128)(2,1)} %get-tuple-element.38), channel_id=1, source_target_pairs={{0,12},{1,13},{2,14},{3,15},{16,28},{17,29},{18,30},{19,31}} | collective-permute-start | bytes 3932168 | tf_op jit(solution)/shard_map/ppermute | solution.py:166
  187.9 95.5 %collective-permute-start.12 = (bf16[5,2,1,128,512]{4,3,1,0,2:T(8,128)(2,1)}, bf16[5,2,1,128,512]{4,3,1,0,2:T(8,128)(2,1)}, u32[]{:S(2)}, u32[]{:S(2)}) collective-permute-start(bf16[5,2,1,128,512]{4,3,1,0,2:T(8,128)(2,1)} %get-tuple-element.39), channel_id=1, source_target_pairs={{0,8},{4,12},{1,9},{5,13},{2,10},{6,14},{3,11},{7,15},{16,24},{20,... | collective-permute-start | bytes 3932168 | tf_op jit(solution)/shard_map/ppermute | solution.py:166
  194.8 90.0 %collective-permute-start.13 = (bf16[5,2,1,128,512]{4,3,1,0,2:T(8,128)(2,1)}, bf16[5,2,1,128,512]{4,3,1,0,2:T(8,128)(2,1)}, u32[]{:S(2)}, u32[]{:S(2)}) collective-permute-start(bf16[5,2,1,128,512]{4,3,1,0,2:T(8,128)(2,1)} %get-tuple-element.40), channel_id=1, source_target_pairs={{0,4},{4,8},{8,12},{1,5},{5,9},{9,13},{2,6},{6,10},{10,14},{3,7},{... | collective-permute-start | bytes 3932168 | tf_op jit(solution)/shard_map/ppermute | solution.py:166
  261.7 15.7 %collective-permute-start.9 = (bf16[2048,256]{1,0:T(8,128)(2,1)}, bf16[2048,256]{1,0:T(8,128)(2,1)S(1)}, u32[]{:S(2)}, u32[]{:S(2)}) collective-permute-start(bf16[2048,256]{1,0:T(8,128)(2,1)} %get-tuple-element.35), channel_id=1, source_target_pairs={{8,4},{12,8},{9,5},{13,9},{10,6},{14,10},{11,7},{15,11},{24,20},{2... | collective-permute-start | bytes 3145736 | tf_op jit(solution)/shard_map/ppermute | solution.py:166
  262.7 2.0 copy-start.13
  262.7 2.2 copy-start.14
  276.2 1.6 copy-start.6
  277.4 46.1 %collective-permute-start.14 = (bf16[2,768,512]{2,1,0:T(8,128)(2,1)}, bf16[2,768,512]{2,1,0:T(8,128)(2,1)}, u32[]{:S(2)}, u32[]{:S(2)}) collective-permute-start(bf16[2,768,512]{2,1,0:T(8,128)(2,1)} %pad_maximum_fusion.2), channel_id=1, source_target_pairs={{0,4},{4,0},{8,12},{12,8},{1,5},{5,1},{9,13},{13,9},{2,6},{6,2},{1... | collective-permute-start | bytes 4718600 | tf_op jit(solution)/shard_map/ppermute | solution.py:220
  279.1 4.2 %copy-start.5 = (bf16[5,2,1,128,512]{4,3,1,0,2:T(8,128)(2,1)S(1)}, bf16[5,2,1,128,512]{4,3,1,0,2:T(8,128)(2,1)}, u32[]{:S(2)}) copy-start(bf16[5,2,1,128,512]{4,3,1,0,2:T(8,128)(2,1)} %copy-done.4) | copy-start | bytes 3932164
  279.1 68.2 %collective-permute-start.10 = (bf16[2048,256]{1,0:T(8,128)(2,1)}, bf16[2048,256]{1,0:T(8,128)(2,1)}, u32[]{:S(2)}, u32[]{:S(2)}) collective-permute-start(bf16[2048,256]{1,0:T(8,128)(2,1)} %add_convert_fusion.1), channel_id=1, source_target_pairs={{4,0},{8,4},{12,8},{5,1},{9,5},{13,9},{6,2},{10,6},{14,10},{7,3},{... | collective-permute-start | bytes 3145736 | tf_op jit(solution)/shard_map/ppermute | solution.py:166
  283.3 1.5 copy-start.3
  323.5 23.8 %copy-start = (f32[2048,256]{1,0:T(8,128)S(1)}, f32[2048,256]{1,0:T(8,128)}, u32[]{:S(2)}) copy-start(f32[2048,256]{1,0:T(8,128)} %get-tuple-element.34) | copy-start | bytes 6291460
  325.7 29.9 %collective-permute-start.15 = (bf16[1,768,512]{2,1,0:T(8,128)(2,1)S(1)}, bf16[1,768,512]{2,1,0:T(8,128)(2,1)S(1)}, u32[]{:S(2)}, u32[]{:S(2)}) collective-permute-start(bf16[1,768,512]{2,1,0:T(8,128)(2,1)S(1)} %dynamic-slice_convert_fusion), channel_id=1, source_target_pairs={{0,8},{4,12},{8,0},{12,4},{1,9},{5,13},{9,1},{13,5},{2,10},{6,14},... | collective-permute-start | bytes 2359304 | tf_op jit(solution)/shard_map/ppermute | solution.py:220
  355.6 1.2 copy-start.16
  355.6 15.4 %collective-permute-start.16 = (bf16[2,256,512]{2,1,0:T(8,128)(2,1)}, bf16[2,256,512]{2,1,0:T(8,128)(2,1)}, u32[]{:S(2)}, u32[]{:S(2)}) collective-permute-start(bf16[2,256,512]{2,1,0:T(8,128)(2,1)} %pad_maximum_fusion.10), channel_id=1, source_target_pairs={{0,4},{4,0},{8,12},{12,8},{1,5},{5,1},{9,13},{13,9},{2,6},{6,2},{1... | collective-permute-start | bytes 1572872 | tf_op jit(solution)/shard_map/ppermute | solution.py:220
  360.0 32.1 %all-to-all-start = ((bf16[4,1,128,512]{3,2,1,0:T(8,128)(2,1)}), bf16[4,1,128,512]{3,2,1,0:T(8,128)(2,1)S(1)}, u32[]{:S(2)}, u32[]{:S(2)}) async-start(bf16[4,1,128,512]{3,2,1,0:T(8,128)(2,1)} %bitcast.127), calls=%async_computation | async-start | bytes 1048576 | tf_op jit(solution)/shard_map/all_to_all | solution.py:334
  366.7 7.0 %copy-start.11 = (bf16[2048,256]{1,0:T(8,128)(2,1)S(1)}, bf16[2048,256]{1,0:T(8,128)(2,1)}, u32[]{:S(2)}) copy-start(bf16[2048,256]{1,0:T(8,128)(2,1)} %get-tuple-element.23) | copy-start | bytes 3145732
  366.8 7.0 %copy-start.12 = (bf16[2048,256]{1,0:T(8,128)(2,1)S(1)}, bf16[2048,256]{1,0:T(8,128)(2,1)}, u32[]{:S(2)}) copy-start(bf16[2048,256]{1,0:T(8,128)(2,1)} %get-tuple-element.28) | copy-start | bytes 3145732
  372.3 16.6 %collective-permute-start.17 = (bf16[1,256,512]{2,1,0:T(8,128)(2,1)S(1)}, bf16[1,256,512]{2,1,0:T(8,128)(2,1)S(1)}, u32[]{:S(2)}, u32[]{:S(2)}) collective-permute-start(bf16[1,256,512]{2,1,0:T(8,128)(2,1)S(1)} %dynamic-slice_convert_fusion.1), channel_id=1, source_target_pairs={{0,8},{4,12},{8,0},{12,4},{1,9},{5,13},{9,1},{13,5},{2,10},{6,14},... | collective-permute-start | bytes 786440 | tf_op jit(solution)/shard_map/ppermute | solution.py:220
  373.8 15.2 %copy-start.15 = (bf16[1,1,1,4,128,512]{5,4,3,1,2,0:T(8,128)(2,1)S(1)}, bf16[1,1,1,4,128,512]{5,4,3,1,2,0:T(8,128)(2,1)}, u32[]{:S(2)}) copy-start(bf16[1,1,1,4,128,512]{5,4,3,1,2,0:T(8,128)(2,1)} %get-tuple-element.42) | copy-start | bytes 1572868
  392.1 13.7 %all-to-all-start.1 = ((bf16[4,1,128,512]{3,2,1,0:T(8,128)(2,1)}), bf16[4,1,128,512]{3,2,1,0:T(8,128)(2,1)S(1)}, u32[]{:S(2)}, u32[]{:S(2)}) async-start(bf16[4,1,128,512]{3,2,1,0:T(8,128)(2,1)} %bitcast.128), calls=%async_computation.1 | async-start | bytes 1048576 | tf_op jit(solution)/shard_map/all_to_all | solution.py:334

commit v4 on v3

--- a/solution.py
+++ b/solution.py
@@ -283,7 +283,9 @@
     parts_sent = []
     for k in range(kv_count):
         last = k == kv_count - 1
-        gate = after(skip, *leftward) if whole_blocks and k == 1 else skip
+        gate = skip
+        if whole_blocks and k < 2:
+            gate = after(skip, *(leftward[1:] if k else leftward[:1]))
         head_out, head_dq, *grads = attention(queries, out_grad, gate, windows[k], k, group)
         far, own = grads[:reach], grads[reach]
         outs.append(head_out)

time: 408 us -> 384 us (0.941)
  waiting for transfers between devices: 142 us -> 61.4 us
  starting transfers between devices: 60.2 us -> 117 us
    ppermute x14, waiting for transfers between devices: 92.3 us -> 22.4 us  [shifted(): return lax.ppermute(x, axis, pairs)]
    ppermute x14, starting transfers between devices: 48.4 us -> 93.7 us  [shifted(): return lax.ppermute(x, axis, pairs)]
    ppermute x4, starting transfers between devices: 1.56 us -> 15.6 us  [swap_sum(): got = lax.ppermute(send, 'seq', [(i, i ^ step) for i in range(n)])]
    ppermute x4, waiting for transfers between devices: 42.1 us -> 31 us  [swap_sum(): got = lax.ppermute(send, 'seq', [(i, i ^ step) for i in range(n)])]
  transfers between devices with their start and end apart: 20 -> 20, of which waited for: 7 -> 6; matrix products, arithmetic and copies ran while one was open for 17% -> 18% of each run, Pallas kernels for 32% -> 34%
where the time goes in v4:
time: 384 us; the launch traced here: 383 us
  Pallas kernels  129 us (34%)
  starting transfers between devices  117 us (30%)
  waiting for transfers between devices  61.4 us (16%)
  matrix products  27.5 us (7%)
  other arithmetic  26.1 us (7%)
  local copies, waits for them, and re-layouts  21 us (5%)
    pallas_call x2, Pallas kernels, attention(): pl.pallas_call(functools.partial(attn_body, reach, tile, group), out_shap...  129 us
    ppermute x14, starting transfers between devices, shifted(): return lax.ppermute(x, axis, pairs)  93.7 us
    ppermute x4, waiting for transfers between devices, swap_sum(): got = lax.ppermute(send, 'seq', [(i, i ^ step) for i in range(n)])  31 us
    dot_general x6, matrix products, bmm(): return jnp.einsum(spec, a, b, preferred_element_type=jnp.float32)  27.5 us
    ppermute x14, waiting for transfers between devices, shifted(): return lax.ppermute(x, axis, pairs)  22.4 us
    ppermute x4, starting transfers between devices, swap_sum(): got = lax.ppermute(send, 'seq', [(i, i ^ step) for i in range(n)])  15.6 us
    all_to_all x2, waiting for transfers between devices, per_device(): new = lax.all_to_all(new, 'seq', 0, 0)  8.01 us
  transfers between devices with their start and end apart: 20, of which 6 were waited for; matrix products, arithmetic and copies ran while one was open for 18% of the time, Pallas kernels for 34%

profile of v4, /device:TPU:0, one launch (start us, length us, event | category | flops | bytes accessed | tf_op | source)
XLA Modules:
  0.0 382.6 jit_solution(7119704413222129673)
XLA Ops:
  0.6 1.7 fusion.23
  3.4 5.9 %collective-permute-start.1 = (bf16[2048,256]{1,0:T(8,128)(2,1)}, bf16[2048,256]{1,0:T(8,128)(2,1)}, u32[]{:S(2)}, u32[]{:S(2)}) collective-permute-start(bf16[2048,256]{1,0:T(8,128)(2,1)} %pad_maximum_fusion.3.rest_2_), channel_id=1, source_target_pairs={{0,4},{4,8},{8,12},{1,5},{5,9},{9,13},{2,6},{6,10},{10,14},{3,7},{... | collective-permute-start | bytes 3145736 | tf_op jit(solution)/shard_map/ppermute | solution.py:166
  10.2 2.2 bitcast_dynamic-update-slice_fusion.7
  15.1 1.3 collective-permute-start
  16.4 14.6 %collective-permute-done.1.rest_1_ = bf16[2048,256]{1,0:T(8,128)(2,1)} collective-permute-done((bf16[2048,256]{1,0:T(8,128)(2,1)}, bf16[2048,256]{1,0:T(8,128)(2,1)}, u32[]{:S(2)}, u32[]{:S(2)}) %collective-permute-start.1) | collective-permute-done | bytes 1048608 | tf_op jit(solution)/shard_map/ppermute | solution.py:166
  31.0 1.7 collective-permute-start.2
  33.8 3.0 broadcast_in_dim.15
  38.0 1.3 collective-permute-start.3
  39.3 1.3 collective-permute-start.4
  40.6 7.8 %collective-permute-done = bf16[5,2,1,128,512]{4,3,1,0,2:T(8,128)(2,1)} collective-permute-done((bf16[5,2,1,128,512]{4,3,1,0,2:T(8,128)(2,1)}, bf16[5,2,1,128,512]{4,3,1,0,2:T(8,128)(2,1)}, u32[]{:S(2)}, u32[]{:S(2)}) %collective-permute-start) | collective-permute-done | bytes 1310752 | tf_op jit(solution)/shard_map/ppermute | solution.py:166
  48.4 60.4 %collective-permute-start.6 = (bf16[2048,256]{1,0:T(8,128)(2,1)}, bf16[2048,256]{1,0:T(8,128)(2,1)}, u32[]{:S(2)}, u32[]{:S(2)}) collective-permute-start(bf16[2048,256]{1,0:T(8,128)(2,1)} %pad_maximum_fusion.4.rest_2_), channel_id=1, source_target_pairs={{0,4},{4,8},{8,12},{1,5},{5,9},{9,13},{2,6},{6,10},{10,14},{3,7},{... | collective-permute-start | bytes 3145736 | tf_op jit(solution)/shard_map/ppermute | solution.py:166
  108.8 2.3 collective-permute-start.5
  111.1 64.6 %window_attention.2 = (bf16[2048,256]{1,0:T(8,128)(2,1)}, bf16[2048,256]{1,0:T(8,128)(2,1)}, bf16[2048,256]{1,0:T(8,128)(2,1)}, bf16[2048,256]{1,0:T(8,128)(2,1)}, f32[2048,256]{1,0:T(8,128)}) custom-call(s32[1]{0:T(128)} %bitcast.skip_ref, bf16[2048,512]{1,0:T(8,128)(2,1)} %q_ref.3, bf16[2048,512]{1,0:T(8,128)(2,1)} %g_ref.3, ...), custom_call_target="tpu_custom_call" | custom-call | flops 25769803776 | bytes 16777216 | tf_op jit(solution)/shard_map/window_attention/pallas_call | solution.py:131
  175.7 1.3 collective-permute-start.7
  178.1 1.4 collective-permute-start.8
  179.6 9.6 %collective-permute-start.11 = (bf16[5,2,1,128,512]{4,3,1,0,2:T(8,128)(2,1)}, bf16[5,2,1,128,512]{4,3,1,0,2:T(8,128)(2,1)}, u32[]{:S(2)}, u32[]{:S(2)}) collective-permute-start(bf16[5,2,1,128,512]{4,3,1,0,2:T(8,128)(2,1)} %get-tuple-element.40), channel_id=1, source_target_pairs={{0,12},{1,13},{2,14},{3,15},{16,28},{17,29},{18,30},{19,31}} | collective-permute-start | bytes 3932168 | tf_op jit(solution)/shard_map/ppermute | solution.py:166
  189.2 2.4 collective-permute-start.12
  191.6 2.5 collective-permute-start.13
  194.0 64.6 %window_attention.3 = (bf16[2048,256]{1,0:T(8,128)(2,1)}, bf16[2048,256]{1,0:T(8,128)(2,1)}, bf16[2048,256]{1,0:T(8,128)(2,1)}, bf16[2048,256]{1,0:T(8,128)(2,1)}, f32[2048,256]{1,0:T(8,128)}) custom-call(s32[1]{0:T(128)} %bitcast.skip_ref, bf16[2048,512]{1,0:T(8,128)(2,1)} %q_ref.3, bf16[2048,512]{1,0:T(8,128)(2,1)} %g_ref.3, ...), custom_call_target="tpu_custom_call" | custom-call | flops 25769803776 | bytes 16777216 | tf_op jit(solution)/shard_map/window_attention/pallas_call | solution.py:131
  259.6 2.0 add_convert_fusion.2
  261.8 9.3 %convolution_convert_fusion = bf16[768,2048]{1,0:T(8,128)(2,1)S(1)} fusion(bf16[2048,2048]{1,0:T(8,128)(2,1)} %param.14, bf16[2048,256]{1,0:T(8,128)(2,1)S(1)} %copy-done.14, bf16[2048,256]{1,0:T(8,128)(2,1)S(1)} %add_convert_fusion.2, bf16[2048,256]{1,0:T(8,128)(2,1)S(1)} %copy-done.13), kind=kOutput, calls=%fused_computation | convolution fusion | flops 6453460992 | bytes 14680064 | tf_op jit(solution)/shard_map/tj,tk->jk/dot_general | solution.py:195
  271.6 1.5 pad_maximum_fusion.1
  273.1 1.3 pad_maximum_fusion.2
  274.7 1.3 add_convert_fusion.1
  276.0 1.4 collective-permute-start.10
  277.5 2.8 bitcast_dynamic-update-slice_fusion.2
  280.2 1.5 bitcast_dynamic-update-slice_fusion.1
  281.7 1.5 bitcast_dynamic-update-slice_fusion
  283.2 4.0 %fusion.20 = (bf16[1,2,1,4,128,512]{5,4,3,1,2,0:T(8,128)(2,1)S(1)}, bf16[1,2,1,4,128,512]{5,4,3,1,2,0:T(8,128)(2,1)S(1)}, bf16[1,2,1,4,128,512]{5,4,3,1,2,0:T(8,128)(2,1)}, bf16[1,2,1,4,128,512]{5,4,3,1,2,0:T(8,128)(2,1)}) fusion(bf16[5,2,1,4,128,512]{5,4,3,1,2,0:T(8,128)(2,1)} %bitcast_dynamic-update-slice_fusion), kind=kLoop, calls=%fused_computation.81 | loop fusion | bytes 8388608 | tf_op jit(solution)/shard_map/unstack | solution.py:316
  287.2 1.8 convolution_convert_fusion.3
  288.9 2.9 fusion.19
  291.8 4.4 %convolution_multiply_fusion = f32[2,512,512]{2,1,0:T(8,128)} fusion(bf16[2,512,512]{2,1,0:T(8,128)(2,1)} %bitcast.125, bf16[2,512,512]{2,1,0:T(8,128)(2,1)} %bitcast.124, bf16[2,512,512]{2,1,0:T(8,128)(2,1)} %convolution_convert_fusion.3), kind=kOutput, calls=%fused_computation.13 | convolution fusion | flops 1074790400 | bytes 5242880 | tf_op jit(solution)/shard_map/cbrk,cbkj->cbrj/dot_general | solution.py:195
  296.3 5.7 %collective-permute-done.14 = bf16[2,768,512]{2,1,0:T(8,128)(2,1)} collective-permute-done((bf16[2,768,512]{2,1,0:T(8,128)(2,1)}, bf16[2,768,512]{2,1,0:T(8,128)(2,1)}, u32[]{:S(2)}, u32[]{:S(2)}) %collective-permute-start.14) | collective-permute-done | bytes 1572896 | tf_op jit(solution)/shard_map/ppermute | solution.py:220
  301.9 2.1 convert_add_fusion
  304.1 12.0 %collective-permute-start.15 = (bf16[1,768,512]{2,1,0:T(8,128)(2,1)S(1)}, bf16[1,768,512]{2,1,0:T(8,128)(2,1)S(1)}, u32[]{:S(2)}, u32[]{:S(2)}) collective-permute-start(bf16[1,768,512]{2,1,0:T(8,128)(2,1)S(1)} %dynamic-slice_convert_fusion), channel_id=1, source_target_pairs={{0,8},{4,12},{8,0},{12,4},{1,9},{5,13},{9,1},{13,5},{2,10},{6,14},... | collective-permute-start | bytes 2359304 | tf_op jit(solution)/shard_map/ppermute | solution.py:220
  316.1 1.6 add_convert_fusion
  317.7 5.7 %convolution_convert_fusion.1 = bf16[256,2048]{1,0:T(8,128)(2,1)S(1)} fusion(bf16[2048,256]{1,0:T(8,128)(2,1)S(1)} %add_convert_fusion, bf16[2048,2048]{1,0:T(8,128)(2,1)} %param.14), kind=kOutput, calls=%fused_computation.7 | convolution fusion | flops 2148007936 | bytes 10485760 | tf_op jit(solution)/shard_map/tj,tk->jk/dot_general | solution.py:195
  325.0 15.3 %collective-permute-done.15 = bf16[1,768,512]{2,1,0:T(8,128)(2,1)S(1)} collective-permute-done((bf16[1,768,512]{2,1,0:T(8,128)(2,1)S(1)}, bf16[1,768,512]{2,1,0:T(8,128)(2,1)S(1)}, u32[]{:S(2)}, u32[]{:S(2)}) %collective-permute-start.15) | collective-permute-done | bytes 786464 | tf_op jit(solution)/shard_map/ppermute | solution.py:220
  341.4 3.2 convolution_convert_fusion.5
  344.6 3.7 all-to-all-start
  348.3 1.3 convert_add_fusion.1
  349.7 3.0 collective-permute-start.17
  352.7 1.5 pad_maximum_fusion
  354.2 10.0 %collective-permute-done.17 = bf16[1,256,512]{2,1,0:T(8,128)(2,1)S(1)} collective-permute-done((bf16[1,256,512]{2,1,0:T(8,128)(2,1)S(1)}, bf16[1,256,512]{2,1,0:T(8,128)(2,1)S(1)}, u32[]{:S(2)}, u32[]{:S(2)}) %collective-permute-start.17) | collective-permute-done | bytes 262176 | tf_op jit(solution)/shard_map/ppermute | solution.py:220
  364.3 3.1 convolution_convert_fusion.4
  367.4 3.5 all-to-all-start.1
  373.1 8.0 %all-to-all-done.1 = bf16[4,1,128,512]{3,2,1,0:T(8,128)(2,1)S(1)} async-done(((bf16[4,1,128,512]{3,2,1,0:T(8,128)(2,1)}), bf16[4,1,128,512]{3,2,1,0:T(8,128)(2,1)S(1)}, u32[]{:S(2)}, u32[]{:S(2)}) %all-to-all-start.1) | async-done | bytes 524320 | tf_op jit(solution)/shard_map/all_to_all | solution.py:336
  381.1 1.5 maximum_convert_fusion
  (69 shorter events, 15.3 us)
Async XLA Ops:
  2.3 7.0 %copy-start.7 = (bf16[8,128,512]{2,1,0:T(8,128)(2,1)S(1)}, bf16[8,128,512]{2,1,0:T(8,128)(2,1)}, u32[]{:S(2)}) copy-start(bf16[8,128,512]{2,1,0:T(8,128)(2,1)} %param.15) | copy-start | bytes 3145732
  3.4 27.6 %collective-permute-start.1 = (bf16[2048,256]{1,0:T(8,128)(2,1)}, bf16[2048,256]{1,0:T(8,128)(2,1)}, u32[]{:S(2)}, u32[]{:S(2)}) collective-permute-start(bf16[2048,256]{1,0:T(8,128)(2,1)} %pad_maximum_fusion.3.rest_2_), channel_id=1, source_target_pairs={{0,4},{4,8},{8,12},{1,5},{5,9},{9,13},{2,6},{6,10},{10,14},{3,7},{... | collective-permute-start | bytes 3145736 | tf_op jit(solution)/shard_map/ppermute | solution.py:166
  9.3 3.1 copy-start.8
  10.2 3.1 copy-start.9
  12.4 1.8 copy-start.10
  15.1 33.2 %collective-permute-start = (bf16[5,2,1,128,512]{4,3,1,0,2:T(8,128)(2,1)}, bf16[5,2,1,128,512]{4,3,1,0,2:T(8,128)(2,1)}, u32[]{:S(2)}, u32[]{:S(2)}) collective-permute-start(bf16[5,2,1,128,512]{4,3,1,0,2:T(8,128)(2,1)} %get-tuple-element.40), channel_id=1, source_target_pairs={{4,0},{8,4},{12,8},{5,1},{9,5},{13,9},{6,2},{10,6},{14,10},{7,3},{... | collective-permute-start | bytes 3932168 | tf_op jit(solution)/shard_map/ppermute | solution.py:166
  31.0 17.3 %collective-permute-start.2 = (bf16[2048,256]{1,0:T(8,128)(2,1)}, bf16[2048,256]{1,0:T(8,128)(2,1)}, u32[]{:S(2)}, u32[]{:S(2)}) collective-permute-start(bf16[2048,256]{1,0:T(8,128)(2,1)} %collective-permute-done.1.rest_1_), channel_id=1, source_target_pairs={{4,8},{8,12},{5,9},{9,13},{6,10},{10,14},{7,11},{11,15},{20,24},{2... | collective-permute-start | bytes 3145736 | tf_op jit(solution)/shard_map/ppermute | solution.py:166
  38.0 139.0 %collective-permute-start.3 = (bf16[5,2,1,128,512]{4,3,1,0,2:T(8,128)(2,1)}, bf16[5,2,1,128,512]{4,3,1,0,2:T(8,128)(2,1)S(1)}, u32[]{:S(2)}, u32[]{:S(2)}) collective-permute-start(bf16[5,2,1,128,512]{4,3,1,0,2:T(8,128)(2,1)} %get-tuple-element.41), channel_id=1, source_target_pairs={{8,0},{12,4},{9,1},{13,5},{10,2},{14,6},{11,3},{15,7},{24,16},{28,... | collective-permute-start | bytes 3932168 | tf_op jit(solution)/shard_map/ppermute | solution.py:166
  39.3 140.3 %collective-permute-start.4 = (bf16[5,2,1,128,512]{4,3,1,0,2:T(8,128)(2,1)}, bf16[5,2,1,128,512]{4,3,1,0,2:T(8,128)(2,1)S(1)}, u32[]{:S(2)}, u32[]{:S(2)}) collective-permute-start(bf16[5,2,1,128,512]{4,3,1,0,2:T(8,128)(2,1)} %get-tuple-element.42), channel_id=1, source_target_pairs={{12,0},{13,1},{14,2},{15,3},{28,16},{29,17},{30,18},{31,19}} | collective-permute-start | bytes 3932168 | tf_op jit(solution)/shard_map/ppermute | solution.py:166
  48.4 140.8 %collective-permute-start.6 = (bf16[2048,256]{1,0:T(8,128)(2,1)}, bf16[2048,256]{1,0:T(8,128)(2,1)}, u32[]{:S(2)}, u32[]{:S(2)}) collective-permute-start(bf16[2048,256]{1,0:T(8,128)(2,1)} %pad_maximum_fusion.4.rest_2_), channel_id=1, source_target_pairs={{0,4},{4,8},{8,12},{1,5},{5,9},{9,13},{2,6},{6,10},{10,14},{3,7},{... | collective-permute-start | bytes 3145736 | tf_op jit(solution)/shard_map/ppermute | solution.py:166
  108.8 82.8 %collective-permute-start.5 = (bf16[2048,256]{1,0:T(8,128)(2,1)}, bf16[2048,256]{1,0:T(8,128)(2,1)}, u32[]{:S(2)}, u32[]{:S(2)}) collective-permute-start(bf16[2048,256]{1,0:T(8,128)(2,1)} %pad_maximum_fusion.4.rest_2_), channel_id=1, source_target_pairs={{0,8},{4,12},{1,9},{5,13},{2,10},{6,14},{3,11},{7,15},{16,24},{20,... | collective-permute-start | bytes 3145736 | tf_op jit(solution)/shard_map/ppermute | solution.py:166
  175.7 82.9 %collective-permute-start.7 = (bf16[2048,256]{1,0:T(8,128)(2,1)}, bf16[2048,256]{1,0:T(8,128)(2,1)}, u32[]{:S(2)}, u32[]{:S(2)}) collective-permute-start(bf16[2048,256]{1,0:T(8,128)(2,1)} %get-tuple-element.34), channel_id=1, source_target_pairs={{4,0},{8,4},{12,8},{5,1},{9,5},{13,9},{6,2},{10,6},{14,10},{7,3},{... | collective-permute-start | bytes 3145736 | tf_op jit(solution)/shard_map/ppermute | solution.py:166
  177.0 1.1 copy-start.4
  178.1 81.5 %copy-start.1 = (f32[2048,256]{1,0:T(8,128)S(1)}, f32[2048,256]{1,0:T(8,128)}, u32[]{:S(2)}) copy-start(f32[2048,256]{1,0:T(8,128)} %get-tuple-element.33) | copy-start | bytes 6291460
  178.1 81.5 %collective-permute-start.8 = (bf16[2048,256]{1,0:T(8,128)(2,1)}, bf16[2048,256]{1,0:T(8,128)(2,1)}, u32[]{:S(2)}, u32[]{:S(2)}) collective-permute-start(bf16[2048,256]{1,0:T(8,128)(2,1)} %get-tuple-element.35), channel_id=1, source_target_pairs={{8,0},{12,4},{9,1},{13,5},{10,2},{14,6},{11,3},{15,7},{24,16},{28,... | collective-permute-start | bytes 3145736 | tf_op jit(solution)/shard_map/ppermute | solution.py:166
  179.6 79.1 %copy-start.2 = (bf16[5,2,1,128,512]{4,3,1,0,2:T(8,128)(2,1)}, bf16[5,2,1,128,512]{4,3,1,0,2:T(8,128)(2,1)S(1)}, u32[]{:S(2)}) copy-start(bf16[5,2,1,128,512]{4,3,1,0,2:T(8,128)(2,1)S(1)} %collective-permute-done.4) | copy-start | bytes 3932164
  179.6 97.9 %collective-permute-start.11 = (bf16[5,2,1,128,512]{4,3,1,0,2:T(8,128)(2,1)}, bf16[5,2,1,128,512]{4,3,1,0,2:T(8,128)(2,1)}, u32[]{:S(2)}, u32[]{:S(2)}) collective-permute-start(bf16[5,2,1,128,512]{4,3,1,0,2:T(8,128)(2,1)} %get-tuple-element.40), channel_id=1, source_target_pairs={{0,12},{1,13},{2,14},{3,15},{16,28},{17,29},{18,30},{19,31}} | collective-permute-start | bytes 3932168 | tf_op jit(solution)/shard_map/ppermute | solution.py:166
  189.2 91.1 %collective-permute-start.12 = (bf16[5,2,1,128,512]{4,3,1,0,2:T(8,128)(2,1)}, bf16[5,2,1,128,512]{4,3,1,0,2:T(8,128)(2,1)}, u32[]{:S(2)}, u32[]{:S(2)}) collective-permute-start(bf16[5,2,1,128,512]{4,3,1,0,2:T(8,128)(2,1)} %get-tuple-element.41), channel_id=1, source_target_pairs={{0,8},{4,12},{1,9},{5,13},{2,10},{6,14},{3,11},{7,15},{16,24},{20,... | collective-permute-start | bytes 3932168 | tf_op jit(solution)/shard_map/ppermute | solution.py:166
  191.6 90.1 %collective-permute-start.13 = (bf16[5,2,1,128,512]{4,3,1,0,2:T(8,128)(2,1)}, bf16[5,2,1,128,512]{4,3,1,0,2:T(8,128)(2,1)}, u32[]{:S(2)}, u32[]{:S(2)}) collective-permute-start(bf16[5,2,1,128,512]{4,3,1,0,2:T(8,128)(2,1)} %get-tuple-element.42), channel_id=1, source_target_pairs={{0,4},{4,8},{8,12},{1,5},{5,9},{9,13},{2,6},{6,10},{10,14},{3,7},{... | collective-permute-start | bytes 3932168 | tf_op jit(solution)/shard_map/ppermute | solution.py:166
  258.6 15.7 %collective-permute-start.9 = (bf16[2048,256]{1,0:T(8,128)(2,1)}, bf16[2048,256]{1,0:T(8,128)(2,1)S(1)}, u32[]{:S(2)}, u32[]{:S(2)}) collective-permute-start(bf16[2048,256]{1,0:T(8,128)(2,1)} %get-tuple-element.37), channel_id=1, source_target_pairs={{8,4},{12,8},{9,5},{13,9},{10,6},{14,10},{11,7},{15,11},{24,20},{2... | collective-permute-start | bytes 3145736 | tf_op jit(solution)/shard_map/ppermute | solution.py:166
  259.6 2.0 copy-start.13
  259.6 2.2 copy-start.14
  273.1 1.6 copy-start.6
  274.4 27.6 %collective-permute-start.14 = (bf16[2,768,512]{2,1,0:T(8,128)(2,1)}, bf16[2,768,512]{2,1,0:T(8,128)(2,1)}, u32[]{:S(2)}, u32[]{:S(2)}) collective-permute-start(bf16[2,768,512]{2,1,0:T(8,128)(2,1)} %pad_maximum_fusion.2), channel_id=1, source_target_pairs={{0,4},{4,0},{8,12},{12,8},{1,5},{5,1},{9,13},{13,9},{2,6},{6,2},{1... | collective-permute-start | bytes 4718600 | tf_op jit(solution)/shard_map/ppermute | solution.py:220
  276.0 4.2 %copy-start.5 = (bf16[5,2,1,128,512]{4,3,1,0,2:T(8,128)(2,1)S(1)}, bf16[5,2,1,128,512]{4,3,1,0,2:T(8,128)(2,1)}, u32[]{:S(2)}) copy-start(bf16[5,2,1,128,512]{4,3,1,0,2:T(8,128)(2,1)} %copy-done.4) | copy-start | bytes 3932164
  276.0 40.1 %collective-permute-start.10 = (bf16[2048,256]{1,0:T(8,128)(2,1)}, bf16[2048,256]{1,0:T(8,128)(2,1)}, u32[]{:S(2)}, u32[]{:S(2)}) collective-permute-start(bf16[2048,256]{1,0:T(8,128)(2,1)} %add_convert_fusion.1), channel_id=1, source_target_pairs={{4,0},{8,4},{12,8},{5,1},{9,5},{13,9},{6,2},{10,6},{14,10},{7,3},{... | collective-permute-start | bytes 3145736 | tf_op jit(solution)/shard_map/ppermute | solution.py:166
  280.2 1.5 copy-start.3
  301.9 14.2 %copy-start = (f32[2048,256]{1,0:T(8,128)S(1)}, f32[2048,256]{1,0:T(8,128)}, u32[]{:S(2)}) copy-start(f32[2048,256]{1,0:T(8,128)} %get-tuple-element.36) | copy-start | bytes 6291460
  304.1 36.1 %collective-permute-start.15 = (bf16[1,768,512]{2,1,0:T(8,128)(2,1)S(1)}, bf16[1,768,512]{2,1,0:T(8,128)(2,1)S(1)}, u32[]{:S(2)}, u32[]{:S(2)}) collective-permute-start(bf16[1,768,512]{2,1,0:T(8,128)(2,1)S(1)} %dynamic-slice_convert_fusion), channel_id=1, source_target_pairs={{0,8},{4,12},{8,0},{12,4},{1,9},{5,13},{9,1},{13,5},{2,10},{6,14},... | collective-permute-start | bytes 2359304 | tf_op jit(solution)/shard_map/ppermute | solution.py:220
  324.4 17.0 %copy-start.16 = (bf16[1,1,1,4,128,512]{5,4,3,1,2,0:T(8,128)(2,1)S(1)}, bf16[1,1,1,4,128,512]{5,4,3,1,2,0:T(8,128)(2,1)}, u32[]{:S(2)}) copy-start(bf16[1,1,1,4,128,512]{5,4,3,1,2,0:T(8,128)(2,1)} %get-tuple-element.43) | copy-start | bytes 1572868
  324.4 23.9 %collective-permute-start.16 = (bf16[2,256,512]{2,1,0:T(8,128)(2,1)}, bf16[2,256,512]{2,1,0:T(8,128)(2,1)}, u32[]{:S(2)}, u32[]{:S(2)}) collective-permute-start(bf16[2,256,512]{2,1,0:T(8,128)(2,1)} %pad_maximum_fusion.10), channel_id=1, source_target_pairs={{0,4},{4,0},{8,12},{12,8},{1,5},{5,1},{9,13},{13,9},{2,6},{6,2},{1... | collective-permute-start | bytes 1572872 | tf_op jit(solution)/shard_map/ppermute | solution.py:220
  344.6 22.8 %all-to-all-start = ((bf16[4,1,128,512]{3,2,1,0:T(8,128)(2,1)}), bf16[4,1,128,512]{3,2,1,0:T(8,128)(2,1)S(1)}, u32[]{:S(2)}, u32[]{:S(2)}) async-start(bf16[4,1,128,512]{3,2,1,0:T(8,128)(2,1)} %bitcast.127), calls=%async_computation | async-start | bytes 1048576 | tf_op jit(solution)/shard_map/all_to_all | solution.py:336
  348.3 4.4 %copy-start.11 = (bf16[2048,256]{1,0:T(8,128)(2,1)S(1)}, bf16[2048,256]{1,0:T(8,128)(2,1)}, u32[]{:S(2)}) copy-start(bf16[2048,256]{1,0:T(8,128)(2,1)} %get-tuple-element.25) | copy-start | bytes 3145732
  348.3 4.4 %copy-start.12 = (bf16[2048,256]{1,0:T(8,128)(2,1)S(1)}, bf16[2048,256]{1,0:T(8,128)(2,1)}, u32[]{:S(2)}) copy-start(bf16[2048,256]{1,0:T(8,128)(2,1)} %get-tuple-element.30) | copy-start | bytes 3145732
  349.7 14.5 %collective-permute-start.17 = (bf16[1,256,512]{2,1,0:T(8,128)(2,1)S(1)}, bf16[1,256,512]{2,1,0:T(8,128)(2,1)S(1)}, u32[]{:S(2)}, u32[]{:S(2)}) collective-permute-start(bf16[1,256,512]{2,1,0:T(8,128)(2,1)S(1)} %dynamic-slice_convert_fusion.1), channel_id=1, source_target_pairs={{0,8},{4,12},{8,0},{12,4},{1,9},{5,13},{9,1},{13,5},{2,10},{6,14},... | collective-permute-start | bytes 786440 | tf_op jit(solution)/shard_map/ppermute | solution.py:220
  352.7 11.6 %copy-start.15 = (bf16[1,1,1,4,128,512]{5,4,3,1,2,0:T(8,128)(2,1)S(1)}, bf16[1,1,1,4,128,512]{5,4,3,1,2,0:T(8,128)(2,1)}, u32[]{:S(2)}) copy-start(bf16[1,1,1,4,128,512]{5,4,3,1,2,0:T(8,128)(2,1)} %get-tuple-element.44) | copy-start | bytes 1572868
  367.4 13.7 %all-to-all-start.1 = ((bf16[4,1,128,512]{3,2,1,0:T(8,128)(2,1)}), bf16[4,1,128,512]{3,2,1,0:T(8,128)(2,1)S(1)}, u32[]{:S(2)}, u32[]{:S(2)}) async-start(bf16[4,1,128,512]{3,2,1,0:T(8,128)(2,1)} %bitcast.128), calls=%async_computation.1 | async-start | bytes 1048576 | tf_op jit(solution)/shard_map/all_to_all | solution.py:336

commit v5 on v4

--- a/solution.py
+++ b/solution.py
@@ -276,7 +276,7 @@
         for d in range(1, n):
             packed = message((seq_index + n - d) % n)
             if d > 1:
-                packed = after(packed, windows[0][reach - 1])
+                packed = after(packed, leftward[0])
             leftward.append(shifted(packed, "seq", -d))
         rightward = []
     outs, query_grads, key_grads, value_grads, joined = [], [], [], [], []

time: 384 us -> 369 us (0.961)
  starting transfers between devices: 117 us -> 59 us
  waiting for transfers between devices: 61.4 us -> 104 us
    ppermute x14, starting transfers between devices: 93.7 us -> 45.1 us  [shifted(): return lax.ppermute(x, axis, pairs)]
    ppermute x14, waiting for transfers between devices: 22.4 us -> 55.9 us  [shifted(): return lax.ppermute(x, axis, pairs)]
    ppermute x4, starting transfers between devices: 15.6 us -> 6.89 us  [swap_sum(): got = lax.ppermute(send, 'seq', [(i, i ^ step) for i in range(n)])]
    ppermute x4, waiting for transfers between devices: 31 us -> 37.2 us  [swap_sum(): got = lax.ppermute(send, 'seq', [(i, i ^ step) for i in range(n)])]
  transfers between devices with their start and end apart: 20 -> 20, of which waited for: 6 -> 8; matrix products, arithmetic and copies ran while one was open for 18% -> 19% of each run, Pallas kernels for 34% -> 35%
where the time goes in v5:
time: 369 us; the launch traced here: 368 us
  Pallas kernels  129 us (35%)
  waiting for transfers between devices  104 us (28%)
  starting transfers between devices  59 us (16%)
  matrix products  27.5 us (7%)
  other arithmetic  25.9 us (7%)
  local copies, waits for them, and re-layouts  21 us (6%)
    pallas_call x2, Pallas kernels, attention(): pl.pallas_call(functools.partial(attn_body, reach, tile, group), out_shap...  129 us
    ppermute x14, waiting for transfers between devices, shifted(): return lax.ppermute(x, axis, pairs)  55.9 us
    ppermute x14, starting transfers between devices, shifted(): return lax.ppermute(x, axis, pairs)  45.1 us
    ppermute x4, waiting for transfers between devices, swap_sum(): got = lax.ppermute(send, 'seq', [(i, i ^ step) for i in range(n)])  37.2 us
    dot_general x6, matrix products, bmm(): return jnp.einsum(spec, a, b, preferred_element_type=jnp.float32)  27.5 us
    all_to_all x2, waiting for transfers between devices, per_device(): new = lax.all_to_all(new, 'seq', 0, 0)  11.3 us
  transfers between devices with their start and end apart: 20, of which 8 were waited for; matrix products, arithmetic and copies ran while one was open for 19% of the time, Pallas kernels for 35%

profile of v5, /device:TPU:0, one launch (start us, length us, event | category | flops | bytes accessed | tf_op | source)
XLA Modules:
  0.0 368.0 jit_solution(6199211981134123741)
XLA Ops:
  0.6 1.7 fusion.23
  3.4 5.9 %collective-permute-start.1 = (bf16[2048,256]{1,0:T(8,128)(2,1)}, bf16[2048,256]{1,0:T(8,128)(2,1)}, u32[]{:S(2)}, u32[]{:S(2)}) collective-permute-start(bf16[2048,256]{1,0:T(8,128)(2,1)} %pad_maximum_fusion.3.rest_2_), channel_id=1, source_target_pairs={{0,4},{4,8},{8,12},{1,5},{5,9},{9,13},{2,6},{6,10},{10,14},{3,7},{... | collective-permute-start | bytes 3145736 | tf_op jit(solution)/shard_map/ppermute | solution.py:166
  10.2 2.2 bitcast_dynamic-update-slice_fusion.7
  15.1 1.3 collective-permute-start
  16.4 14.6 %collective-permute-done.1.rest_1_ = bf16[2048,256]{1,0:T(8,128)(2,1)} collective-permute-done((bf16[2048,256]{1,0:T(8,128)(2,1)}, bf16[2048,256]{1,0:T(8,128)(2,1)}, u32[]{:S(2)}, u32[]{:S(2)}) %collective-permute-start.1) | collective-permute-done | bytes 1048608 | tf_op jit(solution)/shard_map/ppermute | solution.py:166
  31.0 1.7 collective-permute-start.2
  33.8 3.0 broadcast_in_dim.15
  38.0 9.6 %collective-permute-done = bf16[5,2,1,128,512]{4,3,1,0,2:T(8,128)(2,1)} collective-permute-done((bf16[5,2,1,128,512]{4,3,1,0,2:T(8,128)(2,1)}, bf16[5,2,1,128,512]{4,3,1,0,2:T(8,128)(2,1)}, u32[]{:S(2)}, u32[]{:S(2)}) %collective-permute-start) | collective-permute-done | bytes 1310752 | tf_op jit(solution)/shard_map/ppermute | solution.py:166
  47.6 1.3 collective-permute-start.3
  48.9 1.3 collective-permute-start.4
  50.2 11.6 %collective-permute-start.6 = (bf16[2048,256]{1,0:T(8,128)(2,1)}, bf16[2048,256]{1,0:T(8,128)(2,1)}, u32[]{:S(2)}, u32[]{:S(2)}) collective-permute-start(bf16[2048,256]{1,0:T(8,128)(2,1)} %pad_maximum_fusion.4.rest_2_), channel_id=1, source_target_pairs={{0,4},{4,8},{8,12},{1,5},{5,9},{9,13},{2,6},{6,10},{10,14},{3,7},{... | collective-permute-start | bytes 3145736 | tf_op jit(solution)/shard_map/ppermute | solution.py:166
  61.7 5.4 %collective-permute-start.5 = (bf16[2048,256]{1,0:T(8,128)(2,1)}, bf16[2048,256]{1,0:T(8,128)(2,1)}, u32[]{:S(2)}, u32[]{:S(2)}) collective-permute-start(bf16[2048,256]{1,0:T(8,128)(2,1)} %pad_maximum_fusion.4.rest_2_), channel_id=1, source_target_pairs={{0,8},{4,12},{1,9},{5,13},{2,10},{6,14},{3,11},{7,15},{16,24},{20,... | collective-permute-start | bytes 3145736 | tf_op jit(solution)/shard_map/ppermute | solution.py:166
  67.2 64.6 %window_attention.2 = (bf16[2048,256]{1,0:T(8,128)(2,1)}, bf16[2048,256]{1,0:T(8,128)(2,1)}, bf16[2048,256]{1,0:T(8,128)(2,1)}, bf16[2048,256]{1,0:T(8,128)(2,1)}, f32[2048,256]{1,0:T(8,128)}) custom-call(s32[1]{0:T(128)} %bitcast.skip_ref, bf16[2048,512]{1,0:T(8,128)(2,1)} %q_ref.3, bf16[2048,512]{1,0:T(8,128)(2,1)} %g_ref.3, ...), custom_call_target="tpu_custom_call" | custom-call | flops 25769803776 | bytes 16777216 | tf_op jit(solution)/shard_map/window_attention/pallas_call | solution.py:131
  131.8 1.3 collective-permute-start.7
  133.1 3.2 collective-permute-done.3
  137.4 1.4 collective-permute-start.8
  138.9 6.4 %collective-permute-start.11 = (bf16[5,2,1,128,512]{4,3,1,0,2:T(8,128)(2,1)}, bf16[5,2,1,128,512]{4,3,1,0,2:T(8,128)(2,1)}, u32[]{:S(2)}, u32[]{:S(2)}) collective-permute-start(bf16[5,2,1,128,512]{4,3,1,0,2:T(8,128)(2,1)} %get-tuple-element.40), channel_id=1, source_target_pairs={{0,12},{1,13},{2,14},{3,15},{16,28},{17,29},{18,30},{19,31}} | collective-permute-start | bytes 3932168 | tf_op jit(solution)/shard_map/ppermute | solution.py:166
  145.2 2.9 collective-permute-start.12
  148.2 2.3 collective-permute-start.13
  150.5 64.6 %window_attention.3 = (bf16[2048,256]{1,0:T(8,128)(2,1)}, bf16[2048,256]{1,0:T(8,128)(2,1)}, bf16[2048,256]{1,0:T(8,128)(2,1)}, bf16[2048,256]{1,0:T(8,128)(2,1)}, f32[2048,256]{1,0:T(8,128)}) custom-call(s32[1]{0:T(128)} %bitcast.skip_ref, bf16[2048,512]{1,0:T(8,128)(2,1)} %q_ref.3, bf16[2048,512]{1,0:T(8,128)(2,1)} %g_ref.3, ...), custom_call_target="tpu_custom_call" | custom-call | flops 25769803776 | bytes 16777216 | tf_op jit(solution)/shard_map/window_attention/pallas_call | solution.py:131
  216.1 2.0 add_convert_fusion.2
  218.3 9.3 %convolution_convert_fusion = bf16[768,2048]{1,0:T(8,128)(2,1)S(1)} fusion(bf16[2048,2048]{1,0:T(8,128)(2,1)} %param.14, bf16[2048,256]{1,0:T(8,128)(2,1)S(1)} %copy-done.14, bf16[2048,256]{1,0:T(8,128)(2,1)S(1)} %add_convert_fusion.2, bf16[2048,256]{1,0:T(8,128)(2,1)S(1)} %copy-done.13), kind=kOutput, calls=%fused_computation | convolution fusion | flops 6453460992 | bytes 14680064 | tf_op jit(solution)/shard_map/tj,tk->jk/dot_general | solution.py:195
  228.0 1.5 pad_maximum_fusion.1
  229.5 1.3 pad_maximum_fusion.2
  231.2 1.3 add_convert_fusion.1
  232.5 1.4 collective-permute-start.10
  233.9 2.8 bitcast_dynamic-update-slice_fusion.2
  236.7 1.5 bitcast_dynamic-update-slice_fusion.1
  238.2 1.5 bitcast_dynamic-update-slice_fusion
  239.6 4.0 %fusion.20 = (bf16[1,2,1,4,128,512]{5,4,3,1,2,0:T(8,128)(2,1)S(1)}, bf16[1,2,1,4,128,512]{5,4,3,1,2,0:T(8,128)(2,1)S(1)}, bf16[1,2,1,4,128,512]{5,4,3,1,2,0:T(8,128)(2,1)}, bf16[1,2,1,4,128,512]{5,4,3,1,2,0:T(8,128)(2,1)}) fusion(bf16[5,2,1,4,128,512]{5,4,3,1,2,0:T(8,128)(2,1)} %bitcast_dynamic-update-slice_fusion), kind=kLoop, calls=%fused_computation.81 | loop fusion | bytes 8388608 | tf_op jit(solution)/shard_map/unstack | solution.py:316
  243.7 1.8 convolution_convert_fusion.3
  245.4 2.9 fusion.19
  248.3 4.4 %convolution_multiply_fusion = f32[2,512,512]{2,1,0:T(8,128)} fusion(bf16[2,512,512]{2,1,0:T(8,128)(2,1)} %bitcast.125, bf16[2,512,512]{2,1,0:T(8,128)(2,1)} %bitcast.124, bf16[2,512,512]{2,1,0:T(8,128)(2,1)} %convolution_convert_fusion.3), kind=kOutput, calls=%fused_computation.13 | convolution fusion | flops 1074790400 | bytes 5242880 | tf_op jit(solution)/shard_map/cbrk,cbkj->cbrj/dot_general | solution.py:195
  252.7 15.7 %collective-permute-done.14 = bf16[2,768,512]{2,1,0:T(8,128)(2,1)} collective-permute-done((bf16[2,768,512]{2,1,0:T(8,128)(2,1)}, bf16[2,768,512]{2,1,0:T(8,128)(2,1)}, u32[]{:S(2)}, u32[]{:S(2)}) %collective-permute-start.14) | collective-permute-done | bytes 1572896 | tf_op jit(solution)/shard_map/ppermute | solution.py:220
  268.5 2.1 convert_add_fusion
  270.7 6.8 %collective-permute-start.15 = (bf16[1,768,512]{2,1,0:T(8,128)(2,1)S(1)}, bf16[1,768,512]{2,1,0:T(8,128)(2,1)S(1)}, u32[]{:S(2)}, u32[]{:S(2)}) collective-permute-start(bf16[1,768,512]{2,1,0:T(8,128)(2,1)S(1)} %dynamic-slice_convert_fusion), channel_id=1, source_target_pairs={{0,8},{4,12},{8,0},{12,4},{1,9},{5,13},{9,1},{13,5},{2,10},{6,14},... | collective-permute-start | bytes 2359304 | tf_op jit(solution)/shard_map/ppermute | solution.py:220
  277.5 28.4 %collective-permute-done.10 = bf16[2048,256]{1,0:T(8,128)(2,1)} collective-permute-done((bf16[2048,256]{1,0:T(8,128)(2,1)}, bf16[2048,256]{1,0:T(8,128)(2,1)}, u32[]{:S(2)}, u32[]{:S(2)}) %collective-permute-start.10) | collective-permute-done | bytes 1048608 | tf_op jit(solution)/shard_map/ppermute | solution.py:166
  305.9 1.6 add_convert_fusion
  307.4 5.7 %convolution_convert_fusion.1 = bf16[256,2048]{1,0:T(8,128)(2,1)S(1)} fusion(bf16[2048,256]{1,0:T(8,128)(2,1)S(1)} %add_convert_fusion, bf16[2048,2048]{1,0:T(8,128)(2,1)} %param.14), kind=kOutput, calls=%fused_computation.7 | convolution fusion | flops 2148007936 | bytes 10485760 | tf_op jit(solution)/shard_map/tj,tk->jk/dot_general | solution.py:195
  315.3 3.2 convolution_convert_fusion.5
  318.5 3.5 all-to-all-start
  322.0 9.5 %collective-permute-done.16 = bf16[2,256,512]{2,1,0:T(8,128)(2,1)} collective-permute-done((bf16[2,256,512]{2,1,0:T(8,128)(2,1)}, bf16[2,256,512]{2,1,0:T(8,128)(2,1)}, u32[]{:S(2)}, u32[]{:S(2)}) %collective-permute-start.16) | collective-permute-done | bytes 524320 | tf_op jit(solution)/shard_map/ppermute | solution.py:220
  332.8 1.5 pad_maximum_fusion
  334.3 12.0 %collective-permute-done.17 = bf16[1,256,512]{2,1,0:T(8,128)(2,1)S(1)} collective-permute-done((bf16[1,256,512]{2,1,0:T(8,128)(2,1)S(1)}, bf16[1,256,512]{2,1,0:T(8,128)(2,1)S(1)}, u32[]{:S(2)}, u32[]{:S(2)}) %collective-permute-start.17) | collective-permute-done | bytes 262176 | tf_op jit(solution)/shard_map/ppermute | solution.py:220
  346.4 3.1 convolution_convert_fusion.4
  349.5 3.5 all-to-all-start.1
  355.2 11.3 %all-to-all-done.1 = bf16[4,1,128,512]{3,2,1,0:T(8,128)(2,1)S(1)} async-done(((bf16[4,1,128,512]{3,2,1,0:T(8,128)(2,1)}), bf16[4,1,128,512]{3,2,1,0:T(8,128)(2,1)S(1)}, u32[]{:S(2)}, u32[]{:S(2)}) %all-to-all-start.1) | async-done | bytes 524320 | tf_op jit(solution)/shard_map/all_to_all | solution.py:336
  366.6 1.5 maximum_convert_fusion
  (69 shorter events, 16.0 us)
Async XLA Ops:
  2.3 7.0 %copy-start.7 = (bf16[8,128,512]{2,1,0:T(8,128)(2,1)S(1)}, bf16[8,128,512]{2,1,0:T(8,128)(2,1)}, u32[]{:S(2)}) copy-start(bf16[8,128,512]{2,1,0:T(8,128)(2,1)} %param.15) | copy-start | bytes 3145732
  3.4 27.6 %collective-permute-start.1 = (bf16[2048,256]{1,0:T(8,128)(2,1)}, bf16[2048,256]{1,0:T(8,128)(2,1)}, u32[]{:S(2)}, u32[]{:S(2)}) collective-permute-start(bf16[2048,256]{1,0:T(8,128)(2,1)} %pad_maximum_fusion.3.rest_2_), channel_id=1, source_target_pairs={{0,4},{4,8},{8,12},{1,5},{5,9},{9,13},{2,6},{6,10},{10,14},{3,7},{... | collective-permute-start | bytes 3145736 | tf_op jit(solution)/shard_map/ppermute | solution.py:166
  9.3 3.1 copy-start.8
  10.2 3.1 copy-start.9
  12.4 1.8 copy-start.10
  15.1 32.4 %collective-permute-start = (bf16[5,2,1,128,512]{4,3,1,0,2:T(8,128)(2,1)}, bf16[5,2,1,128,512]{4,3,1,0,2:T(8,128)(2,1)}, u32[]{:S(2)}, u32[]{:S(2)}) collective-permute-start(bf16[5,2,1,128,512]{4,3,1,0,2:T(8,128)(2,1)} %get-tuple-element.40), channel_id=1, source_target_pairs={{4,0},{8,4},{12,8},{5,1},{9,5},{13,9},{6,2},{10,6},{14,10},{7,3},{... | collective-permute-start | bytes 3932168 | tf_op jit(solution)/shard_map/ppermute | solution.py:166
  31.0 19.1 %collective-permute-start.2 = (bf16[2048,256]{1,0:T(8,128)(2,1)}, bf16[2048,256]{1,0:T(8,128)(2,1)}, u32[]{:S(2)}, u32[]{:S(2)}) collective-permute-start(bf16[2048,256]{1,0:T(8,128)(2,1)} %collective-permute-done.1.rest_1_), channel_id=1, source_target_pairs={{4,8},{8,12},{5,9},{9,13},{6,10},{10,14},{7,11},{11,15},{20,24},{2... | collective-permute-start | bytes 3145736 | tf_op jit(solution)/shard_map/ppermute | solution.py:166
  47.6 88.7 %collective-permute-start.3 = (bf16[5,2,1,128,512]{4,3,1,0,2:T(8,128)(2,1)}, bf16[5,2,1,128,512]{4,3,1,0,2:T(8,128)(2,1)S(1)}, u32[]{:S(2)}, u32[]{:S(2)}) collective-permute-start(bf16[5,2,1,128,512]{4,3,1,0,2:T(8,128)(2,1)} %get-tuple-element.41), channel_id=1, source_target_pairs={{8,0},{12,4},{9,1},{13,5},{10,2},{14,6},{11,3},{15,7},{24,16},{28,... | collective-permute-start | bytes 3932168 | tf_op jit(solution)/shard_map/ppermute | solution.py:166
  48.9 90.0 %collective-permute-start.4 = (bf16[5,2,1,128,512]{4,3,1,0,2:T(8,128)(2,1)}, bf16[5,2,1,128,512]{4,3,1,0,2:T(8,128)(2,1)S(1)}, u32[]{:S(2)}, u32[]{:S(2)}) collective-permute-start(bf16[5,2,1,128,512]{4,3,1,0,2:T(8,128)(2,1)} %get-tuple-element.42), channel_id=1, source_target_pairs={{12,0},{13,1},{14,2},{15,3},{28,16},{29,17},{30,18},{31,19}} | collective-permute-start | bytes 3932168 | tf_op jit(solution)/shard_map/ppermute | solution.py:166
  50.2 95.0 %collective-permute-start.6 = (bf16[2048,256]{1,0:T(8,128)(2,1)}, bf16[2048,256]{1,0:T(8,128)(2,1)}, u32[]{:S(2)}, u32[]{:S(2)}) collective-permute-start(bf16[2048,256]{1,0:T(8,128)(2,1)} %pad_maximum_fusion.4.rest_2_), channel_id=1, source_target_pairs={{0,4},{4,8},{8,12},{1,5},{5,9},{9,13},{2,6},{6,10},{10,14},{3,7},{... | collective-permute-start | bytes 3145736 | tf_op jit(solution)/shard_map/ppermute | solution.py:166
  61.7 86.4 %collective-permute-start.5 = (bf16[2048,256]{1,0:T(8,128)(2,1)}, bf16[2048,256]{1,0:T(8,128)(2,1)}, u32[]{:S(2)}, u32[]{:S(2)}) collective-permute-start(bf16[2048,256]{1,0:T(8,128)(2,1)} %pad_maximum_fusion.4.rest_2_), channel_id=1, source_target_pairs={{0,8},{4,12},{1,9},{5,13},{2,10},{6,14},{3,11},{7,15},{16,24},{20,... | collective-permute-start | bytes 3145736 | tf_op jit(solution)/shard_map/ppermute | solution.py:166
  131.8 83.3 %collective-permute-start.7 = (bf16[2048,256]{1,0:T(8,128)(2,1)}, bf16[2048,256]{1,0:T(8,128)(2,1)}, u32[]{:S(2)}, u32[]{:S(2)}) collective-permute-start(bf16[2048,256]{1,0:T(8,128)(2,1)} %get-tuple-element.34), channel_id=1, source_target_pairs={{4,0},{8,4},{12,8},{5,1},{9,5},{13,9},{6,2},{10,6},{14,10},{7,3},{... | collective-permute-start | bytes 3145736 | tf_op jit(solution)/shard_map/ppermute | solution.py:166
  136.3 1.1 copy-start.4
  137.4 78.7 %copy-start.1 = (f32[2048,256]{1,0:T(8,128)S(1)}, f32[2048,256]{1,0:T(8,128)}, u32[]{:S(2)}) copy-start(f32[2048,256]{1,0:T(8,128)} %get-tuple-element.33) | copy-start | bytes 6291460
  137.4 78.7 %collective-permute-start.8 = (bf16[2048,256]{1,0:T(8,128)(2,1)}, bf16[2048,256]{1,0:T(8,128)(2,1)}, u32[]{:S(2)}, u32[]{:S(2)}) collective-permute-start(bf16[2048,256]{1,0:T(8,128)(2,1)} %get-tuple-element.35), channel_id=1, source_target_pairs={{8,0},{12,4},{9,1},{13,5},{10,2},{14,6},{11,3},{15,7},{24,16},{28,... | collective-permute-start | bytes 3145736 | tf_op jit(solution)/shard_map/ppermute | solution.py:166
  138.8 76.2 %copy-start.2 = (bf16[5,2,1,128,512]{4,3,1,0,2:T(8,128)(2,1)}, bf16[5,2,1,128,512]{4,3,1,0,2:T(8,128)(2,1)S(1)}, u32[]{:S(2)}) copy-start(bf16[5,2,1,128,512]{4,3,1,0,2:T(8,128)(2,1)S(1)} %collective-permute-done.4) | copy-start | bytes 3932164
  138.9 95.1 %collective-permute-start.11 = (bf16[5,2,1,128,512]{4,3,1,0,2:T(8,128)(2,1)}, bf16[5,2,1,128,512]{4,3,1,0,2:T(8,128)(2,1)}, u32[]{:S(2)}, u32[]{:S(2)}) collective-permute-start(bf16[5,2,1,128,512]{4,3,1,0,2:T(8,128)(2,1)} %get-tuple-element.40), channel_id=1, source_target_pairs={{0,12},{1,13},{2,14},{3,15},{16,28},{17,29},{18,30},{19,31}} | collective-permute-start | bytes 3932168 | tf_op jit(solution)/shard_map/ppermute | solution.py:166
  145.2 91.5 %collective-permute-start.12 = (bf16[5,2,1,128,512]{4,3,1,0,2:T(8,128)(2,1)}, bf16[5,2,1,128,512]{4,3,1,0,2:T(8,128)(2,1)}, u32[]{:S(2)}, u32[]{:S(2)}) collective-permute-start(bf16[5,2,1,128,512]{4,3,1,0,2:T(8,128)(2,1)} %get-tuple-element.41), channel_id=1, source_target_pairs={{0,8},{4,12},{1,9},{5,13},{2,10},{6,14},{3,11},{7,15},{16,24},{20,... | collective-permute-start | bytes 3932168 | tf_op jit(solution)/shard_map/ppermute | solution.py:166
  148.2 90.0 %collective-permute-start.13 = (bf16[5,2,1,128,512]{4,3,1,0,2:T(8,128)(2,1)}, bf16[5,2,1,128,512]{4,3,1,0,2:T(8,128)(2,1)}, u32[]{:S(2)}, u32[]{:S(2)}) collective-permute-start(bf16[5,2,1,128,512]{4,3,1,0,2:T(8,128)(2,1)} %get-tuple-element.42), channel_id=1, source_target_pairs={{0,4},{4,8},{8,12},{1,5},{5,9},{9,13},{2,6},{6,10},{10,14},{3,7},{... | collective-permute-start | bytes 3932168 | tf_op jit(solution)/shard_map/ppermute | solution.py:166
  215.1 15.7 %collective-permute-start.9 = (bf16[2048,256]{1,0:T(8,128)(2,1)}, bf16[2048,256]{1,0:T(8,128)(2,1)S(1)}, u32[]{:S(2)}, u32[]{:S(2)}) collective-permute-start(bf16[2048,256]{1,0:T(8,128)(2,1)} %get-tuple-element.37), channel_id=1, source_target_pairs={{8,4},{12,8},{9,5},{13,9},{10,6},{14,10},{11,7},{15,11},{24,20},{2... | collective-permute-start | bytes 3145736 | tf_op jit(solution)/shard_map/ppermute | solution.py:166
  216.1 2.0 copy-start.13
  216.1 2.2 copy-start.14
  229.5 1.6 copy-start.6
  230.8 37.6 %collective-permute-start.14 = (bf16[2,768,512]{2,1,0:T(8,128)(2,1)}, bf16[2,768,512]{2,1,0:T(8,128)(2,1)}, u32[]{:S(2)}, u32[]{:S(2)}) collective-permute-start(bf16[2,768,512]{2,1,0:T(8,128)(2,1)} %pad_maximum_fusion.2), channel_id=1, source_target_pairs={{0,4},{4,0},{8,12},{12,8},{1,5},{5,1},{9,13},{13,9},{2,6},{6,2},{1... | collective-permute-start | bytes 4718600 | tf_op jit(solution)/shard_map/ppermute | solution.py:220
  232.5 4.2 %copy-start.5 = (bf16[5,2,1,128,512]{4,3,1,0,2:T(8,128)(2,1)S(1)}, bf16[5,2,1,128,512]{4,3,1,0,2:T(8,128)(2,1)}, u32[]{:S(2)}) copy-start(bf16[5,2,1,128,512]{4,3,1,0,2:T(8,128)(2,1)} %copy-done.4) | copy-start | bytes 3932164
  232.5 73.4 %collective-permute-start.10 = (bf16[2048,256]{1,0:T(8,128)(2,1)}, bf16[2048,256]{1,0:T(8,128)(2,1)}, u32[]{:S(2)}, u32[]{:S(2)}) collective-permute-start(bf16[2048,256]{1,0:T(8,128)(2,1)} %add_convert_fusion.1), channel_id=1, source_target_pairs={{4,0},{8,4},{12,8},{5,1},{9,5},{13,9},{6,2},{10,6},{14,10},{7,3},{... | collective-permute-start | bytes 3145736 | tf_op jit(solution)/shard_map/ppermute | solution.py:166
  236.7 1.5 copy-start.3
  268.5 37.4 %copy-start = (f32[2048,256]{1,0:T(8,128)S(1)}, f32[2048,256]{1,0:T(8,128)}, u32[]{:S(2)}) copy-start(f32[2048,256]{1,0:T(8,128)} %get-tuple-element.36) | copy-start | bytes 6291460
  270.7 43.5 %collective-permute-start.15 = (bf16[1,768,512]{2,1,0:T(8,128)(2,1)S(1)}, bf16[1,768,512]{2,1,0:T(8,128)(2,1)S(1)}, u32[]{:S(2)}, u32[]{:S(2)}) collective-permute-start(bf16[1,768,512]{2,1,0:T(8,128)(2,1)S(1)} %dynamic-slice_convert_fusion), channel_id=1, source_target_pairs={{0,8},{4,12},{8,0},{12,4},{1,9},{5,13},{9,1},{13,5},{2,10},{6,14},... | collective-permute-start | bytes 2359304 | tf_op jit(solution)/shard_map/ppermute | solution.py:220
  314.1 1.2 copy-start.16
  314.1 17.3 %collective-permute-start.16 = (bf16[2,256,512]{2,1,0:T(8,128)(2,1)}, bf16[2,256,512]{2,1,0:T(8,128)(2,1)}, u32[]{:S(2)}, u32[]{:S(2)}) collective-permute-start(bf16[2,256,512]{2,1,0:T(8,128)(2,1)} %pad_maximum_fusion.10), channel_id=1, source_target_pairs={{0,4},{4,0},{8,12},{12,8},{1,5},{5,1},{9,13},{13,9},{2,6},{6,2},{1... | collective-permute-start | bytes 1572872 | tf_op jit(solution)/shard_map/ppermute | solution.py:220
  318.5 31.0 %all-to-all-start = ((bf16[4,1,128,512]{3,2,1,0:T(8,128)(2,1)}), bf16[4,1,128,512]{3,2,1,0:T(8,128)(2,1)S(1)}, u32[]{:S(2)}, u32[]{:S(2)}) async-start(bf16[4,1,128,512]{3,2,1,0:T(8,128)(2,1)} %bitcast.127), calls=%async_computation | async-start | bytes 1048576 | tf_op jit(solution)/shard_map/all_to_all | solution.py:336
  322.0 10.8 %copy-start.11 = (bf16[2048,256]{1,0:T(8,128)(2,1)S(1)}, bf16[2048,256]{1,0:T(8,128)(2,1)}, u32[]{:S(2)}) copy-start(bf16[2048,256]{1,0:T(8,128)(2,1)} %get-tuple-element.25) | copy-start | bytes 3145732
  322.0 10.8 %copy-start.12 = (bf16[2048,256]{1,0:T(8,128)(2,1)S(1)}, bf16[2048,256]{1,0:T(8,128)(2,1)}, u32[]{:S(2)}) copy-start(bf16[2048,256]{1,0:T(8,128)(2,1)} %get-tuple-element.30) | copy-start | bytes 3145732
  332.7 13.6 %collective-permute-start.17 = (bf16[1,256,512]{2,1,0:T(8,128)(2,1)S(1)}, bf16[1,256,512]{2,1,0:T(8,128)(2,1)S(1)}, u32[]{:S(2)}, u32[]{:S(2)}) collective-permute-start(bf16[1,256,512]{2,1,0:T(8,128)(2,1)S(1)} %dynamic-slice_convert_fusion.1), channel_id=1, source_target_pairs={{0,8},{4,12},{8,0},{12,4},{1,9},{5,13},{9,1},{13,5},{2,10},{6,14},... | collective-permute-start | bytes 786440 | tf_op jit(solution)/shard_map/ppermute | solution.py:220
  332.8 13.6 %copy-start.15 = (bf16[1,1,1,4,128,512]{5,4,3,1,2,0:T(8,128)(2,1)S(1)}, bf16[1,1,1,4,128,512]{5,4,3,1,2,0:T(8,128)(2,1)}, u32[]{:S(2)}) copy-start(bf16[1,1,1,4,128,512]{5,4,3,1,2,0:T(8,128)(2,1)} %get-tuple-element.44) | copy-start | bytes 1572868
  349.5 17.1 %all-to-all-start.1 = ((bf16[4,1,128,512]{3,2,1,0:T(8,128)(2,1)}), bf16[4,1,128,512]{3,2,1,0:T(8,128)(2,1)S(1)}, u32[]{:S(2)}, u32[]{:S(2)}) async-start(bf16[4,1,128,512]{3,2,1,0:T(8,128)(2,1)} %bitcast.128), calls=%async_computation.1 | async-start | bytes 1048576 | tf_op jit(solution)/shard_map/all_to_all | solution.py:336

commit v6 on v5

--- a/solution.py
+++ b/solution.py
@@ -199,7 +199,7 @@
     return bmm("tj,tk->jk", columns, layer_input).astype(jnp.bfloat16)
 
 
-def swap_sum(term, n, width):
+def swap_sum(term, n, width, sent=None):
     index = lax.axis_index("seq")
     if n & (n - 1):
         parts = jnp.stack([term[:, i * width:(i + 1) * width] for i in range(n)])
@@ -217,6 +217,8 @@
             pairs = pieces.reshape((pieces.shape[0] // 2, 2) + pieces.shape[1:])
             keep = lax.dynamic_index_in_dim(pairs, mine, 1, False)
             send = lax.dynamic_index_in_dim(pairs, 1 - mine, 1, False).astype(jnp.bfloat16)
+        if sent is not None:
+            sent.append(send)
         got = lax.ppermute(send, "seq", [(i, i ^ step) for i in range(n)])
         pieces = keep.astype(jnp.float32) + got.astype(jnp.float32)
         step *= 2
@@ -294,45 +296,50 @@
             for d in range(1, n):
                 packed = after(message((seq_index + d) % n), head_out)
                 rightward.append(shifted(packed, "seq", d))
-        if not last:
-            for d in range(1, reach + 1):
-                own = own + shifted(far[reach - d], "seq", -d).astype(jnp.float32)
-        else:
-            if whole_blocks:
-                early = jnp.concatenate(joined + [head_dq], axis=1)
-                early_term = swap_sum(project(early, layer_input), n, per_owner * order)
+        if whole_blocks and last:
+            back = [shifted(far[reach - d], "seq", -d) for d in range(1, reach + 1)]
+            early = jnp.concatenate(joined + [head_dq], axis=1)
+            sent = []
+            early_term = swap_sum(project(early, layer_input), n, per_owner * order, sent)
+            for d in range(1, n):
+                source = (seq_index + d) % n
+                piece = jnp.where(seq_index + d < n, leftward[d - 1], rightward[n - d - 1])
+                whole = lax.dynamic_update_slice_in_dim(whole, piece[:, :, :, None], source, 3)
+            m_own, lo_own, ln_own, ro_own, rn_own = whole.reshape(
+                5, kv_count, per_owner, order, order)
+            right_turn = bmm("cbrk,cbrj->cbkj", ro_own, rn_own).astype(jnp.bfloat16)
+            turned = bmm("cbrk,cbkj->cbrj", m_own, right_turn).astype(jnp.bfloat16)
+            carried = moment_decay * bmm("cbrk,cbkj->cbrj", lo_own, turned)
+            back[0] = after(back[0], carried, *sent)
+        elif last and kv_count == 1:
             carry = far[0]
             for d in range(reach, 0, -1):
                 carry = shifted(carry, "seq", -1, d)
-                if whole_blocks and d == reach:
-                    whole = after(whole, carry)
                 if d > 1:
                     carry = (carry.astype(jnp.float32) + far[reach - d + 1].astype(jnp.float32)).astype(jnp.bfloat16)
-            if whole_blocks:
-                for d in range(1, n):
-                    source = (seq_index + d) % n
-                    piece = jnp.where(seq_index + d < n, leftward[d - 1], rightward[n - d - 1])
-                    whole = lax.dynamic_update_slice_in_dim(whole, piece[:, :, :, None], source, 3)
-                m_own, lo_own, ln_own, ro_own, rn_own = whole.reshape(
-                    5, kv_count, per_owner, order, order)
-                right_turn = bmm("cbrk,cbrj->cbkj", ro_own, rn_own).astype(jnp.bfloat16)
-                turned = bmm("cbrk,cbkj->cbrj", m_own, right_turn).astype(jnp.bfloat16)
-                carried = moment_decay * bmm("cbrk,cbkj->cbrj", lo_own, turned)
-                carry = after(carry, carried)
-            own = own + carry.astype(jnp.float32)
+            back = [carry]
+        else:
+            back = [shifted(far[reach - d], "seq", -d) for d in range(1, reach + 1)]
+        for piece in back:
+            own = own + piece.astype(jnp.float32)
         kv_grad = own.astype(jnp.bfloat16)
         key_grads.append(kv_grad[:, :hd])
         value_grads.append(kv_grad[:, hd:])
         joined.append(jnp.concatenate([head_dq, kv_grad], axis=1))
     if whole_blocks:
         late_term = swap_sum(project(kv_grad, layer_input), n, per_owner * order)
-        grads = jnp.concatenate([early_term, late_term], axis=0).astype(jnp.bfloat16)
         news = []
+        ready = None
         for k in range(kv_count):
-            grad = grads[k * order:(k + 1) * order].reshape(order, per_owner, order)
+            grad = early_term[k * order:(k + 1) * order]
+            if k == kv_count - 1:
+                late = late_term if ready is None else after(late_term, ready)
+                grad = jnp.concatenate([grad, late], axis=0)
+            grad = grad.astype(jnp.bfloat16).reshape(order, per_owner, order)
             inner = carried[k] + (1.0 - moment_decay) * bmm("jbr,bjk->brk", grad, rn_own[k])
             new = bmm("brk,brj->bkj", ln_own[k], inner.astype(jnp.bfloat16)).astype(jnp.bfloat16)
             new = jnp.transpose(new.reshape(per_owner, n, share_rows, order), (1, 0, 2, 3))
+            ready = new
             new = lax.all_to_all(new, "seq", 0, 0)
             news.append(new.reshape(row_blocks, share_rows, order).astype(jnp.float32))
     if whole_blocks:

time: 369 us -> 387 us (1.049)
  waiting for transfers between devices: 104 us -> 129 us
  local copies, waits for them, and re-layouts: 21 us -> 26.1 us
  starting transfers between devices: 59 us -> 54.1 us
  matrix products: 27.5 us -> 22.7 us
    ppermute x4, waiting for transfers between devices: 37.2 us -> 78.7 us  [swap_sum(): got = lax.ppermute(send, 'seq', [(i, i ^ step) for i in range(n)])]
    ppermute x14, waiting for transfers between devices: 55.9 us -> 28.5 us  [shifted(): return lax.ppermute(x, axis, pairs)]
    all_to_all x2, waiting for transfers between devices: 11.3 us -> 22 us  [per_device(): new = lax.all_to_all(new, 'seq', 0, 0)]
    dot_general x6, matrix products: 27.5 us -> 22.7 us  [bmm(): return jnp.einsum(spec, a, b, preferred_element_type=jnp.float32)]
    ppermute x4, starting transfers between devices: 6.89 us -> 2.72 us  [swap_sum(): got = lax.ppermute(send, 'seq', [(i, i ^ step) for i in range(n)])]
    unnamed x38 -> x46, local copies, waits for them, and re-layouts: 6.53 us -> 9.3 us
  transfers between devices with their start and end apart: 20 -> 20, of which waited for: 8 -> 9; matrix products, arithmetic and copies ran while one was open for 19% -> 16% of each run, Pallas kernels for 35% -> 33%
where the time goes in v6:
time: 387 us; the launch traced here: 386 us
  waiting for transfers between devices  129 us (33%)
  Pallas kernels  129 us (33%)
  starting transfers between devices  54.1 us (14%)
  local copies, waits for them, and re-layouts  26.1 us (7%)
  other arithmetic  23.6 us (6%)
  matrix products  22.7 us (6%)
    pallas_call x2, Pallas kernels, attention(): pl.pallas_call(functools.partial(attn_body, reach, tile, group), out_shap...  129 us
    ppermute x4, waiting for transfers between devices, swap_sum(): got = lax.ppermute(send, 'seq', [(i, i ^ step) for i in range(n)])  78.7 us
    ppermute x14, starting transfers between devices, shifted(): return lax.ppermute(x, axis, pairs)  44.4 us
    ppermute x14, waiting for transfers between devices, shifted(): return lax.ppermute(x, axis, pairs)  28.5 us
    dot_general x6, matrix products, bmm(): return jnp.einsum(spec, a, b, preferred_element_type=jnp.float32)  22.7 us
    all_to_all x2, waiting for transfers between devices, per_device(): new = lax.all_to_all(new, 'seq', 0, 0)  22 us
    unnamed x46, local copies, waits for them, and re-layouts  9.3 us
  transfers between devices with their start and end apart: 20, of which 9 were waited for; matrix products, arithmetic and copies ran while one was open for 16% of the time, Pallas kernels for 33%

profile of v6, /device:TPU:0, one launch (start us, length us, event | category | flops | bytes accessed | tf_op | source)
XLA Modules:
  0.0 386.1 jit_solution(1858871717942207674)
XLA Ops:
  0.6 1.7 fusion.26
  3.4 6.0 %collective-permute-start.1 = (bf16[2048,256]{1,0:T(8,128)(2,1)}, bf16[2048,256]{1,0:T(8,128)(2,1)}, u32[]{:S(2)}, u32[]{:S(2)}) collective-permute-start(bf16[2048,256]{1,0:T(8,128)(2,1)} %pad_maximum_fusion.3.rest_2_), channel_id=1, source_target_pairs={{0,4},{4,8},{8,12},{1,5},{5,9},{9,13},{2,6},{6,10},{10,14},{3,7},{... | collective-permute-start | bytes 3145736 | tf_op jit(solution)/shard_map/ppermute | solution.py:166
  10.3 2.2 bitcast_dynamic-update-slice_fusion.7
  15.3 1.3 collective-permute-start
  16.6 14.4 %collective-permute-done.1.rest_1_ = bf16[2048,256]{1,0:T(8,128)(2,1)} collective-permute-done((bf16[2048,256]{1,0:T(8,128)(2,1)}, bf16[2048,256]{1,0:T(8,128)(2,1)}, u32[]{:S(2)}, u32[]{:S(2)}) %collective-permute-start.1) | collective-permute-done | bytes 1048608 | tf_op jit(solution)/shard_map/ppermute | solution.py:166
  32.9 2.9 broadcast_in_dim.15
  35.9 1.2 bitcast_dynamic-update-slice_fusion.3
  37.1 10.7 %collective-permute-done = bf16[5,2,1,128,512]{4,3,1,0,2:T(8,128)(2,1)} collective-permute-done((bf16[5,2,1,128,512]{4,3,1,0,2:T(8,128)(2,1)}, bf16[5,2,1,128,512]{4,3,1,0,2:T(8,128)(2,1)}, u32[]{:S(2)}, u32[]{:S(2)}) %collective-permute-start) | collective-permute-done | bytes 1310752 | tf_op jit(solution)/shard_map/ppermute | solution.py:166
  47.7 1.3 collective-permute-start.3
  49.0 1.3 collective-permute-start.4
  50.4 11.4 %collective-permute-start.6 = (bf16[2048,256]{1,0:T(8,128)(2,1)}, bf16[2048,256]{1,0:T(8,128)(2,1)}, u32[]{:S(2)}, u32[]{:S(2)}) collective-permute-start(bf16[2048,256]{1,0:T(8,128)(2,1)} %pad_maximum_fusion.4.rest_2_), channel_id=1, source_target_pairs={{0,4},{4,8},{8,12},{1,5},{5,9},{9,13},{2,6},{6,10},{10,14},{3,7},{... | collective-permute-start | bytes 3145736 | tf_op jit(solution)/shard_map/ppermute | solution.py:166
  61.7 5.3 %collective-permute-start.5 = (bf16[2048,256]{1,0:T(8,128)(2,1)}, bf16[2048,256]{1,0:T(8,128)(2,1)}, u32[]{:S(2)}, u32[]{:S(2)}) collective-permute-start(bf16[2048,256]{1,0:T(8,128)(2,1)} %pad_maximum_fusion.4.rest_2_), channel_id=1, source_target_pairs={{0,8},{4,12},{1,9},{5,13},{2,10},{6,14},{3,11},{7,15},{16,24},{20,... | collective-permute-start | bytes 3145736 | tf_op jit(solution)/shard_map/ppermute | solution.py:166
  67.0 64.6 %window_attention.2 = (bf16[2048,256]{1,0:T(8,128)(2,1)}, bf16[2048,256]{1,0:T(8,128)(2,1)}, bf16[2048,256]{1,0:T(8,128)(2,1)}, bf16[2048,256]{1,0:T(8,128)(2,1)}, f32[2048,256]{1,0:T(8,128)}) custom-call(s32[1]{0:T(128)} %bitcast.skip_ref, bf16[2048,512]{1,0:T(8,128)(2,1)} %q_ref.3, bf16[2048,512]{1,0:T(8,128)(2,1)} %g_ref.3, bf16[2048,256]{1,0:T(8,128)(2,1)} %copy-done.18, ...), custom_call_target="tpu_custom_call" | custom-call | flops 25769803776 | bytes 16777216 | tf_op jit(solution)/shard_map/window_attention/pallas_call | solution.py:131
  131.7 1.3 collective-permute-start.7
  133.0 3.4 collective-permute-done.3
  137.5 1.4 collective-permute-start.8
  138.9 6.2 %collective-permute-start.12 = (bf16[5,2,1,128,512]{4,3,1,0,2:T(8,128)(2,1)}, bf16[5,2,1,128,512]{4,3,1,0,2:T(8,128)(2,1)}, u32[]{:S(2)}, u32[]{:S(2)}) collective-permute-start(bf16[5,2,1,128,512]{4,3,1,0,2:T(8,128)(2,1)} %get-tuple-element.41), channel_id=1, source_target_pairs={{0,12},{1,13},{2,14},{3,15},{16,28},{17,29},{18,30},{19,31}} | collective-permute-start | bytes 3932168 | tf_op jit(solution)/shard_map/ppermute | solution.py:166
  145.1 3.1 collective-permute-start.13
  148.2 2.4 collective-permute-start.14
  150.6 64.6 %window_attention.3 = (bf16[2048,256]{1,0:T(8,128)(2,1)}, bf16[2048,256]{1,0:T(8,128)(2,1)}, bf16[2048,256]{1,0:T(8,128)(2,1)}, bf16[2048,256]{1,0:T(8,128)(2,1)}, f32[2048,256]{1,0:T(8,128)}) custom-call(s32[1]{0:T(128)} %bitcast.skip_ref, bf16[2048,512]{1,0:T(8,128)(2,1)} %q_ref.3, bf16[2048,512]{1,0:T(8,128)(2,1)} %g_ref.3, ...), custom_call_target="tpu_custom_call" | custom-call | flops 25769803776 | bytes 16777216 | tf_op jit(solution)/shard_map/window_attention/pallas_call | solution.py:131
  215.2 1.3 collective-permute-start.9
  216.5 1.5 collective-permute-start.11
  218.1 2.0 add_convert_fusion.1
  220.2 9.2 %convolution_convert_fusion = bf16[768,2048]{1,0:T(8,128)(2,1)S(1)} fusion(bf16[2048,2048]{1,0:T(8,128)(2,1)} %param.14, bf16[2048,256]{1,0:T(8,128)(2,1)S(1)} %copy-done.15, bf16[2048,256]{1,0:T(8,128)(2,1)S(1)} %add_convert_fusion.1, bf16[2048,256]{1,0:T(8,128)(2,1)S(1)} %copy-done.13), kind=kOutput, calls=%fused_computation | convolution fusion | flops 6453460992 | bytes 14680064 | tf_op jit(solution)/shard_map/tj,tk->jk/dot_general | solution.py:195
  230.0 1.5 pad_maximum_fusion.1
  232.3 1.5 pad_maximum_fusion
  233.8 2.6 collective-permute-start.10
  236.4 2.8 bitcast_dynamic-update-slice_fusion.2
  239.2 1.5 bitcast_dynamic-update-slice_fusion.1
  240.7 2.8 bitcast_dynamic-update-slice_fusion
  243.4 3.9 %fusion.23 = (bf16[1,2,1,4,128,512]{5,4,3,1,2,0:T(8,128)(2,1)S(1)}, bf16[1,2,1,4,128,512]{5,4,3,1,2,0:T(8,128)(2,1)S(1)}, bf16[1,2,1,4,128,512]{5,4,3,1,2,0:T(8,128)(2,1)}, bf16[1,2,1,4,128,512]{5,4,3,1,2,0:T(8,128)(2,1)}) fusion(bf16[5,2,1,4,128,512]{5,4,3,1,2,0:T(8,128)(2,1)} %bitcast_dynamic-update-slice_fusion), kind=kLoop, calls=%fused_computation.81 | loop fusion | bytes 8388608 | tf_op jit(solution)/shard_map/unstack | solution.py:308
  248.1 49.7 %collective-permute-done.10 = bf16[2,768,512]{2,1,0:T(8,128)(2,1)S(1)} collective-permute-done((bf16[2,768,512]{2,1,0:T(8,128)(2,1)S(1)}, bf16[2,768,512]{2,1,0:T(8,128)(2,1)S(1)}, u32[]{:S(2)}, u32[]{:S(2)}) %collective-permute-start.10) | collective-permute-done | bytes 1572896 | tf_op jit(solution)/shard_map/ppermute | solution.py:222
  300.8 1.2 slice-done.1
  302.1 2.3 convolution_convert_fusion.1
  306.1 2.9 fusion.22
  309.0 4.1 %convolution_multiply_fusion = f32[2,512,512]{2,1,0:T(8,128)} fusion(bf16[2,512,512]{2,1,0:T(8,128)(2,1)} %bitcast.128, bf16[2,512,512]{2,1,0:T(8,128)(2,1)} %bitcast.127, bf16[2,512,512]{2,1,0:T(8,128)(2,1)S(1)} %convolution_convert_fusion.3), kind=kOutput, calls=%fused_computation.12 | convolution fusion | flops 1074790400 | bytes 5242880 | tf_op jit(solution)/shard_map/cbrk,cbkj->cbrj/dot_general | solution.py:195
  313.1 19.4 %collective-permute-done.16 = bf16[2,256,512]{2,1,0:T(8,128)(2,1)} collective-permute-done((bf16[2,256,512]{2,1,0:T(8,128)(2,1)}, bf16[2,256,512]{2,1,0:T(8,128)(2,1)}, u32[]{:S(2)}, u32[]{:S(2)}) %collective-permute-start.16) | collective-permute-done | bytes 524320 | tf_op jit(solution)/shard_map/ppermute | solution.py:222
  332.5 1.3 convert_add_fusion.1
  333.9 3.3 collective-permute-done.15
  337.3 1.9 add_convert_fusion.2
  339.2 6.3 %collective-permute-done.17 = bf16[1,256,512]{2,1,0:T(8,128)(2,1)S(1)} collective-permute-done((bf16[1,256,512]{2,1,0:T(8,128)(2,1)S(1)}, bf16[1,256,512]{2,1,0:T(8,128)(2,1)S(1)}, u32[]{:S(2)}, u32[]{:S(2)}) %collective-permute-start.17) | collective-permute-done | bytes 262176 | tf_op jit(solution)/shard_map/ppermute | solution.py:222
  346.3 2.9 convolution_convert_fusion.4
  349.2 3.5 all-to-all-start.1
  353.5 3.3 convolution_convert_fusion.5
  356.9 10.3 %all-to-all-done.1 = bf16[4,1,128,512]{3,2,1,0:T(8,128)(2,1)S(1)} async-done(((bf16[4,1,128,512]{3,2,1,0:T(8,128)(2,1)}), bf16[4,1,128,512]{3,2,1,0:T(8,128)(2,1)S(1)}, u32[]{:S(2)}, u32[]{:S(2)}) %all-to-all-start.1) | async-done | bytes 524320 | tf_op jit(solution)/shard_map/all_to_all | solution.py:343
  367.2 3.5 all-to-all-start
  373.0 11.7 %all-to-all-done = bf16[4,1,128,512]{3,2,1,0:T(8,128)(2,1)S(1)} async-done(((bf16[4,1,128,512]{3,2,1,0:T(8,128)(2,1)}), bf16[4,1,128,512]{3,2,1,0:T(8,128)(2,1)S(1)}, u32[]{:S(2)}, u32[]{:S(2)}) %all-to-all-start) | async-done | bytes 524320 | tf_op jit(solution)/shard_map/all_to_all | solution.py:343
  384.7 1.5 maximum_convert_fusion
  (78 shorter events, 18.6 us)
Async XLA Ops:
  2.3 7.1 %copy-start.8 = (bf16[8,128,512]{2,1,0:T(8,128)(2,1)S(1)}, bf16[8,128,512]{2,1,0:T(8,128)(2,1)}, u32[]{:S(2)}) copy-start(bf16[8,128,512]{2,1,0:T(8,128)(2,1)} %param.15) | copy-start | bytes 3145732
  3.4 27.6 %collective-permute-start.1 = (bf16[2048,256]{1,0:T(8,128)(2,1)}, bf16[2048,256]{1,0:T(8,128)(2,1)}, u32[]{:S(2)}, u32[]{:S(2)}) collective-permute-start(bf16[2048,256]{1,0:T(8,128)(2,1)} %pad_maximum_fusion.3.rest_2_), channel_id=1, source_target_pairs={{0,4},{4,8},{8,12},{1,5},{5,9},{9,13},{2,6},{6,10},{10,14},{3,7},{... | collective-permute-start | bytes 3145736 | tf_op jit(solution)/shard_map/ppermute | solution.py:166
  9.4 3.1 copy-start.9
  10.3 3.2 copy-start.10
  12.5 1.9 copy-start.11
  15.3 32.4 %collective-permute-start = (bf16[5,2,1,128,512]{4,3,1,0,2:T(8,128)(2,1)}, bf16[5,2,1,128,512]{4,3,1,0,2:T(8,128)(2,1)}, u32[]{:S(2)}, u32[]{:S(2)}) collective-permute-start(bf16[5,2,1,128,512]{4,3,1,0,2:T(8,128)(2,1)} %get-tuple-element.41), channel_id=1, source_target_pairs={{4,0},{8,4},{12,8},{5,1},{9,5},{13,9},{6,2},{10,6},{14,10},{7,3},{... | collective-permute-start | bytes 3932168 | tf_op jit(solution)/shard_map/ppermute | solution.py:166
  31.0 19.3 %collective-permute-start.2 = (bf16[2048,256]{1,0:T(8,128)(2,1)}, bf16[2048,256]{1,0:T(8,128)(2,1)S(1)}, u32[]{:S(2)}, u32[]{:S(2)}) collective-permute-start(bf16[2048,256]{1,0:T(8,128)(2,1)} %collective-permute-done.1.rest_1_), channel_id=1, source_target_pairs={{4,8},{8,12},{5,9},{9,13},{6,10},{10,14},{7,11},{11,15},{20,24},{2... | collective-permute-start | bytes 3145736 | tf_op jit(solution)/shard_map/ppermute | solution.py:166
  47.7 88.7 %collective-permute-start.3 = (bf16[5,2,1,128,512]{4,3,1,0,2:T(8,128)(2,1)}, bf16[5,2,1,128,512]{4,3,1,0,2:T(8,128)(2,1)S(1)}, u32[]{:S(2)}, u32[]{:S(2)}) collective-permute-start(bf16[5,2,1,128,512]{4,3,1,0,2:T(8,128)(2,1)} %get-tuple-element.42), channel_id=1, source_target_pairs={{8,0},{12,4},{9,1},{13,5},{10,2},{14,6},{11,3},{15,7},{24,16},{28,... | collective-permute-start | bytes 3932168 | tf_op jit(solution)/shard_map/ppermute | solution.py:166
  49.0 89.9 %collective-permute-start.4 = (bf16[5,2,1,128,512]{4,3,1,0,2:T(8,128)(2,1)}, bf16[5,2,1,128,512]{4,3,1,0,2:T(8,128)(2,1)}, u32[]{:S(2)}, u32[]{:S(2)}) collective-permute-start(bf16[5,2,1,128,512]{4,3,1,0,2:T(8,128)(2,1)} %get-tuple-element.43), channel_id=1, source_target_pairs={{12,0},{13,1},{14,2},{15,3},{28,16},{29,17},{30,18},{31,19}} | collective-permute-start | bytes 3932168 | tf_op jit(solution)/shard_map/ppermute | solution.py:166
  50.3 16.7 %copy-start.18 = (bf16[2048,256]{1,0:T(8,128)(2,1)}, bf16[2048,256]{1,0:T(8,128)(2,1)S(1)}, u32[]{:S(2)}) copy-start(bf16[2048,256]{1,0:T(8,128)(2,1)S(1)} %collective-permute-done.2.rest_0_) | copy-start | bytes 3145732
  50.4 94.7 %collective-permute-start.6 = (bf16[2048,256]{1,0:T(8,128)(2,1)}, bf16[2048,256]{1,0:T(8,128)(2,1)}, u32[]{:S(2)}, u32[]{:S(2)}) collective-permute-start(bf16[2048,256]{1,0:T(8,128)(2,1)} %pad_maximum_fusion.4.rest_2_), channel_id=1, source_target_pairs={{0,4},{4,8},{8,12},{1,5},{5,9},{9,13},{2,6},{6,10},{10,14},{3,7},{... | collective-permute-start | bytes 3145736 | tf_op jit(solution)/shard_map/ppermute | solution.py:166
  61.7 86.4 %collective-permute-start.5 = (bf16[2048,256]{1,0:T(8,128)(2,1)}, bf16[2048,256]{1,0:T(8,128)(2,1)}, u32[]{:S(2)}, u32[]{:S(2)}) collective-permute-start(bf16[2048,256]{1,0:T(8,128)(2,1)} %pad_maximum_fusion.4.rest_2_), channel_id=1, source_target_pairs={{0,8},{4,12},{1,9},{5,13},{2,10},{6,14},{3,11},{7,15},{16,24},{20,... | collective-permute-start | bytes 3145736 | tf_op jit(solution)/shard_map/ppermute | solution.py:166
  131.7 83.5 %collective-permute-start.7 = (bf16[2048,256]{1,0:T(8,128)(2,1)}, bf16[2048,256]{1,0:T(8,128)(2,1)S(1)}, u32[]{:S(2)}, u32[]{:S(2)}) collective-permute-start(bf16[2048,256]{1,0:T(8,128)(2,1)} %get-tuple-element.35), channel_id=1, source_target_pairs={{4,0},{8,4},{12,8},{5,1},{9,5},{13,9},{6,2},{10,6},{14,10},{7,3},{... | collective-permute-start | bytes 3145736 | tf_op jit(solution)/shard_map/ppermute | solution.py:166
  136.4 1.1 copy-start.5
  137.5 80.6 %copy-start.2 = (f32[2048,256]{1,0:T(8,128)S(1)}, f32[2048,256]{1,0:T(8,128)}, u32[]{:S(2)}) copy-start(f32[2048,256]{1,0:T(8,128)} %get-tuple-element.34) | copy-start | bytes 6291460
  137.5 79.0 %collective-permute-start.8 = (bf16[2048,256]{1,0:T(8,128)(2,1)}, bf16[2048,256]{1,0:T(8,128)(2,1)}, u32[]{:S(2)}, u32[]{:S(2)}) collective-permute-start(bf16[2048,256]{1,0:T(8,128)(2,1)} %get-tuple-element.36), channel_id=1, source_target_pairs={{8,0},{12,4},{9,1},{13,5},{10,2},{14,6},{11,3},{15,7},{24,16},{28,... | collective-permute-start | bytes 3145736 | tf_op jit(solution)/shard_map/ppermute | solution.py:166
  138.9 94.9 %collective-permute-start.12 = (bf16[5,2,1,128,512]{4,3,1,0,2:T(8,128)(2,1)}, bf16[5,2,1,128,512]{4,3,1,0,2:T(8,128)(2,1)}, u32[]{:S(2)}, u32[]{:S(2)}) collective-permute-start(bf16[5,2,1,128,512]{4,3,1,0,2:T(8,128)(2,1)} %get-tuple-element.41), channel_id=1, source_target_pairs={{0,12},{1,13},{2,14},{3,15},{16,28},{17,29},{18,30},{19,31}} | collective-permute-start | bytes 3932168 | tf_op jit(solution)/shard_map/ppermute | solution.py:166
  145.1 94.1 %collective-permute-start.13 = (bf16[5,2,1,128,512]{4,3,1,0,2:T(8,128)(2,1)}, bf16[5,2,1,128,512]{4,3,1,0,2:T(8,128)(2,1)}, u32[]{:S(2)}, u32[]{:S(2)}) collective-permute-start(bf16[5,2,1,128,512]{4,3,1,0,2:T(8,128)(2,1)} %get-tuple-element.42), channel_id=1, source_target_pairs={{0,8},{4,12},{1,9},{5,13},{2,10},{6,14},{3,11},{7,15},{16,24},{20,... | collective-permute-start | bytes 3932168 | tf_op jit(solution)/shard_map/ppermute | solution.py:166
  148.2 92.5 %collective-permute-start.14 = (bf16[5,2,1,128,512]{4,3,1,0,2:T(8,128)(2,1)}, bf16[5,2,1,128,512]{4,3,1,0,2:T(8,128)(2,1)}, u32[]{:S(2)}, u32[]{:S(2)}) collective-permute-start(bf16[5,2,1,128,512]{4,3,1,0,2:T(8,128)(2,1)} %get-tuple-element.43), channel_id=1, source_target_pairs={{0,4},{4,8},{8,12},{1,5},{5,9},{9,13},{2,6},{6,10},{10,14},{3,7},{... | collective-permute-start | bytes 3932168 | tf_op jit(solution)/shard_map/ppermute | solution.py:166
  215.2 2.8 copy-start.7
  215.2 84.2 %collective-permute-start.9 = (bf16[2048,256]{1,0:T(8,128)(2,1)}, bf16[2048,256]{1,0:T(8,128)(2,1)S(1)}, u32[]{:S(2)}, u32[]{:S(2)}) collective-permute-start(bf16[2048,256]{1,0:T(8,128)(2,1)} %get-tuple-element.38), channel_id=1, source_target_pairs={{4,0},{8,4},{12,8},{5,1},{9,5},{13,9},{6,2},{10,6},{14,10},{7,3},{... | collective-permute-start | bytes 3145736 | tf_op jit(solution)/shard_map/ppermute | solution.py:166
  216.5 82.9 %collective-permute-start.11 = (bf16[2048,256]{1,0:T(8,128)(2,1)}, bf16[2048,256]{1,0:T(8,128)(2,1)S(1)}, u32[]{:S(2)}, u32[]{:S(2)}) collective-permute-start(bf16[2048,256]{1,0:T(8,128)(2,1)} %get-tuple-element.40), channel_id=1, source_target_pairs={{8,0},{12,4},{9,1},{13,5},{10,2},{14,6},{11,3},{15,7},{24,16},{28,... | collective-permute-start | bytes 3145736 | tf_op jit(solution)/shard_map/ppermute | solution.py:166
  218.0 2.0 copy-start.13
  218.0 2.2 copy-start.15
  230.0 1.5 copy-start.12
  230.0 2.3 copy-start.14
  233.8 5.4 %copy-start.6 = (bf16[5,2,1,128,512]{4,3,1,0,2:T(8,128)(2,1)S(1)}, bf16[5,2,1,128,512]{4,3,1,0,2:T(8,128)(2,1)}, u32[]{:S(2)}) copy-start(bf16[5,2,1,128,512]{4,3,1,0,2:T(8,128)(2,1)} %copy-done.5) | copy-start | bytes 3932164
  233.8 64.1 %collective-permute-start.10 = (bf16[2,768,512]{2,1,0:T(8,128)(2,1)S(1)}, bf16[2,768,512]{2,1,0:T(8,128)(2,1)S(1)}, u32[]{:S(2)}, u32[]{:S(2)}) collective-permute-start(bf16[2,768,512]{2,1,0:T(8,128)(2,1)S(1)} %pad_maximum_fusion.2), channel_id=1, source_target_pairs={{0,4},{4,0},{8,12},{12,8},{1,5},{5,1},{9,13},{13,9},{2,6},{6,2},{1... | collective-permute-start | bytes 4718600 | tf_op jit(solution)/shard_map/ppermute | solution.py:222
  247.4 53.5 %slice-start = ((s8[8388608]{0:T(1024)(128)(4,1)}), s8[4194304]{0:T(1024)(128)(4,1)S(1)}, s32[]{:S(2)}) async-start(s8[8388608]{0:T(1024)(128)(4,1)} %bitcast.116), calls=%async_computation.2 | async-start | bytes 8388608
  297.8 2.5 copy-start.1
  297.8 4.2 %slice-start.1 = ((s8[8388608]{0:T(1024)(128)(4,1)}), s8[4194304]{0:T(1024)(128)(4,1)S(1)}, s32[]{:S(2)}) async-start(s8[8388608]{0:T(1024)(128)(4,1)} %bitcast.116), calls=%async_computation.3 | async-start | bytes 8388608
  298.4 2.0 copy-start
  299.4 37.8 %collective-permute-start.15 = (bf16[1,768,512]{2,1,0:T(8,128)(2,1)}, bf16[1,768,512]{2,1,0:T(8,128)(2,1)}, u32[]{:S(2)}, u32[]{:S(2)}) collective-permute-start(bf16[1,768,512]{2,1,0:T(8,128)(2,1)} %dynamic-slice_convert_fusion), channel_id=1, source_target_pairs={{0,8},{4,12},{8,0},{12,4},{1,9},{5,13},{9,1},{13,5},{2,10},{6,14},... | collective-permute-start | bytes 2359304 | tf_op jit(solution)/shard_map/ppermute | solution.py:222
  306.1 26.4 %collective-permute-start.16 = (bf16[2,256,512]{2,1,0:T(8,128)(2,1)}, bf16[2,256,512]{2,1,0:T(8,128)(2,1)}, u32[]{:S(2)}, u32[]{:S(2)}) collective-permute-start(bf16[2,256,512]{2,1,0:T(8,128)(2,1)} %pad_maximum_fusion.7), channel_id=1, source_target_pairs={{0,4},{4,0},{8,12},{12,8},{1,5},{5,1},{9,13},{13,9},{2,6},{6,2},{1... | collective-permute-start | bytes 1572872 | tf_op jit(solution)/shard_map/ppermute | solution.py:222
  333.8 12.4 %copy-start.16 = (bf16[1,1,1,4,128,512]{5,4,3,1,2,0:T(8,128)(2,1)S(1)}, bf16[1,1,1,4,128,512]{5,4,3,1,2,0:T(8,128)(2,1)}, u32[]{:S(2)}) copy-start(bf16[1,1,1,4,128,512]{5,4,3,1,2,0:T(8,128)(2,1)} %get-tuple-element.46) | copy-start | bytes 1572868
  333.9 12.4 %copy-start.17 = (bf16[1,1,1,4,128,512]{5,4,3,1,2,0:T(8,128)(2,1)S(1)}, bf16[1,1,1,4,128,512]{5,4,3,1,2,0:T(8,128)(2,1)}, u32[]{:S(2)}) copy-start(bf16[1,1,1,4,128,512]{5,4,3,1,2,0:T(8,128)(2,1)} %get-tuple-element.47) | copy-start | bytes 1572868
  333.9 11.6 %collective-permute-start.17 = (bf16[1,256,512]{2,1,0:T(8,128)(2,1)S(1)}, bf16[1,256,512]{2,1,0:T(8,128)(2,1)S(1)}, u32[]{:S(2)}, u32[]{:S(2)}) collective-permute-start(bf16[1,256,512]{2,1,0:T(8,128)(2,1)S(1)} %dynamic-slice_convert_fusion.1), channel_id=1, source_target_pairs={{0,8},{4,12},{8,0},{12,4},{1,9},{5,13},{9,1},{13,5},{2,10},{6,14},... | collective-permute-start | bytes 786440 | tf_op jit(solution)/shard_map/ppermute | solution.py:222
  339.2 7.1 %copy-start.4 = (bf16[1,768,512]{2,1,0:T(8,128)(2,1)}, bf16[1,768,512]{2,1,0:T(8,128)(2,1)S(1)}, u32[]{:S(2)}) copy-start(bf16[1,768,512]{2,1,0:T(8,128)(2,1)S(1)} %add_convert_fusion.2) | copy-start | bytes 2359300
  349.2 18.0 %all-to-all-start.1 = ((bf16[4,1,128,512]{3,2,1,0:T(8,128)(2,1)}), bf16[4,1,128,512]{3,2,1,0:T(8,128)(2,1)S(1)}, u32[]{:S(2)}, u32[]{:S(2)}) async-start(bf16[4,1,128,512]{3,2,1,0:T(8,128)(2,1)} %bitcast.55), calls=%async_computation.1 | async-start | bytes 1048576 | tf_op jit(solution)/shard_map/all_to_all | solution.py:343
  356.9 13.9 %copy-start.3 = (bf16[2048,128]{1,0:T(8,128)(2,1)S(1)}, bf16[2048,128]{1,0:T(8,128)(2,1)}, u32[]{:S(2)}) copy-start(bf16[2048,128]{1,0:T(8,128)(2,1)} %get-tuple-element.81) | copy-start | bytes 1572868
  367.2 17.4 %all-to-all-start = ((bf16[4,1,128,512]{3,2,1,0:T(8,128)(2,1)}), bf16[4,1,128,512]{3,2,1,0:T(8,128)(2,1)S(1)}, u32[]{:S(2)}, u32[]{:S(2)}) async-start(bf16[4,1,128,512]{3,2,1,0:T(8,128)(2,1)} %bitcast.129), calls=%async_computation | async-start | bytes 1048576 | tf_op jit(solution)/shard_map/all_to_all | solution.py:343

commit v7 on v5

--- a/solution.py
+++ b/solution.py
@@ -195,11 +195,37 @@
     return jnp.einsum(spec, a, b, preferred_element_type=jnp.float32)
 
 
+def pack_body(owner_ref, *refs):
+    del owner_ref
+    for i, ref in enumerate(refs[:-1]):
+        refs[-1][i] = ref[:, 0]
+
+
+def pack(owner, arrays):
+    heads, _, blocks, rows, order = arrays[0].shape
+    shape = (len(arrays), heads, blocks, rows, order)
+    return pl.pallas_call(
+        pack_body,
+        out_shape=jax.ShapeDtypeStruct(shape, arrays[0].dtype),
+        grid_spec=pltpu.PrefetchScalarGridSpec(
+            num_scalar_prefetch=1,
+            grid=(1,),
+            in_specs=[pl.BlockSpec(
+                (heads, 1, blocks, rows, order), lambda i, who: (0, who[0], 0, 0, 0))] * len(arrays),
+            out_specs=pl.BlockSpec(shape, lambda i, who: (0,) * 5),
+        ),
+        compiler_params=pltpu.CompilerParams(vmem_limit_bytes=32 << 20),
+        cost_estimate=pl.CostEstimate(
+            flops=1 << 20, bytes_accessed=4 << 20, transcendentals=0),
+        name="pack_blocks",
+    )(jnp.reshape(owner, (1,)).astype(jnp.int32), *arrays)
+
+
 def project(columns, layer_input):
     return bmm("tj,tk->jk", columns, layer_input).astype(jnp.bfloat16)
 
 
-def swap_sum(term, n, width):
+def swap_sum(term, n, width, hold=None):
     index = lax.axis_index("seq")
     if n & (n - 1):
         parts = jnp.stack([term[:, i * width:(i + 1) * width] for i in range(n)])
@@ -217,6 +243,8 @@
             pairs = pieces.reshape((pieces.shape[0] // 2, 2) + pieces.shape[1:])
             keep = lax.dynamic_index_in_dim(pairs, mine, 1, False)
             send = lax.dynamic_index_in_dim(pairs, 1 - mine, 1, False).astype(jnp.bfloat16)
+        if hold is not None and step > 1:
+            send = after(send, hold)
         got = lax.ppermute(send, "seq", [(i, i ^ step) for i in range(n)])
         pieces = keep.astype(jnp.float32) + got.astype(jnp.float32)
         step *= 2
@@ -245,19 +273,11 @@
     skip = jnp.reshape(reach - seq_index, (1,)).astype(jnp.int32)
 
     windows = []
-    gate = None
-    for k in range(kv_count):
-        held = pairs[k] if gate is None else after(pairs[k], gate)
-        shards = [pairs[k]]
-        if k == 0:
-            for hop in range(reach):
-                held = shifted(held, "seq", 1, hop)
-                shards.insert(0, held)
-            gate = held
-        else:
-            for d in range(1, reach + 1):
-                shards.insert(0, shifted(held, "seq", d))
-        windows.append(shards)
+    shards = [pairs[0]]
+    for hop in range(reach):
+        shards.insert(0, shifted(shards[0], "seq", 1, hop))
+    windows.append(shards)
+    gate = shards[0]
 
     if whole_blocks:
         cut = [
@@ -274,11 +294,16 @@
             whole, message(seq_index)[:, :, :, None], seq_index, 3)
         leftward = []
         for d in range(1, n):
-            packed = message((seq_index + n - d) % n)
-            if d > 1:
-                packed = after(packed, leftward[0])
+            owner = (seq_index + n - d) % n
+            packed = after(message(owner), leftward[0]) if d > 1 else pack(owner, cut)
             leftward.append(shifted(packed, "seq", -d))
         rightward = []
+    if whole_blocks:
+        gate = leftward[0]
+    for k in range(1, kv_count):
+        held = after(pairs[k], gate)
+        windows.append([shifted(held, "seq", d) for d in range(reach, 0, -1)] + [pairs[k]])
+
     outs, query_grads, key_grads, value_grads, joined = [], [], [], [], []
     parts_sent = []
     for k in range(kv_count):
@@ -325,14 +350,19 @@
         value_grads.append(kv_grad[:, hd:])
         joined.append(jnp.concatenate([head_dq, kv_grad], axis=1))
     if whole_blocks:
-        late_term = swap_sum(project(kv_grad, layer_input), n, per_owner * order)
-        grads = jnp.concatenate([early_term, late_term], axis=0).astype(jnp.bfloat16)
         news = []
+        ready = None
         for k in range(kv_count):
-            grad = grads[k * order:(k + 1) * order].reshape(order, per_owner, order)
+            grad = early_term[k * order:(k + 1) * order]
+            if k == kv_count - 1:
+                late_term = swap_sum(
+                    project(kv_grad, layer_input), n, per_owner * order, ready)
+                grad = jnp.concatenate([grad, late_term], axis=0)
+            grad = grad.astype(jnp.bfloat16).reshape(order, per_owner, order)
             inner = carried[k] + (1.0 - moment_decay) * bmm("jbr,bjk->brk", grad, rn_own[k])
             new = bmm("brk,brj->bkj", ln_own[k], inner.astype(jnp.bfloat16)).astype(jnp.bfloat16)
             new = jnp.transpose(new.reshape(per_owner, n, share_rows, order), (1, 0, 2, 3))
+            ready = new
             new = lax.all_to_all(new, "seq", 0, 0)
             news.append(new.reshape(row_blocks, share_rows, order).astype(jnp.float32))
     if whole_blocks:

time: 369 us -> 378 us (1.024)
  local copies, waits for them, and re-layouts: 21 us -> 30.9 us
  waiting for transfers between devices: 104 us -> 109 us
  matrix products: 27.5 us -> 22.9 us
    ppermute x14, starting transfers between devices: 45.1 us -> 34.6 us  [shifted(): return lax.ppermute(x, axis, pairs)]
    ppermute x4, waiting for transfers between devices: 37.2 us -> 29.6 us  [swap_sum(): got = lax.ppermute(send, 'seq', [(i, i ^ step) for i in range(n)])]
    ppermute x4, starting transfers between devices: 6.89 us -> 14.5 us  [swap_sum(): got = lax.ppermute(send, 'seq', [(i, i ^ step) for i in range(n)])]
    all_to_all x2, waiting for transfers between devices: 11.3 us -> 18.8 us  [per_device(): new = lax.all_to_all(new, 'seq', 0, 0)]
    ppermute x14, waiting for transfers between devices: 55.9 us -> 60.6 us  [shifted(): return lax.ppermute(x, axis, pairs)]
    unnamed x38 -> x54, local copies, waits for them, and re-layouts: 6.53 us -> 11.1 us
    dot_general x6, matrix products: 27.5 us -> 22.9 us  [bmm(): return jnp.einsum(spec, a, b, preferred_element_type=jnp.float32)]
where the time goes in v7:
time: 378 us; the launch traced here: 377 us
  Pallas kernels  130 us (34%)
  waiting for transfers between devices  109 us (29%)
  starting transfers between devices  56.7 us (15%)
  local copies, waits for them, and re-layouts  30.9 us (8%)
  other arithmetic  26.1 us (7%)
  matrix products  22.9 us (6%)
    pallas_call x2, Pallas kernels, attention(): pl.pallas_call(functools.partial(attn_body, reach, tile, group), out_shap...  129 us
    ppermute x14, waiting for transfers between devices, shifted(): return lax.ppermute(x, axis, pairs)  60.6 us
    ppermute x14, starting transfers between devices, shifted(): return lax.ppermute(x, axis, pairs)  34.6 us
    ppermute x4, waiting for transfers between devices, swap_sum(): got = lax.ppermute(send, 'seq', [(i, i ^ step) for i in range(n)])  29.6 us
    dot_general x6, matrix products, bmm(): return jnp.einsum(spec, a, b, preferred_element_type=jnp.float32)  22.9 us
    all_to_all x2, waiting for transfers between devices, per_device(): new = lax.all_to_all(new, 'seq', 0, 0)  18.8 us
    ppermute x4, starting transfers between devices, swap_sum(): got = lax.ppermute(send, 'seq', [(i, i ^ step) for i in range(n)])  14.5 us
    unnamed x54, local copies, waits for them, and re-layouts  11.1 us
  transfers between devices with their start and end apart: 20, of which 8 were waited for; matrix products, arithmetic and copies ran while one was open for 19% of the time, Pallas kernels for 35%

profile of v7, /device:TPU:0, one launch (start us, length us, event | category | flops | bytes accessed | tf_op | source)
XLA Modules:
  0.0 376.9 jit_solution(11034565077132199700)
XLA Ops:
  0.6 2.7 fusion.27
  4.4 5.9 %collective-permute-start.1 = (bf16[2048,256]{1,0:T(8,128)(2,1)}, bf16[2048,256]{1,0:T(8,128)(2,1)}, u32[]{:S(2)}, u32[]{:S(2)}) collective-permute-start(bf16[2048,256]{1,0:T(8,128)(2,1)} %pad_maximum_fusion.3.rest_2_), channel_id=1, source_target_pairs={{0,4},{4,8},{8,12},{1,5},{5,9},{9,13},{2,6},{6,10},{10,14},{3,7},{... | collective-permute-start | bytes 3145736 | tf_op jit(solution)/shard_map/ppermute | solution.py:166
  10.3 1.2 copy-done.3
  11.6 1.2 copy-done.5
  13.9 1.3 collective-permute-start
  18.4 1.8 bitcast_dynamic-update-slice_fusion.5
  21.0 11.1 %collective-permute-done.1.rest_1_ = bf16[2048,256]{1,0:T(8,128)(2,1)} collective-permute-done((bf16[2048,256]{1,0:T(8,128)(2,1)}, bf16[2048,256]{1,0:T(8,128)(2,1)}, u32[]{:S(2)}, u32[]{:S(2)}) %collective-permute-start.1) | collective-permute-done | bytes 1048608 | tf_op jit(solution)/shard_map/ppermute | solution.py:166
  32.1 1.7 collective-permute-start.2
  38.3 3.0 broadcast_in_dim.15
  42.4 4.0 %collective-permute-done = bf16[5,2,1,128,512]{4,3,2,1,0:T(8,128)(2,1)} collective-permute-done((bf16[5,2,1,128,512]{4,3,2,1,0:T(8,128)(2,1)}, bf16[5,2,1,128,512]{4,3,2,1,0:T(8,128)(2,1)}, u32[]{:S(2)}, u32[]{:S(2)}) %collective-permute-start) | collective-permute-done | bytes 1310752 | tf_op jit(solution)/shard_map/ppermute | solution.py:166
  46.4 4.2 %collective-permute-start.6 = (bf16[2048,256]{1,0:T(8,128)(2,1)}, bf16[2048,256]{1,0:T(8,128)(2,1)}, u32[]{:S(2)}, u32[]{:S(2)}) collective-permute-start(bf16[2048,256]{1,0:T(8,128)(2,1)} %pad_maximum_fusion.4.rest_2_), channel_id=1, source_target_pairs={{0,4},{4,8},{8,12},{1,5},{5,9},{9,13},{2,6},{6,10},{10,14},{3,7},{... | collective-permute-start | bytes 3145736 | tf_op jit(solution)/shard_map/ppermute | solution.py:166
  50.6 2.3 collective-permute-start.5
  52.8 1.3 collective-permute-start.3
  54.1 1.3 collective-permute-start.4
  55.4 64.6 %window_attention.2 = (bf16[2048,256]{1,0:T(8,128)(2,1)}, bf16[2048,256]{1,0:T(8,128)(2,1)}, bf16[2048,256]{1,0:T(8,128)(2,1)}, bf16[2048,256]{1,0:T(8,128)(2,1)}, f32[2048,256]{1,0:T(8,128)}) custom-call(s32[1]{0:T(128)} %bitcast.skip_ref, bf16[2048,512]{1,0:T(8,128)(2,1)} %q_ref.3, bf16[2048,512]{1,0:T(8,128)(2,1)} %g_ref.3, ...), custom_call_target="tpu_custom_call" | custom-call | flops 25769803776 | bytes 16777216 | tf_op jit(solution)/shard_map/window_attention/pallas_call | solution.py:131
  120.0 1.3 collective-permute-start.7
  121.3 19.2 %collective-permute-done.3 = bf16[5,2,1,128,512]{4,3,1,0,2:T(8,128)(2,1)S(1)} collective-permute-done((bf16[5,2,1,128,512]{4,3,1,0,2:T(8,128)(2,1)}, bf16[5,2,1,128,512]{4,3,1,0,2:T(8,128)(2,1)S(1)}, u32[]{:S(2)}, u32[]{:S(2)}) %collective-permute-start.3) | collective-permute-done | bytes 1310752 | tf_op jit(solution)/shard_map/ppermute | solution.py:166
  140.6 1.3 collective-permute-start.8
  141.9 2.4 collective-permute-start.11
  144.2 7.0 %collective-permute-start.12 = (bf16[5,2,1,128,512]{4,3,1,0,2:T(8,128)(2,1)}, bf16[5,2,1,128,512]{4,3,1,0,2:T(8,128)(2,1)}, u32[]{:S(2)}, u32[]{:S(2)}) collective-permute-start(bf16[5,2,1,128,512]{4,3,1,0,2:T(8,128)(2,1)} %get-tuple-element.42), channel_id=1, source_target_pairs={{0,8},{4,12},{1,9},{5,13},{2,10},{6,14},{3,11},{7,15},{16,24},{20,... | collective-permute-start | bytes 3932168 | tf_op jit(solution)/shard_map/ppermute | solution.py:166
  151.2 2.4 collective-permute-start.13
  153.6 64.6 %window_attention.3 = (bf16[2048,256]{1,0:T(8,128)(2,1)}, bf16[2048,256]{1,0:T(8,128)(2,1)}, bf16[2048,256]{1,0:T(8,128)(2,1)}, bf16[2048,256]{1,0:T(8,128)(2,1)}, f32[2048,256]{1,0:T(8,128)}) custom-call(s32[1]{0:T(128)} %bitcast.skip_ref, bf16[2048,512]{1,0:T(8,128)(2,1)} %q_ref.3, bf16[2048,512]{1,0:T(8,128)(2,1)} %g_ref.3, ...), custom_call_target="tpu_custom_call" | custom-call | flops 25769803776 | bytes 16777216 | tf_op jit(solution)/shard_map/window_attention/pallas_call | solution.py:131
  218.2 3.2 pad_maximum_fusion
  221.4 1.5 pad_maximum_fusion.1
  224.0 1.6 add_convert_fusion.2
  225.7 9.2 %convolution_convert_fusion = bf16[768,2048]{1,0:T(8,128)(2,1)S(1)} fusion(bf16[2048,2048]{1,0:T(8,128)(2,1)} %param.14, bf16[2048,256]{1,0:T(8,128)(2,1)S(1)} %copy-done.19, bf16[2048,256]{1,0:T(8,128)(2,1)S(1)} %add_convert_fusion.2, bf16[2048,256]{1,0:T(8,128)(2,1)S(1)} %copy-done.18), kind=kOutput, calls=%fused_computation | convolution fusion | flops 6453460992 | bytes 14680064 | tf_op jit(solution)/shard_map/tj,tk->jk/dot_general | solution.py:195
  236.9 1.4 collective-permute-start.10
  238.3 2.8 bitcast_dynamic-update-slice_fusion
  241.1 1.5 bitcast_dynamic-update-slice_fusion.2
  242.6 1.5 bitcast_dynamic-update-slice_fusion.1
  244.1 4.1 %fusion.24 = (bf16[1,2,1,4,128,512]{5,4,3,1,2,0:T(8,128)(2,1)S(1)}, bf16[1,2,1,4,128,512]{5,4,3,1,2,0:T(8,128)(2,1)S(1)}, bf16[1,2,1,4,128,512]{5,4,3,1,2,0:T(8,128)(2,1)}, bf16[1,2,1,4,128,512]{5,4,3,1,2,0:T(8,128)(2,1)}) fusion(bf16[5,2,1,4,128,512]{5,4,3,1,2,0:T(8,128)(2,1)} %bitcast_dynamic-update-slice_fusion.1), kind=kLoop, calls=%fused_computation.83 | loop fusion | bytes 8388608 | tf_op jit(solution)/shard_map/unstack | solution.py:341
  248.9 24.0 %collective-permute-done.14 = bf16[2,768,512]{2,1,0:T(8,128)(2,1)S(1)} collective-permute-done((bf16[2,768,512]{2,1,0:T(8,128)(2,1)S(1)}, bf16[2,768,512]{2,1,0:T(8,128)(2,1)S(1)}, u32[]{:S(2)}, u32[]{:S(2)}) %collective-permute-start.14) | collective-permute-done | bytes 1572896 | tf_op jit(solution)/shard_map/ppermute | solution.py:248
  274.4 9.8 %collective-permute-start.15 = (bf16[1,768,512]{2,1,0:T(8,128)(2,1)}, bf16[1,768,512]{2,1,0:T(8,128)(2,1)}, u32[]{:S(2)}, u32[]{:S(2)}) collective-permute-start(bf16[1,768,512]{2,1,0:T(8,128)(2,1)} %dynamic-slice_convert_fusion), channel_id=1, source_target_pairs={{0,8},{4,12},{8,0},{12,4},{1,9},{5,13},{9,1},{13,5},{2,10},{6,14},... | collective-permute-start | bytes 2359304 | tf_op jit(solution)/shard_map/ppermute | solution.py:248
  284.3 26.3 %collective-permute-done.10 = bf16[2048,256]{1,0:T(8,128)(2,1)S(1)} collective-permute-done((bf16[2048,256]{1,0:T(8,128)(2,1)S(1)}, bf16[2048,256]{1,0:T(8,128)(2,1)S(1)}, u32[]{:S(2)}, u32[]{:S(2)}) %collective-permute-start.10) | collective-permute-done | bytes 1048608 | tf_op jit(solution)/shard_map/ppermute | solution.py:166
  310.9 2.3 convolution_convert_fusion.1
  314.9 2.9 fusion.23
  317.8 4.1 %convolution_multiply_fusion = f32[2,512,512]{2,1,0:T(8,128)} fusion(bf16[2,512,512]{2,1,0:T(8,128)(2,1)} %bitcast.140, bf16[2,512,512]{2,1,0:T(8,128)(2,1)} %bitcast.139, bf16[2,512,512]{2,1,0:T(8,128)(2,1)S(1)} %convolution_convert_fusion.3), kind=kOutput, calls=%fused_computation.13 | convolution fusion | flops 1074790400 | bytes 5242880 | tf_op jit(solution)/shard_map/cbrk,cbkj->cbrj/dot_general | solution.py:195
  321.9 5.6 %collective-permute-done.16 = bf16[2,256,512]{2,1,0:T(8,128)(2,1)} collective-permute-done((bf16[2,256,512]{2,1,0:T(8,128)(2,1)}, bf16[2,256,512]{2,1,0:T(8,128)(2,1)}, u32[]{:S(2)}, u32[]{:S(2)}) %collective-permute-start.16) | collective-permute-done | bytes 524320 | tf_op jit(solution)/shard_map/ppermute | solution.py:248
  327.5 1.3 convert_add_fusion.1
  328.8 4.6 %collective-permute-start.17 = (bf16[1,256,512]{2,1,0:T(8,128)(2,1)S(1)}, bf16[1,256,512]{2,1,0:T(8,128)(2,1)}, u32[]{:S(2)}, u32[]{:S(2)}) collective-permute-start(bf16[1,256,512]{2,1,0:T(8,128)(2,1)S(1)} %dynamic-slice_convert_fusion.1), channel_id=1, source_target_pairs={{0,8},{4,12},{8,0},{12,4},{1,9},{5,13},{9,1},{13,5},{2,10},{6,14},... | collective-permute-start | bytes 786440 | tf_op jit(solution)/shard_map/ppermute | solution.py:248
  333.4 2.8 add_convert_fusion.3
  336.2 3.3 convolution_convert_fusion.5
  339.5 4.1 %all-to-all-start = ((bf16[4,1,128,512]{3,2,1,0:T(8,128)(2,1)}), bf16[4,1,128,512]{3,2,1,0:T(8,128)(2,1)}, u32[]{:S(2)}, u32[]{:S(2)}) async-start(bf16[4,1,128,512]{3,2,1,0:T(8,128)(2,1)} %bitcast.141), calls=%async_computation | async-start | bytes 1048576 | tf_op jit(solution)/shard_map/all_to_all | solution.py:366
  346.7 3.2 convolution_convert_fusion.4
  349.9 7.2 %all-to-all-done = bf16[4,1,128,512]{3,2,1,0:T(8,128)(2,1)} async-done(((bf16[4,1,128,512]{3,2,1,0:T(8,128)(2,1)}), bf16[4,1,128,512]{3,2,1,0:T(8,128)(2,1)}, u32[]{:S(2)}, u32[]{:S(2)}) %all-to-all-start) | async-done | bytes 524320 | tf_op jit(solution)/shard_map/all_to_all | solution.py:366
  357.1 3.5 all-to-all-start.1
  362.9 11.6 %all-to-all-done.1 = bf16[4,1,128,512]{3,2,1,0:T(8,128)(2,1)S(1)} async-done(((bf16[4,1,128,512]{3,2,1,0:T(8,128)(2,1)}), bf16[4,1,128,512]{3,2,1,0:T(8,128)(2,1)S(1)}, u32[]{:S(2)}, u32[]{:S(2)}) %all-to-all-start.1) | async-done | bytes 524320 | tf_op jit(solution)/shard_map/all_to_all | solution.py:366
  374.4 2.5 maximum_convert_fusion
  (89 shorter events, 24.6 us)
Async XLA Ops:
  0.6 9.7 %copy-start.2 = (bf16[8,128,512]{2,1,0:T(8,128)(2,1)S(1)}, bf16[8,128,512]{2,1,0:T(8,128)(2,1)}, u32[]{:S(2)}) copy-start(bf16[8,128,512]{2,1,0:T(8,128)(2,1)} %param.17) | copy-start | bytes 3145732
  3.3 7.0 %copy-start = (bf16[8,128,512]{2,1,0:T(8,128)(2,1)S(1)}, bf16[8,128,512]{2,1,0:T(8,128)(2,1)}, u32[]{:S(2)}) copy-start(bf16[8,128,512]{2,1,0:T(8,128)(2,1)} %param.15) | copy-start | bytes 3145732
  3.4 7.0 %copy-start.1 = (bf16[8,128,512]{2,1,0:T(8,128)(2,1)S(1)}, bf16[8,128,512]{2,1,0:T(8,128)(2,1)}, u32[]{:S(2)}) copy-start(bf16[8,128,512]{2,1,0:T(8,128)(2,1)} %param.16) | copy-start | bytes 3145732
  4.4 27.6 %collective-permute-start.1 = (bf16[2048,256]{1,0:T(8,128)(2,1)}, bf16[2048,256]{1,0:T(8,128)(2,1)}, u32[]{:S(2)}, u32[]{:S(2)}) collective-permute-start(bf16[2048,256]{1,0:T(8,128)(2,1)} %pad_maximum_fusion.3.rest_2_), channel_id=1, source_target_pairs={{0,4},{4,8},{8,12},{1,5},{5,9},{9,13},{2,6},{6,10},{10,14},{3,7},{... | collective-permute-start | bytes 3145736 | tf_op jit(solution)/shard_map/ppermute | solution.py:166
  10.3 1.2 copy-start.3
  11.6 1.2 copy-start.5
  13.9 32.4 %collective-permute-start = (bf16[5,2,1,128,512]{4,3,2,1,0:T(8,128)(2,1)}, bf16[5,2,1,128,512]{4,3,2,1,0:T(8,128)(2,1)}, u32[]{:S(2)}, u32[]{:S(2)}) collective-permute-start(bf16[5,2,1,128,512]{4,3,2,1,0:T(8,128)(2,1)} %pack_blocks.1), channel_id=1, source_target_pairs={{4,0},{8,4},{12,8},{5,1},{9,5},{13,9},{6,2},{10,6},{14,10},{7,3},{... | collective-permute-start | bytes 3932168 | tf_op jit(solution)/shard_map/ppermute | solution.py:166
  17.6 16.1 %copy-start.6 = (bf16[8,128,512]{2,1,0:T(8,128)(2,1)S(1)}, bf16[8,128,512]{2,1,0:T(8,128)(2,1)}, u32[]{:S(2)}) copy-start(bf16[8,128,512]{2,1,0:T(8,128)(2,1)} %param.19) | copy-start | bytes 3145732
  18.4 17.0 %copy-start.4 = (bf16[8,128,512]{2,1,0:T(8,128)(2,1)S(1)}, bf16[8,128,512]{2,1,0:T(8,128)(2,1)}, u32[]{:S(2)}) copy-start(bf16[8,128,512]{2,1,0:T(8,128)(2,1)} %param.18) | copy-start | bytes 3145732
  32.1 23.4 %collective-permute-start.2 = (bf16[2048,256]{1,0:T(8,128)(2,1)}, bf16[2048,256]{1,0:T(8,128)(2,1)}, u32[]{:S(2)}, u32[]{:S(2)}) collective-permute-start(bf16[2048,256]{1,0:T(8,128)(2,1)} %collective-permute-done.1.rest_1_), channel_id=1, source_target_pairs={{4,8},{8,12},{5,9},{9,13},{6,10},{10,14},{7,11},{11,15},{20,24},{2... | collective-permute-start | bytes 3145736 | tf_op jit(solution)/shard_map/ppermute | solution.py:166
  34.5 2.7 copy-start.12
  34.5 2.7 copy-start.13
  38.3 3.0 copy-start.14
  46.4 97.9 %collective-permute-start.6 = (bf16[2048,256]{1,0:T(8,128)(2,1)}, bf16[2048,256]{1,0:T(8,128)(2,1)}, u32[]{:S(2)}, u32[]{:S(2)}) collective-permute-start(bf16[2048,256]{1,0:T(8,128)(2,1)} %pad_maximum_fusion.4.rest_2_), channel_id=1, source_target_pairs={{0,4},{4,8},{8,12},{1,5},{5,9},{9,13},{2,6},{6,10},{10,14},{3,7},{... | collective-permute-start | bytes 3145736 | tf_op jit(solution)/shard_map/ppermute | solution.py:166
  50.6 100.6 %collective-permute-start.5 = (bf16[2048,256]{1,0:T(8,128)(2,1)}, bf16[2048,256]{1,0:T(8,128)(2,1)}, u32[]{:S(2)}, u32[]{:S(2)}) collective-permute-start(bf16[2048,256]{1,0:T(8,128)(2,1)} %pad_maximum_fusion.4.rest_2_), channel_id=1, source_target_pairs={{0,8},{4,12},{1,9},{5,13},{2,10},{6,14},{3,11},{7,15},{16,24},{20,... | collective-permute-start | bytes 3145736 | tf_op jit(solution)/shard_map/ppermute | solution.py:166
  52.8 87.7 %collective-permute-start.3 = (bf16[5,2,1,128,512]{4,3,1,0,2:T(8,128)(2,1)}, bf16[5,2,1,128,512]{4,3,1,0,2:T(8,128)(2,1)S(1)}, u32[]{:S(2)}, u32[]{:S(2)}) collective-permute-start(bf16[5,2,1,128,512]{4,3,1,0,2:T(8,128)(2,1)} %get-tuple-element.42), channel_id=1, source_target_pairs={{8,0},{12,4},{9,1},{13,5},{10,2},{14,6},{11,3},{15,7},{24,16},{28,... | collective-permute-start | bytes 3932168 | tf_op jit(solution)/shard_map/ppermute | solution.py:166
  54.1 87.7 %collective-permute-start.4 = (bf16[5,2,1,128,512]{4,3,1,0,2:T(8,128)(2,1)}, bf16[5,2,1,128,512]{4,3,1,0,2:T(8,128)(2,1)S(1)}, u32[]{:S(2)}, u32[]{:S(2)}) collective-permute-start(bf16[5,2,1,128,512]{4,3,1,0,2:T(8,128)(2,1)} %get-tuple-element.43), channel_id=1, source_target_pairs={{12,0},{13,1},{14,2},{15,3},{28,16},{29,17},{30,18},{31,19}} | collective-permute-start | bytes 3932168 | tf_op jit(solution)/shard_map/ppermute | solution.py:166
  120.0 102.8 %collective-permute-start.7 = (bf16[2048,256]{1,0:T(8,128)(2,1)}, bf16[2048,256]{1,0:T(8,128)(2,1)S(1)}, u32[]{:S(2)}, u32[]{:S(2)}) collective-permute-start(bf16[2048,256]{1,0:T(8,128)(2,1)} %get-tuple-element.35), channel_id=1, source_target_pairs={{4,0},{8,4},{12,8},{5,1},{9,5},{13,9},{6,2},{10,6},{14,10},{7,3},{... | collective-permute-start | bytes 3145736 | tf_op jit(solution)/shard_map/ppermute | solution.py:166
  140.6 77.6 %copy-start.15 = (bf16[5,2,1,128,512]{4,3,1,0,2:T(8,128)(2,1)}, bf16[5,2,1,128,512]{4,3,1,0,2:T(8,128)(2,1)S(1)}, u32[]{:S(2)}) copy-start(bf16[5,2,1,128,512]{4,3,1,0,2:T(8,128)(2,1)S(1)} %collective-permute-done.3) | copy-start | bytes 3932164
  140.6 83.4 %collective-permute-start.8 = (bf16[2048,256]{1,0:T(8,128)(2,1)}, bf16[2048,256]{1,0:T(8,128)(2,1)}, u32[]{:S(2)}, u32[]{:S(2)}) collective-permute-start(bf16[2048,256]{1,0:T(8,128)(2,1)} %get-tuple-element.36), channel_id=1, source_target_pairs={{8,0},{12,4},{9,1},{13,5},{10,2},{14,6},{11,3},{15,7},{24,16},{28,... | collective-permute-start | bytes 3145736 | tf_op jit(solution)/shard_map/ppermute | solution.py:166
  141.9 96.4 %collective-permute-start.11 = (bf16[5,2,1,128,512]{4,3,2,1,0:T(8,128)(2,1)}, bf16[5,2,1,128,512]{4,3,2,1,0:T(8,128)(2,1)}, u32[]{:S(2)}, u32[]{:S(2)}) collective-permute-start(bf16[5,2,1,128,512]{4,3,2,1,0:T(8,128)(2,1)} %bitcast_dynamic-update-slice_fusion.4), channel_id=1, source_target_pairs={{0,12},{1,13},{2,14},{3,15},{16,28},{17,29},{18,30},{19,31}} | collective-permute-start | bytes 3932168 | tf_op jit(solution)/shard_map/ppermute | solution.py:166
  144.2 96.9 %collective-permute-start.12 = (bf16[5,2,1,128,512]{4,3,1,0,2:T(8,128)(2,1)}, bf16[5,2,1,128,512]{4,3,1,0,2:T(8,128)(2,1)}, u32[]{:S(2)}, u32[]{:S(2)}) collective-permute-start(bf16[5,2,1,128,512]{4,3,1,0,2:T(8,128)(2,1)} %get-tuple-element.42), channel_id=1, source_target_pairs={{0,8},{4,12},{1,9},{5,13},{2,10},{6,14},{3,11},{7,15},{16,24},{20,... | collective-permute-start | bytes 3932168 | tf_op jit(solution)/shard_map/ppermute | solution.py:166
  151.2 91.4 %collective-permute-start.13 = (bf16[5,2,1,128,512]{4,3,1,0,2:T(8,128)(2,1)}, bf16[5,2,1,128,512]{4,3,1,0,2:T(8,128)(2,1)}, u32[]{:S(2)}, u32[]{:S(2)}) collective-permute-start(bf16[5,2,1,128,512]{4,3,1,0,2:T(8,128)(2,1)} %get-tuple-element.43), channel_id=1, source_target_pairs={{0,4},{4,8},{8,12},{1,5},{5,9},{9,13},{2,6},{6,10},{10,14},{3,7},{... | collective-permute-start | bytes 3932168 | tf_op jit(solution)/shard_map/ppermute | solution.py:166
  218.2 3.2 copy-start.18
  218.2 3.2 copy-start.19
  221.4 1.5 copy-start.20
  221.4 2.7 copy-start.9
  222.9 12.7 %collective-permute-start.9 = (bf16[2048,256]{1,0:T(8,128)(2,1)S(1)}, bf16[2048,256]{1,0:T(8,128)(2,1)S(1)}, u32[]{:S(2)}, u32[]{:S(2)}) collective-permute-start(bf16[2048,256]{1,0:T(8,128)(2,1)S(1)} %copy-done.20), channel_id=1, source_target_pairs={{8,4},{12,8},{9,5},{13,9},{10,6},{14,10},{11,7},{15,11},{24,20},{2... | collective-permute-start | bytes 3145736 | tf_op jit(solution)/shard_map/ppermute | solution.py:166
  235.3 1.2 copy-start.17
  235.5 37.4 %collective-permute-start.14 = (bf16[2,768,512]{2,1,0:T(8,128)(2,1)S(1)}, bf16[2,768,512]{2,1,0:T(8,128)(2,1)S(1)}, u32[]{:S(2)}, u32[]{:S(2)}) collective-permute-start(bf16[2,768,512]{2,1,0:T(8,128)(2,1)S(1)} %pad_maximum_fusion.2), channel_id=1, source_target_pairs={{0,4},{4,0},{8,12},{12,8},{1,5},{5,1},{9,13},{13,9},{2,6},{6,2},{1... | collective-permute-start | bytes 4718600 | tf_op jit(solution)/shard_map/ppermute | solution.py:248
  236.9 4.2 %copy-start.16 = (bf16[5,2,1,128,512]{4,3,1,0,2:T(8,128)(2,1)S(1)}, bf16[5,2,1,128,512]{4,3,1,0,2:T(8,128)(2,1)}, u32[]{:S(2)}) copy-start(bf16[5,2,1,128,512]{4,3,1,0,2:T(8,128)(2,1)} %copy-done.15) | copy-start | bytes 3932164
  236.9 73.7 %collective-permute-start.10 = (bf16[2048,256]{1,0:T(8,128)(2,1)S(1)}, bf16[2048,256]{1,0:T(8,128)(2,1)S(1)}, u32[]{:S(2)}, u32[]{:S(2)}) collective-permute-start(bf16[2048,256]{1,0:T(8,128)(2,1)S(1)} %add_convert_fusion.1), channel_id=1, source_target_pairs={{4,0},{8,4},{12,8},{5,1},{9,5},{13,9},{6,2},{10,6},{14,10},{7,3},{... | collective-permute-start | bytes 3145736 | tf_op jit(solution)/shard_map/ppermute | solution.py:166
  244.1 66.8 %slice-start = ((s8[8388608]{0:T(1024)(128)(4,1)}), s8[4194304]{0:T(1024)(128)(4,1)S(1)}, s32[]{:S(2)}) async-start(s8[8388608]{0:T(1024)(128)(4,1)} %bitcast.134), calls=%async_computation.2 | async-start | bytes 8388608
  272.9 37.7 %copy-start.8 = (f32[2048,256]{1,0:T(8,128)S(1)}, f32[2048,256]{1,0:T(8,128)}, u32[]{:S(2)}) copy-start(f32[2048,256]{1,0:T(8,128)} %get-tuple-element.37) | copy-start | bytes 6291460
  272.9 38.0 %slice-start.1 = ((s8[8388608]{0:T(1024)(128)(4,1)}), s8[4194304]{0:T(1024)(128)(4,1)S(1)}, s32[]{:S(2)}) async-start(s8[8388608]{0:T(1024)(128)(4,1)} %bitcast.134), calls=%async_computation.3 | async-start | bytes 8388608
  273.4 37.1 %copy-start.7 = (f32[2,768,512]{2,1,0:T(8,128)}, f32[2,768,512]{2,1,0:T(8,128)S(1)}, u32[]{:S(2)}) copy-start(f32[2,768,512]{2,1,0:T(8,128)S(1)} %convert_add_fusion) | copy-start | bytes 9437188
  274.4 58.9 %collective-permute-start.15 = (bf16[1,768,512]{2,1,0:T(8,128)(2,1)}, bf16[1,768,512]{2,1,0:T(8,128)(2,1)}, u32[]{:S(2)}, u32[]{:S(2)}) collective-permute-start(bf16[1,768,512]{2,1,0:T(8,128)(2,1)} %dynamic-slice_convert_fusion), channel_id=1, source_target_pairs={{0,8},{4,12},{8,0},{12,4},{1,9},{5,13},{9,1},{13,5},{2,10},{6,14},... | collective-permute-start | bytes 2359304 | tf_op jit(solution)/shard_map/ppermute | solution.py:248
  314.9 12.6 %collective-permute-start.16 = (bf16[2,256,512]{2,1,0:T(8,128)(2,1)}, bf16[2,256,512]{2,1,0:T(8,128)(2,1)}, u32[]{:S(2)}, u32[]{:S(2)}) collective-permute-start(bf16[2,256,512]{2,1,0:T(8,128)(2,1)} %pad_maximum_fusion.7), channel_id=1, source_target_pairs={{0,4},{4,0},{8,12},{12,8},{1,5},{5,1},{9,13},{13,9},{2,6},{6,2},{1... | collective-permute-start | bytes 1572872 | tf_op jit(solution)/shard_map/ppermute | solution.py:248
  328.8 16.8 %collective-permute-start.17 = (bf16[1,256,512]{2,1,0:T(8,128)(2,1)S(1)}, bf16[1,256,512]{2,1,0:T(8,128)(2,1)}, u32[]{:S(2)}, u32[]{:S(2)}) collective-permute-start(bf16[1,256,512]{2,1,0:T(8,128)(2,1)S(1)} %dynamic-slice_convert_fusion.1), channel_id=1, source_target_pairs={{0,8},{4,12},{8,0},{12,4},{1,9},{5,13},{9,1},{13,5},{2,10},{6,14},... | collective-permute-start | bytes 786440 | tf_op jit(solution)/shard_map/ppermute | solution.py:248
  339.5 17.6 %all-to-all-start = ((bf16[4,1,128,512]{3,2,1,0:T(8,128)(2,1)}), bf16[4,1,128,512]{3,2,1,0:T(8,128)(2,1)}, u32[]{:S(2)}, u32[]{:S(2)}) async-start(bf16[4,1,128,512]{3,2,1,0:T(8,128)(2,1)} %bitcast.141), calls=%async_computation | async-start | bytes 1048576 | tf_op jit(solution)/shard_map/all_to_all | solution.py:366
  349.9 10.8 %copy-start.11 = (bf16[2048,128]{1,0:T(8,128)(2,1)S(1)}, bf16[2048,128]{1,0:T(8,128)(2,1)}, u32[]{:S(2)}) copy-start(bf16[2048,128]{1,0:T(8,128)(2,1)} %get-tuple-element.76) | copy-start | bytes 1572868
  357.1 17.3 %all-to-all-start.1 = ((bf16[4,1,128,512]{3,2,1,0:T(8,128)(2,1)}), bf16[4,1,128,512]{3,2,1,0:T(8,128)(2,1)S(1)}, u32[]{:S(2)}, u32[]{:S(2)}) async-start(bf16[4,1,128,512]{3,2,1,0:T(8,128)(2,1)} %bitcast.57), calls=%async_computation.1 | async-start | bytes 1048576 | tf_op jit(solution)/shard_map/all_to_all | solution.py:366
  360.6 1.2 copy-start.10

commit v8 on v5

--- a/solution.py
+++ b/solution.py
@@ -195,6 +195,32 @@
     return jnp.einsum(spec, a, b, preferred_element_type=jnp.float32)
 
 
+def pack_body(owner_ref, *refs):
+    del owner_ref
+    for i, ref in enumerate(refs[:-1]):
+        refs[-1][i] = ref[:, 0]
+
+
+def pack(owner, arrays):
+    heads, _, blocks, rows, order = arrays[0].shape
+    shape = (len(arrays), heads, blocks, rows, order)
+    return pl.pallas_call(
+        pack_body,
+        out_shape=jax.ShapeDtypeStruct(shape, arrays[0].dtype),
+        grid_spec=pltpu.PrefetchScalarGridSpec(
+            num_scalar_prefetch=1,
+            grid=(1,),
+            in_specs=[pl.BlockSpec(
+                (heads, 1, blocks, rows, order), lambda i, who: (0, who[0], 0, 0, 0))] * len(arrays),
+            out_specs=pl.BlockSpec(shape, lambda i, who: (0,) * 5),
+        ),
+        compiler_params=pltpu.CompilerParams(vmem_limit_bytes=32 << 20),
+        cost_estimate=pl.CostEstimate(
+            flops=1 << 20, bytes_accessed=4 << 20, transcendentals=0),
+        name="pack_blocks",
+    )(jnp.reshape(owner, (1,)).astype(jnp.int32), *arrays)
+
+
 def project(columns, layer_input):
     return bmm("tj,tk->jk", columns, layer_input).astype(jnp.bfloat16)
 
@@ -274,9 +300,8 @@
             whole, message(seq_index)[:, :, :, None], seq_index, 3)
         leftward = []
         for d in range(1, n):
-            packed = message((seq_index + n - d) % n)
-            if d > 1:
-                packed = after(packed, leftward[0])
+            owner = (seq_index + n - d) % n
+            packed = after(message(owner), leftward[0]) if d > 1 else pack(owner, cut)
             leftward.append(shifted(packed, "seq", -d))
         rightward = []
     outs, query_grads, key_grads, value_grads, joined = [], [], [], [], []

time: 369 us -> 365 us (0.989)
  waiting for transfers between devices: 104 us -> 86.9 us
  local copies, waits for them, and re-layouts: 21 us -> 27.7 us
  starting transfers between devices: 59 us -> 63.6 us
    ppermute x14, waiting for transfers between devices: 55.9 us -> 41.4 us  [shifted(): return lax.ppermute(x, axis, pairs)]
    unnamed x38 -> x56, local copies, waits for them, and re-layouts: 6.53 us -> 11.6 us
    ppermute x14, starting transfers between devices: 45.1 us -> 49.1 us  [shifted(): return lax.ppermute(x, axis, pairs)]
  transfers between devices with their start and end apart: 20 -> 20, of which waited for: 8 -> 8; matrix products, arithmetic and copies ran while one was open for 19% -> 20% of each run, Pallas kernels for 35% -> 36%
where the time goes in v8:
time: 365 us; the launch traced here: 364 us
  Pallas kernels  130 us (36%)
  waiting for transfers between devices  86.9 us (24%)
  starting transfers between devices  63.6 us (17%)
  local copies, waits for them, and re-layouts  27.7 us (8%)
  matrix products  27.7 us (8%)
  other arithmetic  26.6 us (7%)
    pallas_call x2, Pallas kernels, attention(): pl.pallas_call(functools.partial(attn_body, reach, tile, group), out_shap...  129 us
    ppermute x14, starting transfers between devices, shifted(): return lax.ppermute(x, axis, pairs)  49.1 us
    ppermute x14, waiting for transfers between devices, shifted(): return lax.ppermute(x, axis, pairs)  41.4 us
    ppermute x4, waiting for transfers between devices, swap_sum(): got = lax.ppermute(send, 'seq', [(i, i ^ step) for i in range(n)])  34.7 us
    dot_general x6, matrix products, bmm(): return jnp.einsum(spec, a, b, preferred_element_type=jnp.float32)  27.7 us
    unnamed x56, local copies, waits for them, and re-layouts  11.6 us
    all_to_all x2, waiting for transfers between devices, per_device(): new = lax.all_to_all(new, 'seq', 0, 0)  10.8 us
    all_to_all x2, starting transfers between devices, per_device(): new = lax.all_to_all(new, 'seq', 0, 0)  8.35 us
  transfers between devices with their start and end apart: 20, of which 8 were waited for; matrix products, arithmetic and copies ran while one was open for 20% of the time, Pallas kernels for 36%

profile of v8, /device:TPU:0, one launch (start us, length us, event | category | flops | bytes accessed | tf_op | source)
XLA Modules:
  0.0 363.8 jit_solution(5173435536470549451)
XLA Ops:
  0.6 2.7 fusion.23
  4.4 5.9 %collective-permute-start.1 = (bf16[2048,256]{1,0:T(8,128)(2,1)}, bf16[2048,256]{1,0:T(8,128)(2,1)}, u32[]{:S(2)}, u32[]{:S(2)}) collective-permute-start(bf16[2048,256]{1,0:T(8,128)(2,1)} %pad_maximum_fusion.3.rest_2_), channel_id=1, source_target_pairs={{0,4},{4,8},{8,12},{1,5},{5,9},{9,13},{2,6},{6,10},{10,14},{3,7},{... | collective-permute-start | bytes 3145736 | tf_op jit(solution)/shard_map/ppermute | solution.py:166
  11.6 1.2 copy-done.5
  14.0 1.3 collective-permute-start
  18.3 1.7 bitcast_dynamic-update-slice_fusion.5
  21.0 11.1 %collective-permute-done.1.rest_1_ = bf16[2048,256]{1,0:T(8,128)(2,1)} collective-permute-done((bf16[2048,256]{1,0:T(8,128)(2,1)}, bf16[2048,256]{1,0:T(8,128)(2,1)}, u32[]{:S(2)}, u32[]{:S(2)}) %collective-permute-start.1) | collective-permute-done | bytes 1048608 | tf_op jit(solution)/shard_map/ppermute | solution.py:166
  32.1 1.6 collective-permute-start.2
  38.2 2.9 broadcast_in_dim.15
  42.3 4.1 %collective-permute-done = bf16[5,2,1,128,512]{4,3,2,1,0:T(8,128)(2,1)} collective-permute-done((bf16[5,2,1,128,512]{4,3,2,1,0:T(8,128)(2,1)}, bf16[5,2,1,128,512]{4,3,2,1,0:T(8,128)(2,1)}, u32[]{:S(2)}, u32[]{:S(2)}) %collective-permute-start) | collective-permute-done | bytes 1310752 | tf_op jit(solution)/shard_map/ppermute | solution.py:166
  46.4 1.3 collective-permute-start.3
  47.7 1.3 collective-permute-start.4
  49.0 13.8 %collective-permute-start.6 = (bf16[2048,256]{1,0:T(8,128)(2,1)}, bf16[2048,256]{1,0:T(8,128)(2,1)}, u32[]{:S(2)}, u32[]{:S(2)}) collective-permute-start(bf16[2048,256]{1,0:T(8,128)(2,1)} %pad_maximum_fusion.4.rest_2_), channel_id=1, source_target_pairs={{0,4},{4,8},{8,12},{1,5},{5,9},{9,13},{2,6},{6,10},{10,14},{3,7},{... | collective-permute-start | bytes 3145736 | tf_op jit(solution)/shard_map/ppermute | solution.py:166
  62.8 5.4 %collective-permute-start.5 = (bf16[2048,256]{1,0:T(8,128)(2,1)}, bf16[2048,256]{1,0:T(8,128)(2,1)}, u32[]{:S(2)}, u32[]{:S(2)}) collective-permute-start(bf16[2048,256]{1,0:T(8,128)(2,1)} %pad_maximum_fusion.4.rest_2_), channel_id=1, source_target_pairs={{0,8},{4,12},{1,9},{5,13},{2,10},{6,14},{3,11},{7,15},{16,24},{20,... | collective-permute-start | bytes 3145736 | tf_op jit(solution)/shard_map/ppermute | solution.py:166
  68.2 64.6 %window_attention.2 = (bf16[2048,256]{1,0:T(8,128)(2,1)}, bf16[2048,256]{1,0:T(8,128)(2,1)}, bf16[2048,256]{1,0:T(8,128)(2,1)}, bf16[2048,256]{1,0:T(8,128)(2,1)}, f32[2048,256]{1,0:T(8,128)}) custom-call(s32[1]{0:T(128)} %bitcast.skip_ref, bf16[2048,512]{1,0:T(8,128)(2,1)} %q_ref.3, bf16[2048,512]{1,0:T(8,128)(2,1)} %g_ref.3, ...), custom_call_target="tpu_custom_call" | custom-call | flops 25769803776 | bytes 16777216 | tf_op jit(solution)/shard_map/window_attention/pallas_call | solution.py:131
  132.8 1.3 collective-permute-start.7
  136.3 1.4 collective-permute-start.8
  137.7 8.6 %collective-permute-start.11 = (bf16[5,2,1,128,512]{4,3,2,1,0:T(8,128)(2,1)}, bf16[5,2,1,128,512]{4,3,2,1,0:T(8,128)(2,1)}, u32[]{:S(2)}, u32[]{:S(2)}) collective-permute-start(bf16[5,2,1,128,512]{4,3,2,1,0:T(8,128)(2,1)} %bitcast_dynamic-update-slice_fusion.4), channel_id=1, source_target_pairs={{0,12},{1,13},{2,14},{3,15},{16,28},{17,29},{18,30},{19,31}} | collective-permute-start | bytes 3932168 | tf_op jit(solution)/shard_map/ppermute | solution.py:166
  146.3 2.4 collective-permute-start.12
  148.7 2.5 collective-permute-start.13
  151.2 64.6 %window_attention.3 = (bf16[2048,256]{1,0:T(8,128)(2,1)}, bf16[2048,256]{1,0:T(8,128)(2,1)}, bf16[2048,256]{1,0:T(8,128)(2,1)}, bf16[2048,256]{1,0:T(8,128)(2,1)}, f32[2048,256]{1,0:T(8,128)}) custom-call(s32[1]{0:T(128)} %bitcast.skip_ref, bf16[2048,512]{1,0:T(8,128)(2,1)} %q_ref.3, bf16[2048,512]{1,0:T(8,128)(2,1)} %g_ref.3, ...), custom_call_target="tpu_custom_call" | custom-call | flops 25769803776 | bytes 16777216 | tf_op jit(solution)/shard_map/window_attention/pallas_call | solution.py:131
  216.8 2.0 add_convert_fusion.2
  219.0 9.3 %convolution_convert_fusion = bf16[768,2048]{1,0:T(8,128)(2,1)S(1)} fusion(bf16[2048,2048]{1,0:T(8,128)(2,1)} %param.14, bf16[2048,256]{1,0:T(8,128)(2,1)S(1)} %copy-done.20, bf16[2048,256]{1,0:T(8,128)(2,1)S(1)} %add_convert_fusion.2, bf16[2048,256]{1,0:T(8,128)(2,1)S(1)} %copy-done.19), kind=kOutput, calls=%fused_computation | convolution fusion | flops 6453460992 | bytes 14680064 | tf_op jit(solution)/shard_map/tj,tk->jk/dot_general | solution.py:195
  228.8 1.5 pad_maximum_fusion.1
  230.3 1.3 pad_maximum_fusion.2
  231.9 1.3 add_convert_fusion.1
  233.2 1.4 collective-permute-start.10
  234.6 2.8 bitcast_dynamic-update-slice_fusion
  237.4 1.5 bitcast_dynamic-update-slice_fusion.2
  238.9 1.5 bitcast_dynamic-update-slice_fusion.1
  240.3 4.0 %fusion.20 = (bf16[1,2,1,4,128,512]{5,4,3,1,2,0:T(8,128)(2,1)S(1)}, bf16[1,2,1,4,128,512]{5,4,3,1,2,0:T(8,128)(2,1)S(1)}, bf16[1,2,1,4,128,512]{5,4,3,1,2,0:T(8,128)(2,1)}, bf16[1,2,1,4,128,512]{5,4,3,1,2,0:T(8,128)(2,1)}) fusion(bf16[5,2,1,4,128,512]{5,4,3,1,2,0:T(8,128)(2,1)} %bitcast_dynamic-update-slice_fusion.1), kind=kLoop, calls=%fused_computation.81 | loop fusion | bytes 8388608 | tf_op jit(solution)/shard_map/unstack | solution.py:341
  244.4 1.8 convolution_convert_fusion.3
  246.1 2.9 fusion.19
  249.0 4.5 %convolution_multiply_fusion = f32[2,512,512]{2,1,0:T(8,128)} fusion(bf16[2,512,512]{2,1,0:T(8,128)(2,1)} %bitcast.138, bf16[2,512,512]{2,1,0:T(8,128)(2,1)} %bitcast.137, bf16[2,512,512]{2,1,0:T(8,128)(2,1)} %convolution_convert_fusion.3), kind=kOutput, calls=%fused_computation.13 | convolution fusion | flops 1074790400 | bytes 5242880 | tf_op jit(solution)/shard_map/cbrk,cbkj->cbrj/dot_general | solution.py:195
  253.5 15.7 %collective-permute-done.14 = bf16[2,768,512]{2,1,0:T(8,128)(2,1)} collective-permute-done((bf16[2,768,512]{2,1,0:T(8,128)(2,1)}, bf16[2,768,512]{2,1,0:T(8,128)(2,1)}, u32[]{:S(2)}, u32[]{:S(2)}) %collective-permute-start.14) | collective-permute-done | bytes 1572896 | tf_op jit(solution)/shard_map/ppermute | solution.py:246
  269.2 2.1 convert_add_fusion
  271.4 6.0 %collective-permute-start.15 = (bf16[1,768,512]{2,1,0:T(8,128)(2,1)S(1)}, bf16[1,768,512]{2,1,0:T(8,128)(2,1)S(1)}, u32[]{:S(2)}, u32[]{:S(2)}) collective-permute-start(bf16[1,768,512]{2,1,0:T(8,128)(2,1)S(1)} %dynamic-slice_convert_fusion), channel_id=1, source_target_pairs={{0,8},{4,12},{8,0},{12,4},{1,9},{5,13},{9,1},{13,5},{2,10},{6,14},... | collective-permute-start | bytes 2359304 | tf_op jit(solution)/shard_map/ppermute | solution.py:246
  277.4 25.1 %collective-permute-done.10 = bf16[2048,256]{1,0:T(8,128)(2,1)} collective-permute-done((bf16[2048,256]{1,0:T(8,128)(2,1)}, bf16[2048,256]{1,0:T(8,128)(2,1)}, u32[]{:S(2)}, u32[]{:S(2)}) %collective-permute-start.10) | collective-permute-done | bytes 1048608 | tf_op jit(solution)/shard_map/ppermute | solution.py:166
  302.5 1.6 add_convert_fusion
  304.1 5.7 %convolution_convert_fusion.1 = bf16[256,2048]{1,0:T(8,128)(2,1)S(1)} fusion(bf16[2048,256]{1,0:T(8,128)(2,1)S(1)} %add_convert_fusion, bf16[2048,2048]{1,0:T(8,128)(2,1)} %param.14), kind=kOutput, calls=%fused_computation.7 | convolution fusion | flops 2148007936 | bytes 10485760 | tf_op jit(solution)/shard_map/tj,tk->jk/dot_general | solution.py:195
  312.0 3.2 convolution_convert_fusion.5
  315.1 4.9 %all-to-all-start = ((bf16[4,1,128,512]{3,2,1,0:T(8,128)(2,1)}), bf16[4,1,128,512]{3,2,1,0:T(8,128)(2,1)S(1)}, u32[]{:S(2)}, u32[]{:S(2)}) async-start(bf16[4,1,128,512]{3,2,1,0:T(8,128)(2,1)} %bitcast.140), calls=%async_computation | async-start | bytes 1048576 | tf_op jit(solution)/shard_map/all_to_all | solution.py:361
  320.0 4.7 %collective-permute-done.16 = bf16[2,256,512]{2,1,0:T(8,128)(2,1)} collective-permute-done((bf16[2,256,512]{2,1,0:T(8,128)(2,1)}, bf16[2,256,512]{2,1,0:T(8,128)(2,1)}, u32[]{:S(2)}, u32[]{:S(2)}) %collective-permute-start.16) | collective-permute-done | bytes 524320 | tf_op jit(solution)/shard_map/ppermute | solution.py:246
  326.1 1.5 pad_maximum_fusion
  327.6 14.2 %collective-permute-done.17 = bf16[1,256,512]{2,1,0:T(8,128)(2,1)S(1)} collective-permute-done((bf16[1,256,512]{2,1,0:T(8,128)(2,1)S(1)}, bf16[1,256,512]{2,1,0:T(8,128)(2,1)S(1)}, u32[]{:S(2)}, u32[]{:S(2)}) %collective-permute-start.17) | collective-permute-done | bytes 262176 | tf_op jit(solution)/shard_map/ppermute | solution.py:246
  342.6 3.2 convolution_convert_fusion.4
  345.8 3.5 all-to-all-start.1
  351.6 10.8 %all-to-all-done.1 = bf16[4,1,128,512]{3,2,1,0:T(8,128)(2,1)S(1)} async-done(((bf16[4,1,128,512]{3,2,1,0:T(8,128)(2,1)}), bf16[4,1,128,512]{3,2,1,0:T(8,128)(2,1)S(1)}, u32[]{:S(2)}, u32[]{:S(2)}) %all-to-all-start.1) | async-done | bytes 524320 | tf_op jit(solution)/shard_map/all_to_all | solution.py:361
  362.4 1.5 maximum_convert_fusion
  (89 shorter events, 23.8 us)
Async XLA Ops:
  0.6 9.7 %copy-start.2 = (bf16[8,128,512]{2,1,0:T(8,128)(2,1)S(1)}, bf16[8,128,512]{2,1,0:T(8,128)(2,1)}, u32[]{:S(2)}) copy-start(bf16[8,128,512]{2,1,0:T(8,128)(2,1)} %param.17) | copy-start | bytes 3145732
  3.3 7.0 %copy-start = (bf16[8,128,512]{2,1,0:T(8,128)(2,1)S(1)}, bf16[8,128,512]{2,1,0:T(8,128)(2,1)}, u32[]{:S(2)}) copy-start(bf16[8,128,512]{2,1,0:T(8,128)(2,1)} %param.15) | copy-start | bytes 3145732
  3.4 7.0 %copy-start.1 = (bf16[8,128,512]{2,1,0:T(8,128)(2,1)S(1)}, bf16[8,128,512]{2,1,0:T(8,128)(2,1)}, u32[]{:S(2)}) copy-start(bf16[8,128,512]{2,1,0:T(8,128)(2,1)} %param.16) | copy-start | bytes 3145732
  4.4 27.6 %collective-permute-start.1 = (bf16[2048,256]{1,0:T(8,128)(2,1)}, bf16[2048,256]{1,0:T(8,128)(2,1)}, u32[]{:S(2)}, u32[]{:S(2)}) collective-permute-start(bf16[2048,256]{1,0:T(8,128)(2,1)} %pad_maximum_fusion.3.rest_2_), channel_id=1, source_target_pairs={{0,4},{4,8},{8,12},{1,5},{5,9},{9,13},{2,6},{6,10},{10,14},{3,7},{... | collective-permute-start | bytes 3145736 | tf_op jit(solution)/shard_map/ppermute | solution.py:166
  10.4 1.2 copy-start.3
  11.6 1.2 copy-start.5
  14.0 32.4 %collective-permute-start = (bf16[5,2,1,128,512]{4,3,2,1,0:T(8,128)(2,1)}, bf16[5,2,1,128,512]{4,3,2,1,0:T(8,128)(2,1)}, u32[]{:S(2)}, u32[]{:S(2)}) collective-permute-start(bf16[5,2,1,128,512]{4,3,2,1,0:T(8,128)(2,1)} %pack_blocks.1), channel_id=1, source_target_pairs={{4,0},{8,4},{12,8},{5,1},{9,5},{13,9},{6,2},{10,6},{14,10},{7,3},{... | collective-permute-start | bytes 3932168 | tf_op jit(solution)/shard_map/ppermute | solution.py:166
  17.6 16.1 %copy-start.6 = (bf16[8,128,512]{2,1,0:T(8,128)(2,1)S(1)}, bf16[8,128,512]{2,1,0:T(8,128)(2,1)}, u32[]{:S(2)}) copy-start(bf16[8,128,512]{2,1,0:T(8,128)(2,1)} %param.19) | copy-start | bytes 3145732
  18.3 17.0 %copy-start.4 = (bf16[8,128,512]{2,1,0:T(8,128)(2,1)S(1)}, bf16[8,128,512]{2,1,0:T(8,128)(2,1)}, u32[]{:S(2)}) copy-start(bf16[8,128,512]{2,1,0:T(8,128)(2,1)} %param.18) | copy-start | bytes 3145732
  32.1 16.9 %collective-permute-start.2 = (bf16[2048,256]{1,0:T(8,128)(2,1)}, bf16[2048,256]{1,0:T(8,128)(2,1)}, u32[]{:S(2)}, u32[]{:S(2)}) collective-permute-start(bf16[2048,256]{1,0:T(8,128)(2,1)} %collective-permute-done.1.rest_1_), channel_id=1, source_target_pairs={{4,8},{8,12},{5,9},{9,13},{6,10},{10,14},{7,11},{11,15},{20,24},{2... | collective-permute-start | bytes 3145736 | tf_op jit(solution)/shard_map/ppermute | solution.py:166
  34.4 2.7 copy-start.9
  34.4 2.7 copy-start.10
  38.2 2.9 copy-start.11
  41.1 5.3 %copy-start.23 = (bf16[5,2,1,128,512]{4,3,1,0,2:T(8,128)(2,1)S(1)}, bf16[5,2,1,128,512]{4,3,1,0,2:T(8,128)(2,1)}, u32[]{:S(2)}) copy-start(bf16[5,2,1,128,512]{4,3,1,0,2:T(8,128)(2,1)} %get-tuple-element.41) | copy-start | bytes 3932164
  46.4 88.8 %collective-permute-start.3 = (bf16[5,2,1,128,512]{4,3,1,0,2:T(8,128)(2,1)S(1)}, bf16[5,2,1,128,512]{4,3,1,0,2:T(8,128)(2,1)S(1)}, u32[]{:S(2)}, u32[]{:S(2)}) collective-permute-start(bf16[5,2,1,128,512]{4,3,1,0,2:T(8,128)(2,1)S(1)} %copy-done.23), channel_id=1, source_target_pairs={{8,0},{12,4},{9,1},{13,5},{10,2},{14,6},{11,3},{15,7},{24,16},{28,... | collective-permute-start | bytes 3932168 | tf_op jit(solution)/shard_map/ppermute | solution.py:166
  47.7 90.0 %collective-permute-start.4 = (bf16[5,2,1,128,512]{4,3,1,0,2:T(8,128)(2,1)}, bf16[5,2,1,128,512]{4,3,1,0,2:T(8,128)(2,1)S(1)}, u32[]{:S(2)}, u32[]{:S(2)}) collective-permute-start(bf16[5,2,1,128,512]{4,3,1,0,2:T(8,128)(2,1)} %get-tuple-element.42), channel_id=1, source_target_pairs={{12,0},{13,1},{14,2},{15,3},{28,16},{29,17},{30,18},{31,19}} | collective-permute-start | bytes 3932168 | tf_op jit(solution)/shard_map/ppermute | solution.py:166
  49.0 97.4 %collective-permute-start.6 = (bf16[2048,256]{1,0:T(8,128)(2,1)}, bf16[2048,256]{1,0:T(8,128)(2,1)}, u32[]{:S(2)}, u32[]{:S(2)}) collective-permute-start(bf16[2048,256]{1,0:T(8,128)(2,1)} %pad_maximum_fusion.4.rest_2_), channel_id=1, source_target_pairs={{0,4},{4,8},{8,12},{1,5},{5,9},{9,13},{2,6},{6,10},{10,14},{3,7},{... | collective-permute-start | bytes 3145736 | tf_op jit(solution)/shard_map/ppermute | solution.py:166
  62.8 85.9 %collective-permute-start.5 = (bf16[2048,256]{1,0:T(8,128)(2,1)}, bf16[2048,256]{1,0:T(8,128)(2,1)}, u32[]{:S(2)}, u32[]{:S(2)}) collective-permute-start(bf16[2048,256]{1,0:T(8,128)(2,1)} %pad_maximum_fusion.4.rest_2_), channel_id=1, source_target_pairs={{0,8},{4,12},{1,9},{5,13},{2,10},{6,14},{3,11},{7,15},{16,24},{20,... | collective-permute-start | bytes 3145736 | tf_op jit(solution)/shard_map/ppermute | solution.py:166
  132.8 83.0 %collective-permute-start.7 = (bf16[2048,256]{1,0:T(8,128)(2,1)}, bf16[2048,256]{1,0:T(8,128)(2,1)}, u32[]{:S(2)}, u32[]{:S(2)}) collective-permute-start(bf16[2048,256]{1,0:T(8,128)(2,1)} %get-tuple-element.34), channel_id=1, source_target_pairs={{4,0},{8,4},{12,8},{5,1},{9,5},{13,9},{6,2},{10,6},{14,10},{7,3},{... | collective-permute-start | bytes 3145736 | tf_op jit(solution)/shard_map/ppermute | solution.py:166
  135.2 1.1 copy-start.14
  136.3 80.5 %copy-start.8 = (f32[2048,256]{1,0:T(8,128)S(1)}, f32[2048,256]{1,0:T(8,128)}, u32[]{:S(2)}) copy-start(f32[2048,256]{1,0:T(8,128)} %get-tuple-element.33) | copy-start | bytes 6291460
  136.3 80.5 %collective-permute-start.8 = (bf16[2048,256]{1,0:T(8,128)(2,1)}, bf16[2048,256]{1,0:T(8,128)(2,1)}, u32[]{:S(2)}, u32[]{:S(2)}) collective-permute-start(bf16[2048,256]{1,0:T(8,128)(2,1)} %get-tuple-element.35), channel_id=1, source_target_pairs={{8,0},{12,4},{9,1},{13,5},{10,2},{14,6},{11,3},{15,7},{24,16},{28,... | collective-permute-start | bytes 3145736 | tf_op jit(solution)/shard_map/ppermute | solution.py:166
  137.7 78.1 %copy-start.12 = (bf16[5,2,1,128,512]{4,3,1,0,2:T(8,128)(2,1)}, bf16[5,2,1,128,512]{4,3,1,0,2:T(8,128)(2,1)S(1)}, u32[]{:S(2)}) copy-start(bf16[5,2,1,128,512]{4,3,1,0,2:T(8,128)(2,1)S(1)} %collective-permute-done.4) | copy-start | bytes 3932164
  137.7 96.9 %collective-permute-start.11 = (bf16[5,2,1,128,512]{4,3,2,1,0:T(8,128)(2,1)}, bf16[5,2,1,128,512]{4,3,2,1,0:T(8,128)(2,1)}, u32[]{:S(2)}, u32[]{:S(2)}) collective-permute-start(bf16[5,2,1,128,512]{4,3,2,1,0:T(8,128)(2,1)} %bitcast_dynamic-update-slice_fusion.4), channel_id=1, source_target_pairs={{0,12},{1,13},{2,14},{3,15},{16,28},{17,29},{18,30},{19,31}} | collective-permute-start | bytes 3932168 | tf_op jit(solution)/shard_map/ppermute | solution.py:166
  146.3 91.0 %collective-permute-start.12 = (bf16[5,2,1,128,512]{4,3,1,0,2:T(8,128)(2,1)}, bf16[5,2,1,128,512]{4,3,1,0,2:T(8,128)(2,1)}, u32[]{:S(2)}, u32[]{:S(2)}) collective-permute-start(bf16[5,2,1,128,512]{4,3,1,0,2:T(8,128)(2,1)} %get-tuple-element.41), channel_id=1, source_target_pairs={{0,8},{4,12},{1,9},{5,13},{2,10},{6,14},{3,11},{7,15},{16,24},{20,... | collective-permute-start | bytes 3932168 | tf_op jit(solution)/shard_map/ppermute | solution.py:166
  148.7 90.1 %collective-permute-start.13 = (bf16[5,2,1,128,512]{4,3,1,0,2:T(8,128)(2,1)}, bf16[5,2,1,128,512]{4,3,1,0,2:T(8,128)(2,1)}, u32[]{:S(2)}, u32[]{:S(2)}) collective-permute-start(bf16[5,2,1,128,512]{4,3,1,0,2:T(8,128)(2,1)} %get-tuple-element.42), channel_id=1, source_target_pairs={{0,4},{4,8},{8,12},{1,5},{5,9},{9,13},{2,6},{6,10},{10,14},{3,7},{... | collective-permute-start | bytes 3932168 | tf_op jit(solution)/shard_map/ppermute | solution.py:166
  215.8 15.7 %collective-permute-start.9 = (bf16[2048,256]{1,0:T(8,128)(2,1)}, bf16[2048,256]{1,0:T(8,128)(2,1)S(1)}, u32[]{:S(2)}, u32[]{:S(2)}) collective-permute-start(bf16[2048,256]{1,0:T(8,128)(2,1)} %get-tuple-element.37), channel_id=1, source_target_pairs={{8,4},{12,8},{9,5},{13,9},{10,6},{14,10},{11,7},{15,11},{24,20},{2... | collective-permute-start | bytes 3145736 | tf_op jit(solution)/shard_map/ppermute | solution.py:166
  216.8 2.0 copy-start.19
  216.8 2.2 copy-start.20
  230.2 1.6 copy-start.16
  231.5 37.7 %collective-permute-start.14 = (bf16[2,768,512]{2,1,0:T(8,128)(2,1)}, bf16[2,768,512]{2,1,0:T(8,128)(2,1)}, u32[]{:S(2)}, u32[]{:S(2)}) collective-permute-start(bf16[2,768,512]{2,1,0:T(8,128)(2,1)} %pad_maximum_fusion.2), channel_id=1, source_target_pairs={{0,4},{4,0},{8,12},{12,8},{1,5},{5,1},{9,13},{13,9},{2,6},{6,2},{1... | collective-permute-start | bytes 4718600 | tf_op jit(solution)/shard_map/ppermute | solution.py:246
  233.2 4.2 %copy-start.15 = (bf16[5,2,1,128,512]{4,3,1,0,2:T(8,128)(2,1)S(1)}, bf16[5,2,1,128,512]{4,3,1,0,2:T(8,128)(2,1)}, u32[]{:S(2)}) copy-start(bf16[5,2,1,128,512]{4,3,1,0,2:T(8,128)(2,1)} %copy-done.14) | copy-start | bytes 3932164
  233.2 69.3 %collective-permute-start.10 = (bf16[2048,256]{1,0:T(8,128)(2,1)}, bf16[2048,256]{1,0:T(8,128)(2,1)}, u32[]{:S(2)}, u32[]{:S(2)}) collective-permute-start(bf16[2048,256]{1,0:T(8,128)(2,1)} %add_convert_fusion.1), channel_id=1, source_target_pairs={{4,0},{8,4},{12,8},{5,1},{9,5},{13,9},{6,2},{10,6},{14,10},{7,3},{... | collective-permute-start | bytes 3145736 | tf_op jit(solution)/shard_map/ppermute | solution.py:166
  237.4 1.5 copy-start.13
  269.2 33.4 %copy-start.7 = (f32[2048,256]{1,0:T(8,128)S(1)}, f32[2048,256]{1,0:T(8,128)}, u32[]{:S(2)}) copy-start(f32[2048,256]{1,0:T(8,128)} %get-tuple-element.36) | copy-start | bytes 6291460
  271.4 39.4 %collective-permute-start.15 = (bf16[1,768,512]{2,1,0:T(8,128)(2,1)S(1)}, bf16[1,768,512]{2,1,0:T(8,128)(2,1)S(1)}, u32[]{:S(2)}, u32[]{:S(2)}) collective-permute-start(bf16[1,768,512]{2,1,0:T(8,128)(2,1)S(1)} %dynamic-slice_convert_fusion), channel_id=1, source_target_pairs={{0,8},{4,12},{8,0},{12,4},{1,9},{5,13},{9,1},{13,5},{2,10},{6,14},... | collective-permute-start | bytes 2359304 | tf_op jit(solution)/shard_map/ppermute | solution.py:246
  310.0 2.0 copy-start.22
  310.8 13.9 %collective-permute-start.16 = (bf16[2,256,512]{2,1,0:T(8,128)(2,1)}, bf16[2,256,512]{2,1,0:T(8,128)(2,1)}, u32[]{:S(2)}, u32[]{:S(2)}) collective-permute-start(bf16[2,256,512]{2,1,0:T(8,128)(2,1)} %pad_maximum_fusion.10), channel_id=1, source_target_pairs={{0,4},{4,0},{8,12},{12,8},{1,5},{5,1},{9,13},{13,9},{2,6},{6,2},{1... | collective-permute-start | bytes 1572872 | tf_op jit(solution)/shard_map/ppermute | solution.py:246
  315.1 30.7 %all-to-all-start = ((bf16[4,1,128,512]{3,2,1,0:T(8,128)(2,1)}), bf16[4,1,128,512]{3,2,1,0:T(8,128)(2,1)S(1)}, u32[]{:S(2)}, u32[]{:S(2)}) async-start(bf16[4,1,128,512]{3,2,1,0:T(8,128)(2,1)} %bitcast.140), calls=%async_computation | async-start | bytes 1048576 | tf_op jit(solution)/shard_map/all_to_all | solution.py:361
  320.0 6.0 %copy-start.17 = (bf16[2048,256]{1,0:T(8,128)(2,1)S(1)}, bf16[2048,256]{1,0:T(8,128)(2,1)}, u32[]{:S(2)}) copy-start(bf16[2048,256]{1,0:T(8,128)(2,1)} %get-tuple-element.25) | copy-start | bytes 3145732
  320.0 6.0 %copy-start.18 = (bf16[2048,256]{1,0:T(8,128)(2,1)S(1)}, bf16[2048,256]{1,0:T(8,128)(2,1)}, u32[]{:S(2)}) copy-start(bf16[2048,256]{1,0:T(8,128)(2,1)} %get-tuple-element.30) | copy-start | bytes 3145732
  326.0 15.8 %collective-permute-start.17 = (bf16[1,256,512]{2,1,0:T(8,128)(2,1)S(1)}, bf16[1,256,512]{2,1,0:T(8,128)(2,1)S(1)}, u32[]{:S(2)}, u32[]{:S(2)}) collective-permute-start(bf16[1,256,512]{2,1,0:T(8,128)(2,1)S(1)} %dynamic-slice_convert_fusion.1), channel_id=1, source_target_pairs={{0,8},{4,12},{8,0},{12,4},{1,9},{5,13},{9,1},{13,5},{2,10},{6,14},... | collective-permute-start | bytes 786440 | tf_op jit(solution)/shard_map/ppermute | solution.py:246
  326.1 16.5 %copy-start.21 = (bf16[1,768,512]{2,1,0:T(8,128)(2,1)S(1)}, bf16[1,768,512]{2,1,0:T(8,128)(2,1)}, u32[]{:S(2)}) copy-start(bf16[1,768,512]{2,1,0:T(8,128)(2,1)} %add_convert_fusion.3) | copy-start | bytes 2359300
  345.8 16.5 %all-to-all-start.1 = ((bf16[4,1,128,512]{3,2,1,0:T(8,128)(2,1)}), bf16[4,1,128,512]{3,2,1,0:T(8,128)(2,1)S(1)}, u32[]{:S(2)}, u32[]{:S(2)}) async-start(bf16[4,1,128,512]{3,2,1,0:T(8,128)(2,1)} %bitcast.141), calls=%async_computation.1 | async-start | bytes 1048576 | tf_op jit(solution)/shard_map/all_to_all | solution.py:361
